TPU v7x, 32 devices: a whole 2x2x4 slice. The times are simulated.
32 devices in a mesh: clip: 2 (over x), gz: 16 (over z, y, core).
Axes of the slice: x: 2, y: 2, z: 4, core: 2. Of those that a mesh axis runs over, the one named last changes fastest.
Arguments:
- source_term: float32 [2, 128, 64, 128], P(None, ('clip', 'gz')), parts along dimension 1, may hold values from -24 to 24
- material: int32 [128, 64, 128], P(('clip', 'gz')), parts along dimension 0, may hold values from 0 to 2
- orders: int32 [2, 1024], P(None, 'gz'), may hold values from -22 to 22
Outputs:
- solution: float32 [2, 128, 64, 128], P(None, ('clip', 'gz')), parts along dimension 1
- residual: float32 [2, 128, 64, 128], P(None, ('clip', 'gz')), parts along dimension 1
- pupil_orders: float32 [2, 2048], P(None, ('clip', 'gz')), parts along dimension 1
There are 2 independent parts, one for each index of `clip`. A program takes and returns all parts, laid end to end along the dimension named above; an argument that names none is the same for every part. Nothing has to cross between parts.
All inputs are finite; a program needn't handle non-finite values.
Results may differ from a plain program's by a relative error of at most 0.0003.
Values sent between devices are 32-bit elements; how exact they have to be, the bound alone decides.
No kernel may reach another device: no remote copies, remote signals or barrier semaphores. Data moves between devices by JAX's collectives and lax.ppermute only.
A program may use at most 128 MiB of HBM per device.

v0:
```python
import functools
import math

import jax
import jax.numpy as jnp
import numpy as np
from jax import lax
from jax.experimental import pallas as pl
from jax.experimental.pallas import tpu as pltpu
from jax.sharding import PartitionSpec as P

ORD_HALF = 22
HELM_TABLE = ((-0.5, 0.0), (1.0, -1.4), (-1.2, 0.0))
SHIFT_TABLE = ((-0.5, -0.25), (1.0, -0.25 * math.sqrt(11.84)), (-1.2, -0.6))
RELAX = 0.8
KEEP = 1.0 - RELAX
PLANES = 4
OWN = 2 * PLANES
WINDOW = 5 * PLANES
PAD1 = 8
PAD2 = 4
H1 = 0.25
H2 = 0.0625
F32 = jnp.float32

WEIGHTS = tuple(RELAX / complex(6.0 + s[0], s[1]) for s in SHIFT_TABLE)


def pick(code, values):
    return jnp.where(
        code == 1.0,
        values[0],
        jnp.where(code == 2.0, values[1], jnp.where(code == 3.0, values[2], 0.0)),
    )


def weight_of(code):
    return pick(code, [w.real for w in WEIGHTS]), pick(code, [w.imag for w in WEIGHTS])


def shift_of(code):
    return pick(code, [s[0] for s in SHIFT_TABLE]), pick(code, [s[1] for s in SHIFT_TABLE])


def helm_of(code):
    return pick(code, [s[0] for s in HELM_TABLE]), pick(code, [s[1] for s in HELM_TABLE])


def cmul(ar, ai, br, bi):
    return ar * br - ai * bi, ar * bi + ai * br


def around(ref, p, lead=()):
    sums = []
    for c in range(2):
        mid = ref[c, p]
        nx, ny = mid.shape
        total = ref[c, p - 1] + ref[c, p + 1]
        total = total + pltpu.roll(mid, 1, 0) + pltpu.roll(mid, nx - 1, 0)
        total = total + pltpu.roll(mid, 1, 1) + pltpu.roll(mid, ny - 1, 1)
        sums.append(total)
    return sums


def lanes(shape):
    return lax.broadcasted_iota(jnp.int32, shape, len(shape) - 1)


def around_packed(ref, p, part):
    mid = ref[p]
    n = mid.shape[0]
    width = mid.shape[1]
    total = ref[p - 1] + ref[p + 1]
    total = total + pltpu.roll(mid, 1, 0) + pltpu.roll(mid, n - 1, 0)
    at = lanes(mid.shape) % part
    before = jnp.where(at == 0, pltpu.roll(mid, width + 1 - part, 1), pltpu.roll(mid, 1, 1))
    after = jnp.where(at == part - 1, pltpu.roll(mid, part - 1, 1), pltpu.roll(mid, width - 1, 1))
    return total + before + after


def cmul_packed(wr, wi, g, part):
    return wr * g + wi * pltpu.roll(g, part, 1)


def weights_packed(shift, part, factor):
    other = pltpu.roll(shift, part, 1)
    real_lane = lanes(shift.shape) % (2 * part) < part
    dr = 6.0 * factor + jnp.where(real_lane, shift, other)
    di = jnp.where(real_lane, other, shift)
    scale = RELAX / (dr * dr + di * di)
    wi = -di * scale
    return dr * scale, jnp.where(real_lane, -wi, wi)


def dot(a, b):
    return jnp.dot(a, b, precision=lax.Precision.HIGHEST, preferred_element_type=F32)


def iota2(rows, cols):
    return (
        lax.broadcasted_iota(jnp.int32, (rows, cols), 0),
        lax.broadcasted_iota(jnp.int32, (rows, cols), 1),
    )


def restrict_fine(real, imag, tmp):
    nx, ny = real.shape
    tmp[0] = real
    tmp[1] = imag
    half = nx // 2
    rows = [tmp[c, pl.ds(0, half, stride=2), :] + tmp[c, pl.ds(1, half, stride=2), :] for c in range(2)]
    r, c = iota2(2 * ny, ny)
    pool = jnp.where(r // 2 == c, 0.125, 0.0).astype(F32)
    return dot(jnp.concatenate(rows, axis=1), pool)


def each(lower, upper, body):
    def step(p, carry):
        body(p)
        return carry

    lax.fori_loop(lower, upper, step, 0)


def full(shape_dtype):
    return jax.ShapeDtypeStruct(shape_dtype, F32)


VM = pl.BlockSpec(memory_space=pltpu.VMEM)
SM = pl.BlockSpec(memory_space=pltpu.SMEM)


def call(body, outs, inputs, scratch, name):
    size = sum(4 * math.prod(x.shape) for x in inputs) + sum(4 * math.prod(o) for o in outs)
    return pl.pallas_call(
        body,
        out_shape=[full(o) for o in outs],
        in_specs=[SM] + [VM] * (len(inputs) - 1),
        out_specs=[VM] * len(outs),
        scratch_shapes=[pltpu.VMEM(s, F32) for s in scratch],
        cost_estimate=pl.CostEstimate(flops=40 * size, bytes_accessed=size, transcendentals=0),
        name=name,
    )(*inputs)


def first_kernel(at, own, near, swap, orders, out, u, e1, u2, tmp):
    odd = at[1]

    def fill(block, first):
        def body(p):
            code = block[2, p]
            wr, wi = weight_of(code)
            ur, ui = cmul(wr, wi, block[0, p], block[1, p])
            u[0, first + p] = ur
            u[1, first + p] = ui

        each(0, PLANES, body)

    fill(own, PLANES)
    fill(near, 2 * PLANES - 2 * PLANES * odd)
    fill(swap, 2 * PLANES * odd)

    def smooth(p, block, q):
        sr, si = around(u, p)
        er = KEEP * block[0, q] + sr
        ei = KEEP * block[1, q] + si
        wr, wi = weight_of(block[2, q])
        vr, vi = cmul(wr, wi, er, ei)
        u2[0, p] = vr
        u2[1, p] = vi
        return er, ei

    def inner(q):
        er, ei = smooth(PLANES + q, own, q)
        e1[0, q] = er
        e1[1, q] = ei

    each(0, PLANES, inner)

    @pl.when(odd == 0)
    def _():
        smooth(PLANES - 1, swap, PLANES - 1)
        smooth(2 * PLANES, near, 0)

    @pl.when(odd == 1)
    def _():
        smooth(PLANES - 1, near, PLANES - 1)
        smooth(2 * PLANES, swap, 0)

    half = own.shape[2] // 2
    for q in range(PLANES // 2):
        total = [0.0, 0.0, 0.0, 0.0]
        for k in range(2):
            p = 2 * q + k
            s = around(u2, PLANES + p)
            shift = shift_of(own[2, p])
            for c in range(2):
                total[c] = total[c] + KEEP * e1[c, p] + s[c]
                total[2 + c] = total[2 + c] + shift[c]
        out[pl.ds(half * q, half), :] = restrict_fine(total[0], total[1], tmp)
        out[pl.ds(half * (2 + q), half), :] = restrict_fine(total[2], total[3], tmp)
    out[pl.ds(4 * half, 8), :] = jnp.broadcast_to(orders[...], (8, orders.shape[1]))


def coarse_shapes(group, nx, ny):
    n1 = (2 * group + 2 * PAD1, nx // 2, ny)
    n2 = (group + 2 * PAD2, nx // 4, ny)
    return [n1] * 5 + [n2] * 3 + [(nx // 2, ny)]


def coarse_weights(me, masks, pieces, w1r, w1i, w2r, w2i, shift2, tmp):
    half, ny = tmp.shape
    group = len(masks)
    for ref, pad in ((w1r, PAD1), (w1i, PAD1), (w2r, PAD2), (w2i, PAD2)):
        zero = jnp.zeros(ref.shape[1:], F32)
        for k in range(pad):
            ref[k] = zero
            ref[ref.shape[0] - 1 - k] = zero
    for mask, (piece, j) in zip(masks, pieces, strict=True):
        d = me ^ mask
        planes = [piece[j, pl.ds(half * (2 + k), half), :] for k in range(2)]
        for k in range(2):
            wr, wi = weights_packed(planes[k], ny // 2, H1)
            w1r[PAD1 + 2 * d + k] = wr
            w1i[PAD1 + 2 * d + k] = wi
        tmp[...] = planes[0] + planes[1]
        shift2[d] = tmp[pl.ds(0, half // 2, stride=2), :] + tmp[pl.ds(1, half // 2, stride=2), :]
    flat = shift2[...].reshape(group * (half // 2), ny)
    s2 = dot(flat, pool_level1(ny)).reshape(group, half // 2, ny)
    for d in range(group):
        wr, wi = weights_packed(s2[d], ny // 4, H2)
        w2r[PAD2 + d] = wr
        w2i[PAD2 + d] = wi


def pool_level1(ny):
    r, c = iota2(ny, ny)
    return jnp.where(r // 2 == c % (ny // 2), 0.125, 0.0).astype(F32)


def coarse_solve(me, masks, pieces, reach, w1r, w1i, w2r, w2i, g1, u1, e1, u2, v1, g2, va, vb, tmp, out):
    half, ny = tmp.shape
    group = len(masks)
    part1, part2 = ny // 2, ny // 4
    n1 = 2 * group
    for ref, pad in ((g1, PAD1), (u1, PAD1), (u2, PAD1), (v1, PAD1), (va, PAD2), (vb, PAD2)):
        zero = jnp.zeros(ref.shape[1:], F32)
        for k in range(pad):
            ref[k] = zero
            ref[ref.shape[0] - 1 - k] = zero
    for mask, (piece, j) in zip(masks, pieces, strict=True):
        d = me ^ mask
        for k in range(2):
            p = PAD1 + 2 * d + k
            g = piece[j, pl.ds(half * k, half), :]
            g1[p] = g
            u1[p] = cmul_packed(w1r[p], w1i[p], g, part1)

    def pre(p):
        e = KEEP * g1[p] + H1 * around_packed(u1, p, part1)
        u = cmul_packed(w1r[p], w1i[p], e, part1)
        e1[p] = e
        u2[p] = u
        v1[p] = u1[p] + u

    each(PAD1, PAD1 + n1, pre)

    def coarser(d):
        total = 0.0
        for k in range(2):
            p = PAD1 + 2 * d + k
            total = total + KEEP * e1[p] + H1 * around_packed(u2, p, part1)
        tmp[...] = total
        g2[PAD2 + d] = tmp[pl.ds(0, half // 2, stride=2), :] + tmp[pl.ds(1, half // 2, stride=2), :]

    each(0, group, coarser)
    flat = g2[pl.ds(PAD2, group)].reshape(group * (half // 2), ny)
    r2 = dot(flat, pool_level1(ny)).reshape(group, half // 2, ny)
    for d in range(group):
        g2[PAD2 + d] = r2[d]
        va[PAD2 + d] = cmul_packed(w2r[PAD2 + d], w2i[PAD2 + d], r2[d], part2)
    for src, dst in ((va, vb), (vb, va), (va, vb)):

        def sweep(p, src=src, dst=dst):
            s = g2[p] + H2 * around_packed(src, p, part2)
            dst[p] = KEEP * src[p] + cmul_packed(w2r[p], w2i[p], s, part2)

        each(PAD2, PAD2 + group, sweep)
    reach2 = (reach + 2) // 2
    count = 2 * reach2 + 1
    first2 = PAD2 + me - reach2
    flat = vb[pl.ds(first2, count)].reshape(count * (half // 2), ny)
    r, c = iota2(ny, ny)
    spread = jnp.where(c // 2 == r, 1.0, 0.0).astype(F32)
    e2 = dot(flat, spread).reshape(count, half // 2, ny)
    base = PAD1 + 2 * (me - reach2)
    for k in range(count):
        tmp[pl.ds(0, half // 2, stride=2), :] = e2[k]
        tmp[pl.ds(1, half // 2, stride=2), :] = e2[k]
        add = tmp[...]
        v1[base + 2 * k] = v1[base + 2 * k] + add
        v1[base + 2 * k + 1] = v1[base + 2 * k + 1] + add

    def post(src, p):
        s = g1[p] + H1 * around_packed(src, p, part1)
        return KEEP * src[p] + cmul_packed(w1r[p], w1i[p], s, part1)

    start = PAD1 + 2 * me

    def third(p):
        u1[p] = post(v1, p)

    def fourth(k):
        out[k] = post(u1, start - reach + k)

    each(start - reach - 1, start + reach + 3, third)
    each(0, 2 * reach + 2, fourth)


def add_correction(ec, v, tmp, planes):
    half, ny = ec.shape[1:]
    r, c = iota2(ny, 2 * ny)
    spread = jnp.where(c // 2 == r, 1.0, 0.0).astype(F32)

    def body(k):
        both = dot(ec[k], spread)
        for c in range(2):
            e = both[:, c * ny : (c + 1) * ny]
            tmp[c, pl.ds(0, half, stride=2), :] = e
            tmp[c, pl.ds(1, half, stride=2), :] = e
            add = tmp[c]
            v[c, 2 * k] = v[c, 2 * k] + add
            v[c, 2 * k + 1] = v[c, 2 * k + 1] + add

    each(0, planes, body)


def second_kernel(
    masks, layout, at, own, near, swap, skip, far, *refs
):
    n = max(i for i, _ in layout) + 1
    gathered, refs = refs[:n], refs[n:]
    (direction, image, smooth2, weight, pay, w1r, w1i, w2r, w2i), refs = refs[:9], refs[9:]
    f, u, u2, v, code, tmp, ec, e1, shift2 = refs[:9]
    coarse = refs[9:]
    me, odd = at[0], at[1]
    pieces = [(gathered[i], j) for i, j in layout]

    def fill(block, first):
        def body(q):
            p = first + q
            c = block[2, q]
            wr, wi = weight_of(c)
            fr, fi = block[0, q], block[1, q]
            ur, ui = cmul(wr, wi, fr, fi)
            f[0, p], f[1, p] = fr, fi
            weight[0, p], weight[1, p] = wr, wi
            u[0, p], u[1, p] = ur, ui
            code[p] = c

        each(0, PLANES, body)

    fill(own, OWN)
    fill(near, OWN + PLANES - 2 * PLANES * odd)
    fill(swap, OWN - PLANES + 2 * PLANES * odd)
    fill(skip, 4 * PLANES * odd)
    fill(far, 4 * PLANES - 4 * PLANES * odd)

    def pre(p):
        sr, si = around(u, p)
        vr, vi = cmul(weight[0, p], weight[1, p], KEEP * f[0, p] + sr, KEEP * f[1, p] + si)
        v[0, p] = u[0, p] + vr
        v[1, p] = u[1, p] + vi

    each(1, WINDOW - 1, pre)
    coarse_weights(me, masks, pieces, w1r, w1i, w2r, w2i, shift2, coarse[-1])
    coarse_solve(me, masks, pieces, 4, w1r, w1i, w2r, w2i, *coarse, ec)
    add_correction(ec, v, tmp, WINDOW // 2)

    def sweep(src, dst, p):
        sr, si = around(src, p)
        vr, vi = cmul(weight[0, p], weight[1, p], f[0, p] + sr, f[1, p] + si)
        dst[0, p] = KEEP * src[0, p] + vr
        dst[1, p] = KEEP * src[1, p] + vi

    each(2, WINDOW - 2, lambda p: sweep(v, u, p))
    each(3, WINDOW - 3, lambda p: sweep(u, v, p))

    def apply(p):
        sr, si = around(v, p)
        c = code[p]
        hr, hi = helm_of(c)
        vr, vi = v[0, p], v[1, p]
        ar, ai = cmul(hr, hi, vr, vi)
        ar = jnp.where(c > 0.0, ar + 6.0 * vr - sr, 0.0)
        ai = jnp.where(c > 0.0, ai + 6.0 * vi - si, 0.0)
        image[0, p - 4] = ar
        image[1, p - 4] = ai
        ur, ui = cmul(weight[0, p], weight[1, p], ar, ai)
        u[0, p] = ur
        u[1, p] = ui

    each(4, WINDOW - 4, apply)
    nx = own.shape[2]
    rho, cross_r, cross_i = 0.0, 0.0, 0.0
    for q in range(PLANES):
        fr, fi = own[0, q], own[1, q]
        ir, ii = image[0, OWN - 4 + q], image[1, OWN - 4 + q]
        rho = rho + fr * fr + fi * fi
        cross_r = cross_r + fr * ir + fi * ii
        cross_i = cross_i + fr * ii - fi * ir
        for c in range(2):
            direction[c, q] = v[c, OWN + q]
    half = nx // 2
    row = lax.broadcasted_iota(jnp.int32, (8, own.shape[3]), 0)
    sums = [jnp.sum(t, axis=0, keepdims=True) for t in (rho, cross_r, cross_i)]
    tail = jnp.where(row == 0, sums[0], jnp.where(row == 1, sums[1], jnp.where(row == 2, sums[2], 0.0)))
    pay[pl.ds(2 * half, 8), :] = tail

    def pre2(p):
        sr, si = around(u, p)
        er = KEEP * image[0, p - 4] + sr
        ei = KEEP * image[1, p - 4] + si
        vr, vi = cmul(weight[0, p], weight[1, p], er, ei)
        e1[0, p], e1[1, p] = er, ei
        u2[0, p], u2[1, p] = vr, vi
        smooth2[0, p - 5] = u[0, p] + vr
        smooth2[1, p - 5] = u[1, p] + vi

    each(5, WINDOW - 5, pre2)
    for q in range(PLANES // 2):
        total = [0.0, 0.0]
        for k in range(2):
            p = OWN + 2 * q + k
            s = around(u2, p)
            for c in range(2):
                total[c] = total[c] + KEEP * e1[c, p] + s[c]
        pay[pl.ds(half * q, half), :] = restrict_fine(total[0], total[1], tmp)


def phase_kernel(masks, layout, row, at, *refs):
    n = max(i for i, _ in layout) + 1
    gathered = refs[:n]
    table, qrow, found = refs[n:]
    me = at[0]
    ny = found.shape[1]
    nx = table.shape[0] // 2
    for mask, (i, j) in zip(masks, layout, strict=True):
        found[pl.ds(me ^ mask, 1), :] = gathered[i][j, pl.ds(row, 1), :]
    low = lanes((1, ny)) < ny // 2
    x = lax.broadcasted_iota(jnp.int32, (nx, ny), 0)
    for pair in range(len(masks) // 2):
        even = found[pl.ds(2 * pair, 1), :]
        odd = found[pl.ds(2 * pair + 1, 1), :]
        p = jnp.where(low, even, pltpu.roll(odd, ny // 2, 1))
        q = jnp.where(low, pltpu.roll(even, ny // 2, 1), odd)
        turns = (x * p.astype(jnp.int32)) & (nx - 1)
        angle = turns.astype(F32) * (2.0 * math.pi / nx)
        table[pl.ds(0, nx), pl.ds(pair * ny, ny)] = jnp.cos(angle)
        table[pl.ds(nx, nx), pl.ds(pair * ny, ny)] = -jnp.sin(angle)
        qrow[:, pl.ds(pair * ny, ny)] = jnp.broadcast_to(q, (8, ny))


def third_kernel(
    masks, layout, at, own, direction, image, smooth2, weight, w1r, w1i, w2r, w2i, ytable, xtable, qrow, *refs
):
    n = max(i for i, _ in layout) + 1
    gathered, refs = refs[:n], refs[n:]
    (corrected, last_image, halfway, pay, alpha), refs = refs[:5], refs[5:]
    u, v, tmp, ec = refs[:4]
    coarse = refs[4:]
    me = at[0]
    pieces = [(gathered[i], j) for i, j in layout]
    nx, ny = own.shape[2:]
    half = nx // 2
    coarse_solve(me, masks, pieces, 2, w1r, w1i, w2r, w2i, *coarse, ec)

    def take(p):
        v[0, p] = smooth2[0, p - 1]
        v[1, p] = smooth2[1, p - 1]

    each(1, 11, take)
    add_correction(ec, v, tmp, 6)

    def sweep(src, dst, p):
        sr, si = around(src, p)
        w = p + OWN - 4
        vr, vi = cmul(weight[0, w], weight[1, w], image[0, p] + sr, image[1, p] + si)
        dst[0, p] = KEEP * src[0, p] + vr
        dst[1, p] = KEEP * src[1, p] + vi

    each(2, 10, lambda p: sweep(v, u, p))
    each(3, 9, lambda p: sweep(u, v, p))

    sums = 0.0
    for i, j in layout:
        sums = sums + gathered[i][j, pl.ds(2 * half, 8), :]
    rho, cr, ci = [jnp.sum(sums[k : k + 1], axis=1, keepdims=True) for k in range(3)]
    modulus = cr * cr + ci * ci
    ar = rho * cr / modulus
    ai = -rho * ci / modulus
    dots = [0.0, 0.0, 0.0]
    for q in range(PLANES):
        p = 4 + q
        sr, si = around(v, p)
        hr, hi = helm_of(own[2, q])
        wr, wi = v[0, p], v[1, p]
        br, bi = cmul(hr, hi, wr, wi)
        br, bi = br + 6.0 * wr - sr, bi + 6.0 * wi - si
        ir, ii = image[0, p], image[1, p]
        br, bi = cmul(ar, ai, br, bi)
        lr, li = ir - br, ii - bi
        tr, ti = cmul(ar, ai, ir, ii)
        hr, hi = own[0, q] - tr, own[1, q] - ti
        xr, xi = cmul(ar, ai, wr, wi)
        corrected[0, q], corrected[1, q] = direction[0, q] - xr, direction[1, q] - xi
        last_image[0, q], last_image[1, q] = lr, li
        halfway[0, q], halfway[1, q] = hr, hi
        dots[0] = dots[0] + lr * hr + li * hi
        dots[1] = dots[1] + lr * hi - li * hr
        dots[2] = dots[2] + lr * lr + li * li
    dots = [jnp.sum(t, axis=0, keepdims=True) for t in dots]
    row = lax.broadcasted_iota(jnp.int32, (8, ny), 0)
    alpha[...] = jnp.where(row == 0, ar, ai)

    sign = jnp.where(lanes((nx, ny)) < ny // 2, -1.0, 1.0)
    stacked = []
    for field in (direction, corrected):
        plane = field[:, PLANES - 1].reshape(2 * nx, ny)
        m = lax.dot_general(
            ytable[...],
            plane,
            (((1,), (1,)), ((), ())),
            precision=lax.Precision.HIGHEST,
            preferred_element_type=F32,
        )
        t = m[:nx] + sign * pltpu.roll(m[nx:], nx, 1)
        stacked += [-sign * t, pltpu.roll(t, nx, 1)]
    spectrum = dot(jnp.concatenate(stacked, axis=0), xtable[...])
    scale = 1.0 / math.sqrt(nx * ny)
    at_row = lax.broadcasted_iota(jnp.int32, (nx, ny), 0).astype(F32) - ORD_HALF
    for pair in range(len(masks) // 2):
        chosen = at_row == qrow[0:1, pair * ny : (pair + 1) * ny]
        found = [
            scale * jnp.sum(jnp.where(chosen, spectrum[k * nx : (k + 1) * nx, pair * ny : (pair + 1) * ny], 0.0), axis=0, keepdims=True)
            for k in range(4)
        ]
        block = 0.0
        for k, line in enumerate(found + dots):
            block = jnp.where(row == k, line, block)
        pay[2 * pair] = block
        pay[2 * pair + 1] = block


def last_kernel(at, direction, corrected, last_image, halfway, alpha, got, solution, residual, pupil):
    group = got.shape[0]
    ny = got.shape[2]
    total = got[0]
    for k in range(1, group):
        total = total + got[k]
    along_r, along_i, norm = [jnp.sum(total[k : k + 1], axis=1, keepdims=True) for k in (4, 5, 6)]
    wr = along_r / norm
    wi = along_i / norm
    ar = alpha[0:1, 0:1]
    ai = alpha[1:2, 0:1]
    for q in range(PLANES):
        xr, xi = cmul(ar, ai, direction[0, q], direction[1, q])
        yr, yi = cmul(wr, wi, corrected[0, q], corrected[1, q])
        solution[0, q], solution[1, q] = xr + yr, xi + yi
        zr, zi = cmul(wr, wi, last_image[0, q], last_image[1, q])
        residual[0, q], residual[1, q] = halfway[0, q] - zr, halfway[1, q] - zi
    tip = got[group - 1]
    xr, xi = cmul(ar, ai, tip[0:1], tip[1:2])
    yr, yi = cmul(wr, wi, tip[2:3], tip[3:4])
    both = jnp.concatenate([xr + yr, xi + yi], axis=0)
    both = jnp.where(at[1] == 1, pltpu.roll(jnp.broadcast_to(jnp.concatenate([both] * 4, axis=0), (8, ny)), ny // 2, 1)[:2], both)
    pupil[...] = both[:, : ny // 2]


def exchange(x, mask, group):
    return lax.ppermute(x, "gz", [(i, i ^ mask) for i in range(group)])


def swap_across(x, group):
    pairs = []
    for i in range(1, group - 1, 2):
        pairs += [(i, i + 1), (i + 1, i)]
    return lax.ppermute(x, "gz", pairs)


def skip_across(x, group):
    pairs = []
    for i in range(group):
        target = i + 2 if i % 2 == 0 else i - 2
        if 0 <= target < group:
            pairs.append((i, target))
    return lax.ppermute(x, "gz", pairs)


def stages_of(group):
    stages = [[1]]
    stride = 2
    left = group // 2
    if left.bit_length() % 2 == 0:
        stages.insert(0, [stride])
        stride, left = 2 * stride, left // 2
    while left > 1:
        stages.insert(0, [stride, 2 * stride, 3 * stride])
        stride, left = 4 * stride, left // 4
    return stages


def gather(x, group):
    have, masks = x[None], [0]
    stages = stages_of(group)
    for masks_now in stages[:-1]:
        got = [exchange(have, m, group) for m in masks_now]
        masks = masks + [k ^ m for m in masks_now for k in masks]
        have = jnp.concatenate([have] + got, axis=0)
    (m,) = stages[-1]
    other = exchange(have, m, group)
    count = len(masks)
    layout = [(0, j) for j in range(count)] + [(1, j) for j in range(count)]
    return [have, other], masks + [k ^ m for k in masks], layout


def y_phases(nx, ny):
    q = np.arange(nx) - ORD_HALF
    turns = (q[:, None] * np.arange(ny)[None, :]) % ny
    angle = turns.astype(np.float64) * (2.0 * np.pi / ny)
    return np.concatenate([np.cos(angle), -np.sin(angle)], axis=0).astype(np.float32)


def on_device(source_term, material, orders):
    group = lax.axis_size("gz")
    _, planes, nx, ny = source_term.shape
    assert planes == PLANES and 2 * nx == ny and 2 * orders.shape[1] == ny
    me = lax.axis_index("gz")
    at = jnp.stack([me, me % 2]).astype(jnp.int32)
    half = nx // 2

    own = jnp.concatenate([source_term, (material + 1).astype(F32)[None]], axis=0)
    near = exchange(own, 1, group)
    swap = swap_across(own, group)
    order_row = orders.astype(F32).reshape(1, ny)
    fine = (2, PLANES, nx, ny)
    (pay1,) = call(
        first_kernel,
        [(4 * half + 8, ny)],
        [at, own, near, swap, order_row],
        [(2, 3 * PLANES, nx, ny), fine, (2, 3 * PLANES, nx, ny), (2, nx, ny)],
        "first",
    )
    gathered1, masks, layout = gather(pay1, group)
    skip = skip_across(own, group)
    far = exchange(swap, 1, group)

    window = (2, WINDOW, nx, ny)
    shapes1 = (2 * group + 2 * PAD1, half, ny)
    shapes2 = (group + 2 * PAD2, half // 2, ny)
    direction, image, smooth2, weight, pay2, w1r, w1i, w2r, w2i = call(
        functools.partial(second_kernel, masks, layout),
        [
            fine,
            (2, 12, nx, ny),
            (2, 10, nx, ny),
            window,
            (2 * half + 8, ny),
            shapes1,
            shapes1,
            shapes2,
            shapes2,
        ],
        [at, own, near, swap, skip, far, *gathered1],
        [window] * 4
        + [(WINDOW, nx, ny), (2, nx, ny), (10, half, ny), window, (group, half // 2, ny)]
        + coarse_shapes(group, nx, ny),
        "second",
    )
    xtable, qrow = pl.pallas_call(
        functools.partial(phase_kernel, masks, layout, 4 * half),
        out_shape=[full((2 * nx, group * ny // 2)), full((8, group * ny // 2))],
        in_specs=[SM] + [VM] * len(gathered1),
        out_specs=[VM] * 2,
        scratch_shapes=[pltpu.VMEM((group, ny), F32)],
        cost_estimate=pl.CostEstimate(flops=4000000, bytes_accessed=600000, transcendentals=0),
        name="phases",
    )(at, *gathered1)
    gathered2, masks, layout = gather(pay2, group)
    corrected, last_image, halfway, pay3, alpha = call(
        functools.partial(third_kernel, masks, layout),
        [fine, fine, fine, (group, 8, ny), (8, ny)],
        [
            at,
            own,
            direction,
            image,
            smooth2,
            weight,
            w1r,
            w1i,
            w2r,
            w2i,
            jnp.asarray(y_phases(nx, ny)),
            xtable,
            qrow,
            *gathered2,
        ],
        [(2, 12, nx, ny), (2, 12, nx, ny), (2, nx, ny), (6, half, ny)] + coarse_shapes(group, nx, ny),
        "third",
    )
    got = lax.all_to_all(pay3, "gz", 0, 0)
    solution, residual, pupil = call(
        last_kernel,
        [fine, fine, (2, ny // 2)],
        [at, direction, corrected, last_image, halfway, alpha, got],
        [],
        "last",
    )
    return solution, residual, pupil


def solution(mesh):
    return jax.shard_map(
        on_device,
        mesh=mesh,
        in_specs=(
            P(None, ("clip", "gz"), None, None),
            P(("clip", "gz"), None, None),
            P(None, "gz"),
        ),
        out_specs=(
            P(None, ("clip", "gz"), None, None),
            P(None, ("clip", "gz"), None, None),
            P(None, ("clip", "gz")),
        ),
        check_vma=False,
    )
```

profile of v0, /device:TPU:0, one launch (start us, length us, event | category | flops | bytes accessed | tf_op | source)
XLA Modules:
  0.0 144.6 jit_solution(3906641989492537176)
XLA Ops:
  0.6 0.9 convert_bitcast_fusion
  1.5 1.0 pad_maximum_fusion.own
  3.2 4.4 %collective-permute-start = (f32[3,4,64,128]{3,2,1,0:T(8,128)S(1)}, f32[3,4,64,128]{3,2,1,0:T(8,128)S(1)}, u32[]{:S(2)}, u32[]{:S(2)}) collective-permute-start(f32[3,4,64,128]{3,2,1,0:T(8,128)S(1)} %pad_maximum_fusion.own), channel_id=1, source_target_pairs={{0,1},{1,0},{2,3},{3,2},{4,5},{5,4},{6,7},{7,6},{8,9},{9,8},{10,11... | collective-permute-start | bytes 1179656 | tf_op jit(solution)/shard_map/ppermute | solution.py:581
  11.1 3.2 %first.1 = f32[136,128]{1,0:T(8,128)} custom-call(s32[2]{0:T(128)} %pad_add_fusion.at, f32[3,4,64,128]{3,2,1,0:T(8,128)} %copy-done, f32[3,4,64,128]{3,2,1,0:T(8,128)} %copy-done.6, f32[3,4,64,128]{3,2,1,0:T(8,128)} %copy-done.4, f32[1,128]{1,0:T(1,128)} %reshape.9.orders), custom_call_target="tpu_custom_call" | custom-call | flops 49992000 | bytes 1249800 | tf_op jit(solution)/shard_map/first/pallas_call | solution.py:135
  14.3 6.1 %collective-permute-start.4 = (f32[1,136,128]{2,1,0:T(8,128)}, f32[1,136,128]{2,1,0:T(8,128)S(1)}, u32[]{:S(2)}, u32[]{:S(2)}) collective-permute-start(f32[1,136,128]{2,1,0:T(8,128)} %bitcast.8), channel_id=1, source_target_pairs={{0,4},{1,5},{2,6},{3,7},{4,0},{5,1},{6,2},{7,3},{8,12},{9,13},{10,... | collective-permute-start | bytes 208904 | tf_op jit(solution)/shard_map/ppermute | solution.py:581
  20.4 2.6 %collective-permute-start.5 = (f32[1,136,128]{2,1,0:T(8,128)}, f32[1,136,128]{2,1,0:T(8,128)S(1)}, u32[]{:S(2)}, u32[]{:S(2)}) collective-permute-start(f32[1,136,128]{2,1,0:T(8,128)} %bitcast.9), channel_id=1, source_target_pairs={{0,8},{1,9},{2,10},{3,11},{4,12},{5,13},{6,14},{7,15},{8,0},{9,1},... | collective-permute-start | bytes 208904 | tf_op jit(solution)/shard_map/ppermute | solution.py:581
  23.0 1.0 constant_dynamic-update-slice_fusion.4
  23.9 2.6 %collective-permute-done.5 = f32[1,136,128]{2,1,0:T(8,128)S(1)} collective-permute-done((f32[1,136,128]{2,1,0:T(8,128)}, f32[1,136,128]{2,1,0:T(8,128)S(1)}, u32[]{:S(2)}, u32[]{:S(2)}) %collective-permute-start.5) | collective-permute-done | bytes 69664 | tf_op jit(solution)/shard_map/ppermute | solution.py:581
  26.6 2.7 %collective-permute-done.6 = f32[1,136,128]{2,1,0:T(8,128)S(1)} collective-permute-done((f32[1,136,128]{2,1,0:T(8,128)}, f32[1,136,128]{2,1,0:T(8,128)S(1)}, u32[]{:S(2)}, u32[]{:S(2)}) %collective-permute-start.6) | collective-permute-done | bytes 69664 | tf_op jit(solution)/shard_map/ppermute | solution.py:581
  30.2 3.4 %collective-permute-start.7 = (f32[4,136,128]{2,1,0:T(8,128)S(1)}, f32[4,136,128]{2,1,0:T(8,128)S(1)}, u32[]{:S(2)}, u32[]{:S(2)}) collective-permute-start(f32[4,136,128]{2,1,0:T(8,128)S(1)} %pad_maximum_fusion.1), channel_id=1, source_target_pairs={{0,2},{1,3},{2,0},{3,1},{4,6},{5,7},{6,4},{7,5},{8,10},{9,11},{10,... | collective-permute-start | bytes 835592 | tf_op jit(solution)/shard_map/ppermute | solution.py:581
  33.6 6.7 %collective-permute-done.7 = f32[4,136,128]{2,1,0:T(8,128)S(1)} collective-permute-done((f32[4,136,128]{2,1,0:T(8,128)S(1)}, f32[4,136,128]{2,1,0:T(8,128)S(1)}, u32[]{:S(2)}, u32[]{:S(2)}) %collective-permute-start.7) | collective-permute-done | bytes 278560 | tf_op jit(solution)/shard_map/ppermute | solution.py:581
  40.5 2.2 %collective-permute-start.2 = (f32[3,4,64,128]{3,2,1,0:T(8,128)S(1)}, f32[3,4,64,128]{3,2,1,0:T(8,128)S(1)}, u32[]{:S(2)}, u32[]{:S(2)}) collective-permute-start(f32[3,4,64,128]{3,2,1,0:T(8,128)S(1)} %copy-done.1), channel_id=1, source_target_pairs={{0,2},{2,4},{3,1},{4,6},{5,3},{6,8},{7,5},{8,10},{9,7},{10,12},{11... | collective-permute-start | bytes 1179656 | tf_op jit(solution)/shard_map/ppermute | solution.py:597
  42.8 9.4 %collective-permute-done.2.skip = f32[3,4,64,128]{3,2,1,0:T(8,128)S(1)} collective-permute-done((f32[3,4,64,128]{3,2,1,0:T(8,128)S(1)}, f32[3,4,64,128]{3,2,1,0:T(8,128)S(1)}, u32[]{:S(2)}, u32[]{:S(2)}) %collective-permute-start.2) | collective-permute-done | bytes 393248 | tf_op jit(solution)/shard_map/ppermute | solution.py:597
  53.9 33.3 %second.1 = (f32[2,4,64,128]{3,2,1,0:T(8,128)}, f32[2,12,64,128]{3,2,1,0:T(8,128)}, f32[2,10,64,128]{3,2,1,0:T(8,128)}, f32[2,20,64,128]{3,2,1,0:T(8,128)}, f32[...) custom-call(s32[2]{0:T(128)} %pad_add_fusion.at, ...), custom_call_target="tpu_custom_call" | custom-call | flops 323912000 | bytes 8097800 | tf_op jit(solution)/shard_map/second/pallas_call | solution.py:135
  87.1 1.7 %collective-permute-start.10 = (f32[1,72,128]{2,1,0:T(8,128)}, f32[1,72,128]{2,1,0:T(8,128)S(1)}, u32[]{:S(2)}, u32[]{:S(2)}) collective-permute-start(f32[1,72,128]{2,1,0:T(8,128)} %bitcast.12), channel_id=1, source_target_pairs={{0,8},{1,9},{2,10},{3,11},{4,12},{5,13},{6,14},{7,15},{8,0},{9,1},... | collective-permute-start | bytes 110600 | tf_op jit(solution)/shard_map/ppermute | solution.py:581
  88.8 1.4 collective-permute-start.11
  91.5 1.6 %collective-permute-done.10 = f32[1,72,128]{2,1,0:T(8,128)S(1)} collective-permute-done((f32[1,72,128]{2,1,0:T(8,128)}, f32[1,72,128]{2,1,0:T(8,128)S(1)}, u32[]{:S(2)}, u32[]{:S(2)}) %collective-permute-start.10) | collective-permute-done | bytes 36896 | tf_op jit(solution)/shard_map/ppermute | solution.py:581
  93.1 1.9 %collective-permute-done.11 = f32[1,72,128]{2,1,0:T(8,128)S(1)} collective-permute-done((f32[1,72,128]{2,1,0:T(8,128)}, f32[1,72,128]{2,1,0:T(8,128)S(1)}, u32[]{:S(2)}, u32[]{:S(2)}) %collective-permute-start.11) | collective-permute-done | bytes 36896 | tf_op jit(solution)/shard_map/ppermute | solution.py:581
  96.4 1.8 %collective-permute-start.12 = (f32[4,72,128]{2,1,0:T(8,128)S(1)}, f32[4,72,128]{2,1,0:T(8,128)S(1)}, u32[]{:S(2)}, u32[]{:S(2)}) collective-permute-start(f32[4,72,128]{2,1,0:T(8,128)S(1)} %pad_maximum_fusion.2), channel_id=1, source_target_pairs={{0,2},{1,3},{2,0},{3,1},{4,6},{5,7},{6,4},{7,5},{8,10},{9,11},{10,... | collective-permute-start | bytes 442376 | tf_op jit(solution)/shard_map/ppermute | solution.py:581
  98.2 4.1 %collective-permute-done.12 = f32[4,72,128]{2,1,0:T(8,128)S(1)} collective-permute-done((f32[4,72,128]{2,1,0:T(8,128)S(1)}, f32[4,72,128]{2,1,0:T(8,128)S(1)}, u32[]{:S(2)}, u32[]{:S(2)}) %collective-permute-start.12) | collective-permute-done | bytes 147488 | tf_op jit(solution)/shard_map/ppermute | solution.py:581
  102.4 3.1 %phases.1 = (f32[128,1024]{1,0:T(8,128)}, f32[8,1024]{1,0:T(8,128)}) custom-call(s32[2]{0:T(128)} %pad_add_fusion.at, f32[8,136,128]{2,1,0:T(8,128)} %copy-done.2, f32[8,136,128]{2,1,0:T(8,128)} %copy-done.3), custom_call_target="tpu_custom_call" | custom-call | flops 4000000 | bytes 600000 | tf_op jit(solution)/shard_map/phases/pallas_call | solution.py:680
  106.3 25.1 %third.1 = (f32[2,4,64,128]{3,2,1,0:T(8,128)}, f32[2,4,64,128]{3,2,1,0:T(8,128)}, f32[2,4,64,128]{3,2,1,0:T(8,128)}, f32[16,8,128]{2,1,0:T(8,128)}, f32[8,128]{1,0:T(8,128)}) custom-call(s32[2]{0:T(128)} %pad_add_fusion.at, f32[3,4,64,128]{3,2,1,0:T(8,128)} %copy-done, f32[2,4,64,128]{3,2,1,0:T(8,128)} %get-tuple-element.19.direction, ...), custom_call_target="tpu_custom_call" | custom-call | flops 297697600 | bytes 7442440 | tf_op jit(solution)/shard_map/third/pallas_call | solution.py:135
  131.3 11.0 %all_to_all.5.got = f32[16,8,128]{2,1,0:T(8,128)} all-to-all(f32[16,8,128]{2,1,0:T(8,128)} %get-tuple-element.34), channel_id=1, replica_groups=mesh['clip'=2,'gz'=16] {'gz'}, dimensions={0} | all-to-all | bytes 131072 | tf_op jit(solution)/shard_map/all_to_all | solution.py:712
  142.4 2.2 %last.1 = (f32[2,4,64,128]{3,2,1,0:T(8,128)}, f32[2,4,64,128]{3,2,1,0:T(8,128)}, f32[2,64]{1,0:T(2,128)}) custom-call(s32[2]{0:T(128)} %pad_add_fusion.at, f32[2,4,64,128]{3,2,1,0:T(8,128)} %get-tuple-element.19.direction, f32[2,4,64,128]{3,2,1,0:T(8,128)} %get-tuple-element.30.corrected, f32[2,4,64,128]{3,2,1,0:T(8,128)} %get-tuple-element.31.last_image, ...), custom_call_target="tpu_custom_call" | custom-call | flops 65720640 | bytes 1643016 | tf_op jit(solution)/shard_map/last/pallas_call | solution.py:135
  (49 shorter events, 10.3 us)
Async XLA Ops:
  2.5 7.0 %copy-start = (f32[3,4,64,128]{3,2,1,0:T(8,128)}, f32[3,4,64,128]{3,2,1,0:T(8,128)S(1)}, u32[]{:S(2)}) copy-start(f32[3,4,64,128]{3,2,1,0:T(8,128)S(1)} %pad_maximum_fusion.own) | copy-start | bytes 1179652
  2.5 7.0 %collective-permute-start.1 = (f32[3,4,64,128]{3,2,1,0:T(8,128)S(1)}, f32[3,4,64,128]{3,2,1,0:T(8,128)S(1)}, u32[]{:S(2)}, u32[]{:S(2)}) collective-permute-start(f32[3,4,64,128]{3,2,1,0:T(8,128)S(1)} %pad_maximum_fusion.own), channel_id=1, source_target_pairs={{1,2},{2,1},{3,4},{4,3},{5,6},{6,5},{7,8},{8,7},{9,10},{10,9},{11,... | collective-permute-start | bytes 1179656 | tf_op jit(solution)/shard_map/ppermute | solution.py:588
  3.2 6.3 %collective-permute-start = (f32[3,4,64,128]{3,2,1,0:T(8,128)S(1)}, f32[3,4,64,128]{3,2,1,0:T(8,128)S(1)}, u32[]{:S(2)}, u32[]{:S(2)}) collective-permute-start(f32[3,4,64,128]{3,2,1,0:T(8,128)S(1)} %pad_maximum_fusion.own), channel_id=1, source_target_pairs={{0,1},{1,0},{2,3},{3,2},{4,5},{5,4},{6,7},{7,6},{8,9},{9,8},{10,11... | collective-permute-start | bytes 1179656 | tf_op jit(solution)/shard_map/ppermute | solution.py:581
  9.6 0.8 copy-start.4
  10.3 0.8 copy-start.6
  14.3 26.2 %copy-start.1 = (f32[3,4,64,128]{3,2,1,0:T(8,128)S(1)}, f32[3,4,64,128]{3,2,1,0:T(8,128)}, u32[]{:S(2)}) copy-start(f32[3,4,64,128]{3,2,1,0:T(8,128)} %copy-done) | copy-start | bytes 1179652
  14.3 28.4 %copy-start.5 = (f32[3,4,64,128]{3,2,1,0:T(8,128)S(1)}, f32[3,4,64,128]{3,2,1,0:T(8,128)}, u32[]{:S(2)}) copy-start(f32[3,4,64,128]{3,2,1,0:T(8,128)} %copy-done.4) | copy-start | bytes 1179652
  14.3 9.7 %collective-permute-start.4 = (f32[1,136,128]{2,1,0:T(8,128)}, f32[1,136,128]{2,1,0:T(8,128)S(1)}, u32[]{:S(2)}, u32[]{:S(2)}) collective-permute-start(f32[1,136,128]{2,1,0:T(8,128)} %bitcast.8), channel_id=1, source_target_pairs={{0,4},{1,5},{2,6},{3,7},{4,0},{5,1},{6,2},{7,3},{8,12},{9,13},{10,... | collective-permute-start | bytes 208904 | tf_op jit(solution)/shard_map/ppermute | solution.py:581
  20.4 6.2 %collective-permute-start.5 = (f32[1,136,128]{2,1,0:T(8,128)}, f32[1,136,128]{2,1,0:T(8,128)S(1)}, u32[]{:S(2)}, u32[]{:S(2)}) collective-permute-start(f32[1,136,128]{2,1,0:T(8,128)} %bitcast.9), channel_id=1, source_target_pairs={{0,8},{1,9},{2,10},{3,11},{4,12},{5,13},{6,14},{7,15},{8,0},{9,1},... | collective-permute-start | bytes 208904 | tf_op jit(solution)/shard_map/ppermute | solution.py:581
  23.0 6.3 %collective-permute-start.6 = (f32[1,136,128]{2,1,0:T(8,128)}, f32[1,136,128]{2,1,0:T(8,128)S(1)}, u32[]{:S(2)}, u32[]{:S(2)}) collective-permute-start(f32[1,136,128]{2,1,0:T(8,128)} %bitcast.10), channel_id=1, source_target_pairs={{0,12},{1,13},{2,14},{3,15},{4,8},{5,9},{6,10},{7,11},{8,4},{9,5},... | collective-permute-start | bytes 208904 | tf_op jit(solution)/shard_map/ppermute | solution.py:581
  30.2 10.1 %collective-permute-start.7 = (f32[4,136,128]{2,1,0:T(8,128)S(1)}, f32[4,136,128]{2,1,0:T(8,128)S(1)}, u32[]{:S(2)}, u32[]{:S(2)}) collective-permute-start(f32[4,136,128]{2,1,0:T(8,128)S(1)} %pad_maximum_fusion.1), channel_id=1, source_target_pairs={{0,2},{1,3},{2,0},{3,1},{4,6},{5,7},{6,4},{7,5},{8,10},{9,11},{10,... | collective-permute-start | bytes 835592 | tf_op jit(solution)/shard_map/ppermute | solution.py:581
  40.4 11.8 %copy-start.2 = (f32[8,136,128]{2,1,0:T(8,128)}, f32[8,136,128]{2,1,0:T(8,128)S(1)}, u32[]{:S(2)}) copy-start(f32[8,136,128]{2,1,0:T(8,128)S(1)} %constant_dynamic-update-slice_fusion.refs_0_) | copy-start | bytes 1671172
  40.4 11.8 %collective-permute-start.8 = (f32[8,136,128]{2,1,0:T(8,128)S(1)}, f32[8,136,128]{2,1,0:T(8,128)S(1)}, u32[]{:S(2)}, u32[]{:S(2)}) collective-permute-start(f32[8,136,128]{2,1,0:T(8,128)S(1)} %constant_dynamic-update-slice_fusion.refs_0_), channel_id=1, source_target_pairs={{0,1},{1,0},{2,3},{3,2},{4,5},{5,4},{6,7},{7,6},{8,9},{9,8},{10,11... | collective-permute-start | bytes 1671176 | tf_op jit(solution)/shard_map/ppermute | solution.py:581
  40.5 11.7 %collective-permute-start.2 = (f32[3,4,64,128]{3,2,1,0:T(8,128)S(1)}, f32[3,4,64,128]{3,2,1,0:T(8,128)S(1)}, u32[]{:S(2)}, u32[]{:S(2)}) collective-permute-start(f32[3,4,64,128]{3,2,1,0:T(8,128)S(1)} %copy-done.1), channel_id=1, source_target_pairs={{0,2},{2,4},{3,1},{4,6},{5,3},{6,8},{7,5},{8,10},{9,7},{10,12},{11... | collective-permute-start | bytes 1179656 | tf_op jit(solution)/shard_map/ppermute | solution.py:597
  42.7 9.5 %collective-permute-start.3 = (f32[3,4,64,128]{3,2,1,0:T(8,128)S(1)}, f32[3,4,64,128]{3,2,1,0:T(8,128)S(1)}, u32[]{:S(2)}, u32[]{:S(2)}) collective-permute-start(f32[3,4,64,128]{3,2,1,0:T(8,128)S(1)} %copy-done.5), channel_id=1, source_target_pairs={{0,1},{1,0},{2,3},{3,2},{4,5},{5,4},{6,7},{7,6},{8,9},{9,8},{10,11... | collective-permute-start | bytes 1179656 | tf_op jit(solution)/shard_map/ppermute | solution.py:581
  52.2 0.7 copy-start.7
  52.2 0.9 copy-start.8
  53.0 0.8 copy-start.3
  87.1 6.0 %collective-permute-start.10 = (f32[1,72,128]{2,1,0:T(8,128)}, f32[1,72,128]{2,1,0:T(8,128)S(1)}, u32[]{:S(2)}, u32[]{:S(2)}) collective-permute-start(f32[1,72,128]{2,1,0:T(8,128)} %bitcast.12), channel_id=1, source_target_pairs={{0,8},{1,9},{2,10},{3,11},{4,12},{5,13},{6,14},{7,15},{8,0},{9,1},... | collective-permute-start | bytes 110600 | tf_op jit(solution)/shard_map/ppermute | solution.py:581
  88.8 6.2 %collective-permute-start.11 = (f32[1,72,128]{2,1,0:T(8,128)}, f32[1,72,128]{2,1,0:T(8,128)S(1)}, u32[]{:S(2)}, u32[]{:S(2)}) collective-permute-start(f32[1,72,128]{2,1,0:T(8,128)} %bitcast.13), channel_id=1, source_target_pairs={{0,12},{1,13},{2,14},{3,15},{4,8},{5,9},{6,10},{7,11},{8,4},{9,5},... | collective-permute-start | bytes 110600 | tf_op jit(solution)/shard_map/ppermute | solution.py:581
  90.3 5.3 %collective-permute-start.9 = (f32[1,72,128]{2,1,0:T(8,128)}, f32[1,72,128]{2,1,0:T(8,128)S(1)}, u32[]{:S(2)}, u32[]{:S(2)}) collective-permute-start(f32[1,72,128]{2,1,0:T(8,128)} %bitcast.14), channel_id=1, source_target_pairs={{0,4},{1,5},{2,6},{3,7},{4,0},{5,1},{6,2},{7,3},{8,12},{9,13},{10,... | collective-permute-start | bytes 110600 | tf_op jit(solution)/shard_map/ppermute | solution.py:581
  96.4 5.9 %collective-permute-start.12 = (f32[4,72,128]{2,1,0:T(8,128)S(1)}, f32[4,72,128]{2,1,0:T(8,128)S(1)}, u32[]{:S(2)}, u32[]{:S(2)}) collective-permute-start(f32[4,72,128]{2,1,0:T(8,128)S(1)} %pad_maximum_fusion.2), channel_id=1, source_target_pairs={{0,2},{1,3},{2,0},{3,1},{4,6},{5,7},{6,4},{7,5},{8,10},{9,11},{10,... | collective-permute-start | bytes 442376 | tf_op jit(solution)/shard_map/ppermute | solution.py:581
  102.3 3.2 %copy-start.9 = (f32[8,72,128]{2,1,0:T(8,128)}, f32[8,72,128]{2,1,0:T(8,128)S(1)}, u32[]{:S(2)}) copy-start(f32[8,72,128]{2,1,0:T(8,128)S(1)} %constant_dynamic-update-slice_fusion.5.refs_0_) | copy-start | bytes 884740
  102.3 3.2 %collective-permute-start.13 = (f32[8,72,128]{2,1,0:T(8,128)S(1)}, f32[8,72,128]{2,1,0:T(8,128)S(1)}, u32[]{:S(2)}, u32[]{:S(2)}) collective-permute-start(f32[8,72,128]{2,1,0:T(8,128)S(1)} %constant_dynamic-update-slice_fusion.5.refs_0_), channel_id=1, source_target_pairs={{0,1},{1,0},{2,3},{3,2},{4,5},{5,4},{6,7},{7,6},{8,9},{9,8},{10,11... | collective-permute-start | bytes 884744 | tf_op jit(solution)/shard_map/ppermute | solution.py:581
  (1 other events, 0.7 us)
where the time goes:
time: 145 us
  Pallas kernels  66.8 us (46%)
  waiting for transfers between devices  29.7 us (20%)
  starting transfers between devices  24.9 us (17%)
  blocking collectives  11 us (8%)
  local copies, waits for them, and re-layouts  6.32 us (4%)
  other arithmetic  4.91 us (3%)
    pallas_call x4, Pallas kernels, call(): pl.pallas_call(body, out_shape=[full(o) for o in outs], in_specs=[SM] + [...  63.7 us
    ppermute x12, starting transfers between devices, exchange(): return lax.ppermute(x, 'gz', [(i, i ^ mask) for i in range(group)])  22 us
    ppermute x12, waiting for transfers between devices, exchange(): return lax.ppermute(x, 'gz', [(i, i ^ mask) for i in range(group)])  20.3 us
    all_to_all x1, blocking collectives, on_device(): got = lax.all_to_all(pay3, 'gz', 0, 0)  11 us
    ppermute x1, waiting for transfers between devices, skip_across(): return lax.ppermute(x, 'gz', pairs)  9.38 us
    unnamed x30, local copies, waits for them, and re-layouts  5.7 us
    pallas_call x1, Pallas kernels, on_device(): pl.pallas_call(functools.partial(phase_kernel, masks, layout, 4 * half),...  3.14 us
  transfers between devices with their start and end apart: 14, of which 8 were waited for; matrix products, arithmetic and copies ran while one was open for 3% of the time, Pallas kernels for 2%

commit v1 on v0

v1 whole, which is shorter than its diff:
```python
import functools
import math

import jax
import jax.numpy as jnp
import numpy as np
from jax import lax
from jax.experimental import pallas as pl
from jax.experimental.pallas import tpu as pltpu
from jax.sharding import PartitionSpec as P


ORD_HALF = 22
HELM_TABLE = ((-0.5, 0.0), (1.0, -1.4), (-1.2, 0.0))
SHIFT_TABLE = ((-0.5, -0.25), (1.0, -0.25 * math.sqrt(11.84)), (-1.2, -0.6))
RELAX = 0.8
KEEP = 1.0 - RELAX
PLANES = 4
OWN = 2 * PLANES
WINDOW = 5 * PLANES
PAD1 = 8
PAD2 = 4
H1 = 0.25
H2 = 0.0625
F32 = jnp.float32
VMEM_LIMIT = 28 * 2**20

WEIGHTS = tuple(RELAX / complex(6.0 + s[0], s[1]) for s in SHIFT_TABLE)


def pick(code, values):
    return jnp.where(
        code == 1.0,
        values[0],
        jnp.where(code == 2.0, values[1], jnp.where(code == 3.0, values[2], 0.0)),
    )


def weight_of(code):
    return pick(code, [w.real for w in WEIGHTS]), pick(code, [w.imag for w in WEIGHTS])


def shift_of(code):
    return pick(code, [s[0] for s in SHIFT_TABLE]), pick(code, [s[1] for s in SHIFT_TABLE])


def helm_of(code):
    return pick(code, [s[0] for s in HELM_TABLE]), pick(code, [s[1] for s in HELM_TABLE])


def cmul(ar, ai, br, bi):
    return ar * br - ai * bi, ar * bi + ai * br


HALO = 8
CHUNK = 16


def put(ref, c, p, r0, value, nx):
    n = value.shape[0]
    ref[c, p, pl.ds(HALO + r0, n), :] = value
    if r0 == 0:
        ref[c, p, pl.ds(HALO + nx, 1), :] = value[:1]
    if r0 + n == nx:
        ref[c, p, pl.ds(HALO - 1, 1), :] = value[n - 1 :]


def mid(ref, c, p, r0, n=CHUNK):
    return ref[c, p, pl.ds(HALO + r0, n), :]


def around(ref, p, r0, zero):
    sums = []
    for c in range(2):
        m = mid(ref, c, p, r0)
        ny = m.shape[1]
        total = mid(ref, c, p - 1, r0) + mid(ref, c, p + 1, r0)
        total = total + ref[c, p, pl.ds(HALO - 1 + r0 + zero, CHUNK), :]
        total = total + ref[c, p, pl.ds(HALO + 1 + r0 + zero, CHUNK), :]
        total = total + pltpu.roll(m, 1, 1) + pltpu.roll(m, ny - 1, 1)
        sums.append(total)
    return sums


def planes_of(lower, upper, nx, body, most=4):
    size = max(n for n in range(1, most + 1) if (upper - lower) % n == 0)

    def step(k, carry):
        for j in range(size):
            for r0 in range(0, nx, CHUNK):
                body(lower + k * size + j, r0, pl.ds(r0, CHUNK))
        return carry

    lax.fori_loop(0, (upper - lower) // size, step, 0)


def lanes(shape):
    return lax.broadcasted_iota(jnp.int32, shape, len(shape) - 1)


def put_packed(ref, p, count, value):
    n = value.shape[1]
    ref[pl.ds(p, count), pl.ds(HALO, n), :] = value
    ref[pl.ds(p, count), pl.ds(HALO + n, 1), :] = value[:, :1]
    ref[pl.ds(p, count), pl.ds(HALO - 1, 1), :] = value[:, n - 1 :]


def mid_packed(ref, p, count):
    return ref[pl.ds(p, count), pl.ds(HALO, ref.shape[1] - 2 * HALO), :]


def around_packed(ref, p, count, part, zero):
    m = mid_packed(ref, p, count)
    n, width = m.shape[1:]
    total = mid_packed(ref, p - 1, count) + mid_packed(ref, p + 1, count)
    total = total + ref[pl.ds(p, count), pl.ds(HALO - 1 + zero, n), :]
    total = total + ref[pl.ds(p, count), pl.ds(HALO + 1 + zero, n), :]
    at = lanes((1, 1, width)) % part
    before = jnp.where(at == 0, pltpu.roll(m, width + 1 - part, 2), pltpu.roll(m, 1, 2))
    after = jnp.where(at == part - 1, pltpu.roll(m, part - 1, 2), pltpu.roll(m, width - 1, 2))
    return total + before + after


def cmul_packed(wr, wi, g, part):
    return wr * g + wi * pltpu.roll(g, part, g.ndim - 1)


def weights_packed(shift, part, factor):
    other = pltpu.roll(shift, part, 1)
    real_lane = lanes(shift.shape) % (2 * part) < part
    dr = 6.0 * factor + jnp.where(real_lane, shift, other)
    di = jnp.where(real_lane, other, shift)
    scale = RELAX / (dr * dr + di * di)
    return jnp.where(real_lane, dr, -di) * scale


def dot(a, b):
    return jnp.dot(a, b, precision=lax.Precision.HIGHEST, preferred_element_type=F32)


def iota2(rows, cols):
    return (
        lax.broadcasted_iota(jnp.int32, (rows, cols), 0),
        lax.broadcasted_iota(jnp.int32, (rows, cols), 1),
    )


def restrict_fine(tmp):
    nx, ny = tmp.shape[1:]
    half = nx // 2
    rows = [tmp[c, pl.ds(0, half, stride=2), :] + tmp[c, pl.ds(1, half, stride=2), :] for c in range(2)]
    r, c = iota2(2 * ny, ny)
    pool = jnp.where(r // 2 == c, 0.125, 0.0).astype(F32)
    return dot(jnp.concatenate(rows, axis=1), pool)


def pool_level1(ny):
    r, c = iota2(ny, ny)
    return jnp.where(r // 2 == c % (ny // 2), 0.125, 0.0).astype(F32)


def full(shape_dtype):
    return jax.ShapeDtypeStruct(shape_dtype, F32)


VM = pl.BlockSpec(memory_space=pltpu.VMEM)
SM = pl.BlockSpec(memory_space=pltpu.SMEM)


def call(body, outs, inputs, scratch):
    size = sum(4 * math.prod(x.shape) for x in inputs) + sum(4 * math.prod(o) for o in outs)
    return pl.pallas_call(
        body,
        out_shape=[full(o) for o in outs],
        in_specs=[SM] + [VM] * (len(inputs) - 1),
        out_specs=[VM] * len(outs),
        scratch_shapes=[pltpu.VMEM(s, F32) for s in scratch],
        compiler_params=pltpu.CompilerParams(vmem_limit_bytes=VMEM_LIMIT),
        cost_estimate=pl.CostEstimate(flops=40 * size, bytes_accessed=size, transcendentals=0),
    )(*inputs)


def first_kernel(at, own, near, swap, orders, out, u, e1, u2, tmp, tmp1):
    odd, zero = at[1], at[2]
    nx, ny = own.shape[2:]

    def fill(block, lower, upper, first):
        def body(p, r0, rows):
            wr, wi = weight_of(block[2, p, rows])
            ur, ui = cmul(wr, wi, block[0, p, rows], block[1, p, rows])
            put(u, 0, first + p, r0, ur, nx)
            put(u, 1, first + p, r0, ui, nx)

        planes_of(lower, upper, nx, body)

    fill(own, 0, PLANES, 2)

    @pl.when(odd == 0)
    def _():
        fill(swap, 2, 4, -2)
        fill(near, 0, 2, 6)

    @pl.when(odd == 1)
    def _():
        fill(near, 2, 4, -2)
        fill(swap, 0, 2, 6)

    def smooth(p, block, q, r0, rows):
        sr, si = around(u, p, r0, zero)
        er = KEEP * block[0, q, rows] + sr
        ei = KEEP * block[1, q, rows] + si
        wr, wi = weight_of(block[2, q, rows])
        vr, vi = cmul(wr, wi, er, ei)
        put(u2, 0, p, r0, vr, nx)
        put(u2, 1, p, r0, vi, nx)
        return er, ei

    def inner(q, r0, rows):
        er, ei = smooth(2 + q, own, q, r0, rows)
        e1[0, q, rows] = er
        e1[1, q, rows] = ei

    planes_of(0, PLANES, nx, inner)

    def outer(block, q, p):
        planes_of(q, q + 1, nx, lambda q, r0, rows: smooth(p, block, q, r0, rows))

    @pl.when(odd == 0)
    def _():
        outer(swap, PLANES - 1, 1)
        outer(near, 0, 6)

    @pl.when(odd == 1)
    def _():
        outer(near, PLANES - 1, 1)
        outer(swap, 0, 6)

    half = nx // 2
    planes = []
    for q in range(PLANES // 2):
        for r0 in range(0, nx, CHUNK):
            rows = pl.ds(r0, CHUNK)
            total = [0.0, 0.0, 0.0, 0.0]
            for p in (2 * q, 2 * q + 1):
                s = around(u2, 2 + p, r0, zero)
                shift = shift_of(own[2, p, rows])
                for c in range(2):
                    total[c] = total[c] + KEEP * e1[c, p, rows] + s[c]
                    total[2 + c] = total[2 + c] + shift[c]
            for k in range(4):
                tmp[q, k // 2, k % 2, rows] = total[k]
        out[pl.ds(half * q, half), :] = restrict_fine(tmp.at[q, 0])
        shift = restrict_fine(tmp.at[q, 1])
        out[pl.ds(half * (2 + q), half), :] = weights_packed(shift, ny // 2, H1)
        planes.append(shift)
    tmp1[...] = planes[0] + planes[1]
    pooled = tmp1[pl.ds(0, half // 2, stride=2), :] + tmp1[pl.ds(1, half // 2, stride=2), :]
    shift2 = dot(pooled, pool_level1(ny))
    out[pl.ds(4 * half, half // 2), :] = weights_packed(shift2, ny // 4, H2)
    out[pl.ds(4 * half + half // 2, 8), :] = jnp.broadcast_to(orders[...], (8, ny))


def coarse_shapes(group, nx, ny):
    n1 = (2 * group + 2 * PAD1, nx // 2 + 2 * HALO, ny)
    n2 = (group + 2 * PAD2, nx // 4 + 2 * HALO, ny)
    return [n1[:1] + (nx // 2, ny), n1, n1, n1, n1, n2[:1] + (nx // 4, ny), n2, n2, (nx // 2, ny), (group * (nx // 2), ny)]


def clear_edges(ref, pad, count):
    zero = jnp.zeros(ref.shape[1:], F32)
    top = ref.shape[0] - pad
    for k in range(count):
        ref[pad - 1 - k] = zero
        ref[top + k] = zero


def coarse_weights(me, masks, pieces, w1r, w1i, w2r, w2i):
    half, ny = w1r.shape[1:]
    quarter = half // 2
    for ref, pad in ((w1r, PAD1), (w1i, PAD1), (w2r, PAD2), (w2i, PAD2)):
        clear_edges(ref, pad, pad - 1)

    def expand(w, part):
        other = pltpu.roll(w, part, 1)
        real_lane = lanes(w.shape) % (2 * part) < part
        return jnp.where(real_lane, w, other), jnp.where(real_lane, -other, w)

    for mask, (piece, j) in zip(masks, pieces, strict=True):
        d = me ^ mask
        for k in range(2):
            wr, wi = expand(piece[j, pl.ds(half * (2 + k), half), :], ny // 2)
            w1r[PAD1 + 2 * d + k] = wr
            w1i[PAD1 + 2 * d + k] = wi
        wr, wi = expand(piece[j, pl.ds(4 * half, quarter), :], ny // 4)
        w2r[PAD2 + d] = wr
        w2i[PAD2 + d] = wi


def chunked(lower, count, most, body):
    size = max(n for n in range(1, most + 1) if count % n == 0)

    def step(k, carry):
        body(lower + k * size, size)
        return carry

    lax.fori_loop(0, count // size, step, 0)


def coarse_solve(me, zero, masks, pieces, reach, w1r, w1i, w2r, w2i, g1, u1, u2, v1, e1, g2, va, vb, tmp, pool, out):
    half, ny = tmp.shape
    quarter = half // 2
    group = len(masks)
    part1, part2 = ny // 2, ny // 4
    n1 = 2 * group
    clear_edges(g1, PAD1, PAD1 - 1)
    clear_edges(u1, PAD1, 1)
    clear_edges(u2, PAD1, 1)
    clear_edges(v1, PAD1, PAD1 - 1)
    clear_edges(va, PAD2, 1)
    clear_edges(vb, PAD2, PAD2 - 1)
    for mask, (piece, j) in zip(masks, pieces, strict=True):
        p = PAD1 + 2 * (me ^ mask)
        g = piece[j, pl.ds(0, 2 * half), :].reshape(2, half, ny)
        g1[pl.ds(p, 2)] = g
        put_packed(u1, p, 2, cmul_packed(w1r[pl.ds(p, 2)], w1i[pl.ds(p, 2)], g, part1))

    def pre(p, n):
        e = KEEP * g1[pl.ds(p, n)] + H1 * around_packed(u1, p, n, part1, zero)
        u = cmul_packed(w1r[pl.ds(p, n)], w1i[pl.ds(p, n)], e, part1)
        e1[pl.ds(p, n), pl.ds(0, half), :] = e
        put_packed(u2, p, n, u)
        put_packed(v1, p, n, mid_packed(u1, p, n) + u)

    chunked(PAD1, n1, 8, pre)

    def coarser(p, n):
        e = KEEP * e1[pl.ds(p, n), pl.ds(0, half), :] + H1 * around_packed(u2, p, n, part1, zero)
        e = e.reshape(n // 2, 2, half, ny)
        pairs = (e[:, 0] + e[:, 1]).reshape(n // 2 * half, ny)
        pool[pl.ds((p - PAD1) // 2 * half, n // 2 * half), :] = pairs

    chunked(PAD1, n1, 8, coarser)
    rows = group * quarter
    flat = pool[pl.ds(0, rows, stride=2), :] + pool[pl.ds(1, rows, stride=2), :]
    r2 = dot(flat, pool_level1(ny)).reshape(group, quarter, ny)
    inside = pl.ds(PAD2, group)
    g2[inside] = r2
    put_packed(va, PAD2, group, cmul_packed(w2r[inside], w2i[inside], r2, part2))
    for src, dst in ((va, vb), (vb, va), (va, vb)):

        def sweep(p, n, src=src, dst=dst):
            s = g2[pl.ds(p, n)] + H2 * around_packed(src, p, n, part2, zero)
            v = KEEP * mid_packed(src, p, n) + cmul_packed(w2r[pl.ds(p, n)], w2i[pl.ds(p, n)], s, part2)
            put_packed(dst, p, n, v)

        chunked(PAD2, group, 16, sweep)
    reach2 = (reach + 2) // 2
    count = 2 * reach2 + 1
    flat = mid_packed(vb, PAD2 + me - reach2, count).reshape(count * quarter, ny)
    r, c = iota2(ny, ny)
    spread = jnp.where(c // 2 == r, 1.0, 0.0).astype(F32)
    e2 = dot(flat, spread)
    pool[pl.ds(0, count * quarter, stride=2), :] = e2
    pool[pl.ds(1, count * quarter, stride=2), :] = e2
    base = PAD1 + 2 * (me - reach2)
    for k in range(count):
        add = pool[pl.ds(k * half, half), :]
        both = mid_packed(v1, base + 2 * k, 2) + add[None]
        put_packed(v1, base + 2 * k, 2, both)

    def post(src, p, n):
        s = g1[pl.ds(p, n)] + H1 * around_packed(src, p, n, part1, zero)
        return KEEP * mid_packed(src, p, n) + cmul_packed(w1r[pl.ds(p, n)], w1i[pl.ds(p, n)], s, part1)

    start = PAD1 + 2 * me

    def third(p, n):
        put_packed(u1, p, n, post(v1, p, n))

    def fourth(p, n):
        out[pl.ds(p - (start - reach), n)] = post(u1, p, n)

    chunked(start - reach - 1, 2 * reach + 4, 6, third)
    chunked(start - reach, 2 * reach + 2, 5, fourth)


def add_correction(ec, v, tmp, planes, nx):
    half, ny = ec.shape[1:]
    r, c = iota2(ny, 2 * ny)
    spread = jnp.where(c // 2 == r, 1.0, 0.0).astype(F32)

    def body(m, carry):
        k = 2 * m
        both = dot(ec[pl.ds(k, 2)].reshape(2 * half, ny), spread)
        for j in range(2):
            for c in range(2):
                e = both[j * half : (j + 1) * half, c * ny : (c + 1) * ny]
                tmp[j, c, pl.ds(0, half, stride=2), :] = e
                tmp[j, c, pl.ds(1, half, stride=2), :] = e
        for j in range(2):
            for c in range(2):
                for r0 in range(0, nx, CHUNK):
                    add = tmp[j, c, pl.ds(r0, CHUNK)]
                    for p in (2 * (k + j), 2 * (k + j) + 1):
                        put(v, c, p, r0, mid(v, c, p, r0) + add, nx)
        return carry

    lax.fori_loop(0, planes // 2, body, 0)


def second_kernel(masks, layout, at, own, near, swap, skip, far, *refs):
    n = max(i for i, _ in layout) + 1
    gathered, refs = refs[:n], refs[n:]
    (direction, image, smooth2, weight8, pay, w1r, w1i, w2r, w2i), refs = refs[:9], refs[9:]
    f, weight, u, u2, v, code, tmp, ec, e1 = refs[:9]
    coarse = refs[9:]
    me, odd, zero = at[0], at[1], at[2]
    nx, ny = own.shape[2:]
    pieces = [(gathered[i], j) for i, j in layout]

    def fill(block, first):
        def body(q, r0, rows):
            p = first + q
            c = block[2, q, rows]
            wr, wi = weight_of(c)
            fr, fi = block[0, q, rows], block[1, q, rows]
            ur, ui = cmul(wr, wi, fr, fi)
            f[0, p, rows], f[1, p, rows] = fr, fi
            weight[0, p, rows], weight[1, p, rows] = wr, wi
            put(u, 0, p, r0, ur, nx)
            put(u, 1, p, r0, ui, nx)
            code[p, rows] = c

        planes_of(0, PLANES, nx, body)

    fill(own, OWN)
    fill(near, OWN + PLANES - 2 * PLANES * odd)
    fill(swap, OWN - PLANES + 2 * PLANES * odd)
    fill(skip, 4 * PLANES * odd)
    fill(far, 4 * PLANES - 4 * PLANES * odd)

    def pre(p, r0, rows):
        sr, si = around(u, p, r0, zero)
        er = KEEP * f[0, p, rows] + sr
        ei = KEEP * f[1, p, rows] + si
        vr, vi = cmul(weight[0, p, rows], weight[1, p, rows], er, ei)
        put(v, 0, p, r0, mid(u, 0, p, r0) + vr, nx)
        put(v, 1, p, r0, mid(u, 1, p, r0) + vi, nx)

    planes_of(1, WINDOW - 1, nx, pre, 6)
    coarse_weights(me, masks, pieces, w1r, w1i, w2r, w2i)
    coarse_solve(me, zero, masks, pieces, 4, w1r, w1i, w2r, w2i, *coarse, ec)
    add_correction(ec, v, tmp, WINDOW // 2, nx)

    def sweep(src, dst, p, r0, rows):
        sr, si = around(src, p, r0, zero)
        vr, vi = cmul(weight[0, p, rows], weight[1, p, rows], f[0, p, rows] + sr, f[1, p, rows] + si)
        put(dst, 0, p, r0, KEEP * mid(src, 0, p, r0) + vr, nx)
        put(dst, 1, p, r0, KEEP * mid(src, 1, p, r0) + vi, nx)

    planes_of(2, WINDOW - 2, nx, lambda *a: sweep(v, u, *a))
    planes_of(3, WINDOW - 3, nx, lambda *a: sweep(u, v, *a), 7)

    def apply(p, r0, rows):
        sr, si = around(v, p, r0, zero)
        c = code[p, rows]
        hr, hi = helm_of(c)
        vr, vi = mid(v, 0, p, r0), mid(v, 1, p, r0)
        ar, ai = cmul(hr, hi, vr, vi)
        ar = jnp.where(c > 0.0, ar + 6.0 * vr - sr, 0.0)
        ai = jnp.where(c > 0.0, ai + 6.0 * vi - si, 0.0)
        image[0, p - 4, rows] = ar
        image[1, p - 4, rows] = ai
        ur, ui = cmul(weight[0, p, rows], weight[1, p, rows], ar, ai)
        put(u, 0, p, r0, ur, nx)
        put(u, 1, p, r0, ui, nx)

    planes_of(4, WINDOW - 4, nx, apply)
    rho, cross_r, cross_i = 0.0, 0.0, 0.0
    for q in range(PLANES):
        for r0 in range(0, nx, CHUNK):
            rows = pl.ds(r0, CHUNK)
            fr, fi = own[0, q, rows], own[1, q, rows]
            ir, ii = image[0, OWN - 4 + q, rows], image[1, OWN - 4 + q, rows]
            rho = rho + fr * fr + fi * fi
            cross_r = cross_r + fr * ir + fi * ii
            cross_i = cross_i + fr * ii - fi * ir
            for c in range(2):
                direction[c, q, rows] = mid(v, c, OWN + q, r0)
    half = nx // 2
    row = lax.broadcasted_iota(jnp.int32, (8, ny), 0)
    sums = [jnp.sum(t, axis=0, keepdims=True) for t in (rho, cross_r, cross_i)]
    tail = jnp.where(row == 0, sums[0], jnp.where(row == 1, sums[1], jnp.where(row == 2, sums[2], 0.0)))
    pay[pl.ds(2 * half, 8), :] = tail

    def pre2(p, r0, rows):
        sr, si = around(u, p, r0, zero)
        er = KEEP * image[0, p - 4, rows] + sr
        ei = KEEP * image[1, p - 4, rows] + si
        vr, vi = cmul(weight[0, p, rows], weight[1, p, rows], er, ei)
        e1[0, p, rows], e1[1, p, rows] = er, ei
        put(u2, 0, p, r0, vr, nx)
        put(u2, 1, p, r0, vi, nx)
        smooth2[0, p - 5, rows] = mid(u, 0, p, r0) + vr
        smooth2[1, p - 5, rows] = mid(u, 1, p, r0) + vi

    planes_of(5, WINDOW - 5, nx, pre2, 5)
    for q in range(PLANES // 2):
        for r0 in range(0, nx, CHUNK):
            rows = pl.ds(r0, CHUNK)
            total = [0.0, 0.0]
            for k in range(2):
                p = OWN + 2 * q + k
                s = around(u2, p, r0, zero)
                for c in range(2):
                    total[c] = total[c] + KEEP * e1[c, p, rows] + s[c]
            for c in range(2):
                tmp[q, c, rows] = total[c]
        pay[pl.ds(half * q, half), :] = restrict_fine(tmp.at[q])

    def copy(p, r0, rows):
        for c in range(2):
            weight8[c, p, rows] = weight[c, p + OWN - 2, rows]

    planes_of(0, PLANES + 4, nx, copy)


def phase_kernel(masks, layout, row, at, *refs):
    n = max(i for i, _ in layout) + 1
    gathered = refs[:n]
    table, qrow, found = refs[n:]
    me = at[0]
    ny = found.shape[1]
    nx = table.shape[0] // 2
    for mask, (i, j) in zip(masks, layout, strict=True):
        found[pl.ds(me ^ mask, 1), :] = gathered[i][j, pl.ds(row, 1), :]
    low = lanes((1, ny)) < ny // 2
    x = lax.broadcasted_iota(jnp.int32, (nx, ny), 0)
    for pair in range(len(masks) // 2):
        even = found[pl.ds(2 * pair, 1), :]
        odd = found[pl.ds(2 * pair + 1, 1), :]
        p = jnp.where(low, even, pltpu.roll(odd, ny // 2, 1))
        q = jnp.where(low, pltpu.roll(even, ny // 2, 1), odd)
        turns = (x * p.astype(jnp.int32)) & (nx - 1)
        angle = turns.astype(F32) * (2.0 * math.pi / nx)
        table[pl.ds(0, nx), pl.ds(pair * ny, ny)] = jnp.cos(angle)
        table[pl.ds(nx, nx), pl.ds(pair * ny, ny)] = -jnp.sin(angle)
        qrow[:, pl.ds(pair * ny, ny)] = jnp.broadcast_to(q, (8, ny))


def third_kernel(
    masks, layout, at, own, direction, image, smooth2, weight8, w1r, w1i, w2r, w2i, ytable, xtable, qrow, *refs
):
    n = max(i for i, _ in layout) + 1
    gathered, refs = refs[:n], refs[n:]
    (corrected, last_image, halfway, pay, alpha), refs = refs[:5], refs[5:]
    u, v, tmp, ec = refs[:4]
    coarse = refs[4:]
    me, zero = at[0], at[2]
    pieces = [(gathered[i], j) for i, j in layout]
    nx, ny = own.shape[2:]
    half = nx // 2
    coarse_solve(me, zero, masks, pieces, 2, w1r, w1i, w2r, w2i, *coarse, ec)

    def take(p, r0, rows):
        for c in range(2):
            put(v, c, p, r0, smooth2[c, p - 1, rows], nx)

    planes_of(1, 11, nx, take)
    add_correction(ec, v, tmp, 6, nx)

    def sweep(src, dst, p, r0, rows):
        sr, si = around(src, p, r0, zero)
        wr, wi = weight8[0, p - 2, rows], weight8[1, p - 2, rows]
        vr, vi = cmul(wr, wi, image[0, p, rows] + sr, image[1, p, rows] + si)
        put(dst, 0, p, r0, KEEP * mid(src, 0, p, r0) + vr, nx)
        put(dst, 1, p, r0, KEEP * mid(src, 1, p, r0) + vi, nx)

    planes_of(2, 10, nx, lambda *a: sweep(v, u, *a))
    planes_of(3, 9, nx, lambda *a: sweep(u, v, *a))

    sums = 0.0
    for i, j in layout:
        sums = sums + gathered[i][j, pl.ds(2 * half, 8), :]
    rho, cr, ci = [jnp.sum(sums[k : k + 1], axis=1, keepdims=True) for k in range(3)]
    modulus = cr * cr + ci * ci
    ar = rho * cr / modulus
    ai = -rho * ci / modulus
    dots = [0.0, 0.0, 0.0]
    for q in range(PLANES):
        for r0 in range(0, nx, CHUNK):
            rows = pl.ds(r0, CHUNK)
            p = 4 + q
            sr, si = around(v, p, r0, zero)
            hr, hi = helm_of(own[2, q, rows])
            wr, wi = mid(v, 0, p, r0), mid(v, 1, p, r0)
            br, bi = cmul(hr, hi, wr, wi)
            br, bi = br + 6.0 * wr - sr, bi + 6.0 * wi - si
            ir, ii = image[0, p, rows], image[1, p, rows]
            br, bi = cmul(ar, ai, br, bi)
            lr, li = ir - br, ii - bi
            tr, ti = cmul(ar, ai, ir, ii)
            hr, hi = own[0, q, rows] - tr, own[1, q, rows] - ti
            xr, xi = cmul(ar, ai, wr, wi)
            corrected[0, q, rows], corrected[1, q, rows] = direction[0, q, rows] - xr, direction[1, q, rows] - xi
            last_image[0, q, rows], last_image[1, q, rows] = lr, li
            halfway[0, q, rows], halfway[1, q, rows] = hr, hi
            dots[0] = dots[0] + lr * hr + li * hi
            dots[1] = dots[1] + lr * hi - li * hr
            dots[2] = dots[2] + lr * lr + li * li
    dots = [jnp.sum(t, axis=0, keepdims=True) for t in dots]
    row = lax.broadcasted_iota(jnp.int32, (8, ny), 0)
    alpha[...] = jnp.where(row == 0, ar, ai)

    sign = jnp.where(lanes((nx, ny)) < ny // 2, -1.0, 1.0)
    stacked = []
    for field in (direction, corrected):
        plane = field[:, PLANES - 1].reshape(2 * nx, ny)
        m = lax.dot_general(
            ytable[...],
            plane,
            (((1,), (1,)), ((), ())),
            precision=lax.Precision.HIGHEST,
            preferred_element_type=F32,
        )
        t = m[:nx] + sign * pltpu.roll(m[nx:], nx, 1)
        stacked += [-sign * t, pltpu.roll(t, nx, 1)]
    spectrum = dot(jnp.concatenate(stacked, axis=0), xtable[...])
    scale = 1.0 / math.sqrt(nx * ny)
    at_row = lax.broadcasted_iota(jnp.int32, (nx, ny), 0).astype(F32) - ORD_HALF
    for pair in range(len(masks) // 2):
        chosen = at_row == qrow[0:1, pair * ny : (pair + 1) * ny]
        found = [
            scale
            * jnp.sum(
                jnp.where(chosen, spectrum[k * nx : (k + 1) * nx, pair * ny : (pair + 1) * ny], 0.0),
                axis=0,
                keepdims=True,
            )
            for k in range(4)
        ]
        block = 0.0
        for k, line in enumerate(found + dots):
            block = jnp.where(row == k, line, block)
        pay[2 * pair] = block
        pay[2 * pair + 1] = block


def last_kernel(at, direction, corrected, last_image, halfway, alpha, got, solution, residual, pupil):
    group = got.shape[0]
    nx, ny = direction.shape[2:]
    total = got[0]
    for k in range(1, group):
        total = total + got[k]
    along_r, along_i, norm = [jnp.sum(total[k : k + 1], axis=1, keepdims=True) for k in (4, 5, 6)]
    wr = along_r / norm
    wi = along_i / norm
    ar = alpha[0:1, 0:1]
    ai = alpha[1:2, 0:1]
    for q in range(PLANES):
        for r0 in range(0, nx, CHUNK):
            rows = pl.ds(r0, CHUNK)
            xr, xi = cmul(ar, ai, direction[0, q, rows], direction[1, q, rows])
            yr, yi = cmul(wr, wi, corrected[0, q, rows], corrected[1, q, rows])
            solution[0, q, rows], solution[1, q, rows] = xr + yr, xi + yi
            zr, zi = cmul(wr, wi, last_image[0, q, rows], last_image[1, q, rows])
            residual[0, q, rows], residual[1, q, rows] = halfway[0, q, rows] - zr, halfway[1, q, rows] - zi
    tip = got[group - 1]
    xr, xi = cmul(ar, ai, tip[0:1], tip[1:2])
    yr, yi = cmul(wr, wi, tip[2:3], tip[3:4])
    both = jnp.concatenate([xr + yr, xi + yi] * 4, axis=0)
    both = jnp.where(at[1] == 1, pltpu.roll(both, ny // 2, 1), both)
    pupil[...] = both[:2, : ny // 2]


def exchange(x, mask, group):
    return lax.ppermute(x, "gz", [(i, i ^ mask) for i in range(group)])


def swap_across(x, group):
    pairs = []
    for i in range(1, group - 1, 2):
        pairs += [(i, i + 1), (i + 1, i)]
    return lax.ppermute(x, "gz", pairs)


def skip_across(x, group):
    pairs = []
    for i in range(group):
        target = i + 2 if i % 2 == 0 else i - 2
        if 0 <= target < group:
            pairs.append((i, target))
    return lax.ppermute(x, "gz", pairs)


def stages_of(group):
    stages = [[1]]
    stride = 2
    left = group // 2
    if left.bit_length() % 2 == 0:
        stages.insert(0, [stride])
        stride, left = 2 * stride, left // 2
    while left > 1:
        stages.insert(0, [stride, 2 * stride, 3 * stride])
        stride, left = 4 * stride, left // 4
    return stages


def gather(x, group):
    have, masks = x[None], [0]
    stages = stages_of(group)
    for masks_now in stages[:-1]:
        got = [exchange(have, m, group) for m in masks_now]
        masks = masks + [k ^ m for m in masks_now for k in masks]
        have = jnp.concatenate([have] + got, axis=0)
    (m,) = stages[-1]
    other = exchange(have, m, group)
    count = len(masks)
    layout = [(0, j) for j in range(count)] + [(1, j) for j in range(count)]
    return [have, other], masks + [k ^ m for k in masks], layout


def y_phases(nx, ny):
    q = np.arange(nx) - ORD_HALF
    turns = (q[:, None] * np.arange(ny)[None, :]) % ny
    angle = turns.astype(np.float64) * (2.0 * np.pi / ny)
    return np.concatenate([np.cos(angle), -np.sin(angle)], axis=0).astype(np.float32)


def on_device(source_term, material, orders):
    group = lax.axis_size("gz")
    _, planes, nx, ny = source_term.shape
    assert planes == PLANES and 2 * nx == ny and 2 * orders.shape[1] == ny
    me = lax.axis_index("gz")
    at = jnp.stack([me, me % 2, me * 0]).astype(jnp.int32)
    half = nx // 2

    own = jnp.concatenate([source_term, (material + 1).astype(F32)[None]], axis=0)
    near = exchange(own, 1, group)
    swap = swap_across(own, group)
    order_row = orders.astype(F32).reshape(1, ny)
    fine = (2, PLANES, nx, ny)
    tall = nx + 2 * HALO
    (pay1,) = call(
        first_kernel,
        [(4 * half + half // 2 + 8, ny)],
        [at, own, near, swap, order_row],
        [(2, 8, tall, ny), fine, (2, 8, tall, ny), (2, 2, 2, nx, ny), (half, ny)],
    )
    gathered1, masks, layout = gather(pay1, group)
    skip = skip_across(own, group)
    far = exchange(swap, 1, group)

    window = (2, WINDOW, nx, ny)
    haloed = (2, WINDOW, tall, ny)
    shapes1 = (2 * group + 2 * PAD1, half, ny)
    shapes2 = (group + 2 * PAD2, half // 2, ny)
    direction, image, smooth2, weight8, pay2, w1r, w1i, w2r, w2i = call(
        functools.partial(second_kernel, masks, layout),
        [
            fine,
            (2, 12, nx, ny),
            (2, 10, nx, ny),
            (2, PLANES + 4, nx, ny),
            (2 * half + 8, ny),
            shapes1,
            shapes1,
            shapes2,
            shapes2,
        ],
        [at, own, near, swap, skip, far, *gathered1],
        [window, window, haloed, haloed, haloed, (WINDOW, nx, ny), (2, 2, nx, ny), (10, half, ny), window]
        + coarse_shapes(group, nx, ny),
    )
    xtable, qrow = call(
        functools.partial(phase_kernel, masks, layout, 4 * half + half // 2),
        [(2 * nx, group * ny // 2), (8, group * ny // 2)],
        [at, *gathered1],
        [(group, ny)],
    )
    gathered2, masks, layout = gather(pay2, group)
    corrected, last_image, halfway, pay3, alpha = call(
        functools.partial(third_kernel, masks, layout),
        [fine, fine, fine, (group, 8, ny), (8, ny)],
        [
            at,
            own,
            direction,
            image,
            smooth2,
            weight8,
            w1r,
            w1i,
            w2r,
            w2i,
            jnp.asarray(y_phases(nx, ny)),
            xtable,
            qrow,
            *gathered2,
        ],
        [(2, 12, tall, ny), (2, 12, tall, ny), (2, 2, nx, ny), (6, half, ny)] + coarse_shapes(group, nx, ny),
    )
    got = lax.all_to_all(pay3, "gz", 0, 0)
    solution, residual, pupil = call(
        last_kernel, [fine, fine, (2, ny // 2)], [at, direction, corrected, last_image, halfway, alpha, got], []
    )
    return solution, residual, pupil


def solution(mesh):
    return jax.shard_map(
        on_device,
        mesh=mesh,
        in_specs=(
            P(None, ("clip", "gz"), None, None),
            P(("clip", "gz"), None, None),
            P(None, "gz"),
        ),
        out_specs=(
            P(None, ("clip", "gz"), None, None),
            P(None, ("clip", "gz"), None, None),
            P(None, ("clip", "gz")),
        ),
        check_vma=False,
    )
```

time: 145 us -> 95.7 us (0.66)
  Pallas kernels: 66.8 us -> 23.5 us
  local copies, waits for them, and re-layouts: 6.32 us -> 0.89 us
  other arithmetic: 4.91 us -> 1.1 us
  waiting for transfers between devices: 29.7 us -> 32.7 us
    pallas_call x4 -> x5, Pallas kernels: 63.7 us -> 23.5 us  [call(): pl.pallas_call(body, out_shape=[full(o) for o in outs], in_specs=[SM] + [...]
    unnamed x30 -> x14, local copies, waits for them, and re-layouts: 5.7 us -> 0.77 us
    pallas_call x1 -> x0, Pallas kernels: 3.14 us -> none  [on_device(): pl.pallas_call(functools.partial(phase_kernel, masks, layout, 4 * half),...]
    ppermute x12, waiting for transfers between devices: 20.3 us -> 23.3 us  [exchange(): return lax.ppermute(x, 'gz', [(i, i ^ mask) for i in range(group)])]
    concatenate x2, other arithmetic: 1.69 us -> 0.04 us  [gather(): have = jnp.concatenate([have] + got, axis=0)]
  transfers between devices with their start and end apart: 14 -> 14, of which waited for: 8 -> 9; matrix products, arithmetic and copies ran while one was open for 3% -> 0% of each run, Pallas kernels for 2% -> 2%
where the time goes in v1:
time: 95.7 us; the launch traced here: 95.5 us
  waiting for transfers between devices  32.7 us (34%)
  starting transfers between devices  25.8 us (27%)
  Pallas kernels  23.5 us (25%)
  blocking collectives  10.7 us (11%)
  other arithmetic  1.1 us (1%)
    pallas_call x5, Pallas kernels, call(): pl.pallas_call(body, out_shape=[full(o) for o in outs], in_specs=[SM] + [...  23.5 us
    ppermute x12, waiting for transfers between devices, exchange(): return lax.ppermute(x, 'gz', [(i, i ^ mask) for i in range(group)])  23.3 us
    ppermute x12, starting transfers between devices, exchange(): return lax.ppermute(x, 'gz', [(i, i ^ mask) for i in range(group)])  22.9 us
    all_to_all x1, blocking collectives, on_device(): got = lax.all_to_all(pay3, 'gz', 0, 0)  10.7 us
    ppermute x1, waiting for transfers between devices, skip_across(): return lax.ppermute(x, 'gz', pairs)  9.39 us
    ppermute x1, starting transfers between devices, skip_across(): return lax.ppermute(x, 'gz', pairs)  2.21 us
  transfers between devices with their start and end apart: 14, of which 9 were waited for; matrix products, arithmetic and copies ran while one was open for 0% of the time, Pallas kernels for 2%

profile of v1, /device:TPU:0, one launch (start us, length us, event | category | flops | bytes accessed | tf_op | source)
XLA Modules:
  0.0 95.5 jit_solution(8044218375879417655)
XLA Ops:
  0.6 1.0 %convert_bitcast_fusion = f32[1,4,64,128]{3,2,1,0:T(8,128)S(1)} fusion(s32[4,64,128]{2,1,0:T(8,128)} %param.5), kind=kLoop, calls=%fused_computation.3 | loop fusion | flops 65536 | bytes 262144 | tf_op jit(solution)/shard_map/broadcast_in_dim | solution.py:738
  1.7 0.7 collective-permute-start.1
  2.4 4.4 %collective-permute-start = (f32[3,4,64,128]{3,2,1,0:T(8,128)S(1)}, f32[3,4,64,128]{3,2,1,0:T(8,128)S(1)}, u32[]{:S(2)}, u32[]{:S(2)}) collective-permute-start(f32[3,4,64,128]{3,2,1,0:T(8,128)S(1)} %pad_maximum_fusion.own), channel_id=1, source_target_pairs={{0,1},{1,0},{2,3},{3,2},{4,5},{5,4},{6,7},{7,6},{8,9},{9,8},{10,11... | collective-permute-start | bytes 1179656 | tf_op jit(solution)/shard_map/ppermute | solution.py:677
  6.8 0.7 copy-done.2
  8.1 1.8 %shard_map.67 = f32[152,128]{1,0:T(8,128)S(1)} custom-call(s32[3]{0:T(128)S(1)} %pad_add_fusion.at, f32[3,4,64,128]{3,2,1,0:T(8,128)S(1)} %pad_maximum_fusion.own, f32[3,4,64,128]{3,2,1,0:T(8,128)S(1)} %collective-permute-done.near, f32[3,4,64,128]{3,2,1,0:T(8,128)S(1)} %collective-permute-done.1.swap, f32[1,128]{1,0:T(1,128)S(1)} %reshape.9.orders), custom_call_target="tpu_custom_call" | custom-call | flops 50319840 | bytes 1257996 | tf_op jit(solution)/shard_map/pallas_call | solution.py:172
  9.9 6.8 %collective-permute-start.4 = (f32[1,152,128]{2,1,0:T(8,128)S(1)}, f32[1,152,128]{2,1,0:T(8,128)S(1)}, u32[]{:S(2)}, u32[]{:S(2)}) collective-permute-start(f32[1,152,128]{2,1,0:T(8,128)S(1)} %bitcast.8), channel_id=1, source_target_pairs={{0,4},{1,5},{2,6},{3,7},{4,0},{5,1},{6,2},{7,3},{8,12},{9,13},{10,... | collective-permute-start | bytes 233480 | tf_op jit(solution)/shard_map/ppermute | solution.py:677
  16.7 2.6 %collective-permute-start.5 = (f32[1,152,128]{2,1,0:T(8,128)S(1)}, f32[1,152,128]{2,1,0:T(8,128)S(1)}, u32[]{:S(2)}, u32[]{:S(2)}) collective-permute-start(f32[1,152,128]{2,1,0:T(8,128)S(1)} %bitcast.9), channel_id=1, source_target_pairs={{0,8},{1,9},{2,10},{3,11},{4,12},{5,13},{6,14},{7,15},{8,0},{9,1},... | collective-permute-start | bytes 233480 | tf_op jit(solution)/shard_map/ppermute | solution.py:677
  19.3 3.5 %collective-permute-done.5 = f32[1,152,128]{2,1,0:T(8,128)S(1)} collective-permute-done((f32[1,152,128]{2,1,0:T(8,128)S(1)}, f32[1,152,128]{2,1,0:T(8,128)S(1)}, u32[]{:S(2)}, u32[]{:S(2)}) %collective-permute-start.5) | collective-permute-done | bytes 77856 | tf_op jit(solution)/shard_map/ppermute | solution.py:677
  22.8 2.7 %collective-permute-done.6 = f32[1,152,128]{2,1,0:T(8,128)S(1)} collective-permute-done((f32[1,152,128]{2,1,0:T(8,128)S(1)}, f32[1,152,128]{2,1,0:T(8,128)S(1)}, u32[]{:S(2)}, u32[]{:S(2)}) %collective-permute-start.6) | collective-permute-done | bytes 77856 | tf_op jit(solution)/shard_map/ppermute | solution.py:677
  25.5 3.4 %collective-permute-start.7 = (f32[4,152,128]{2,1,0:T(8,128)S(1)}, f32[4,152,128]{2,1,0:T(8,128)S(1)}, u32[]{:S(2)}, u32[]{:S(2)}) collective-permute-start(f32[4,152,128]{2,1,0:T(8,128)S(1)} %pad_maximum_fusion.1), channel_id=1, source_target_pairs={{0,2},{1,3},{2,0},{3,1},{4,6},{5,7},{6,4},{7,5},{8,10},{9,11},{10,... | collective-permute-start | bytes 933896 | tf_op jit(solution)/shard_map/ppermute | solution.py:677
  28.9 7.4 %collective-permute-done.7 = f32[4,152,128]{2,1,0:T(8,128)S(1)} collective-permute-done((f32[4,152,128]{2,1,0:T(8,128)S(1)}, f32[4,152,128]{2,1,0:T(8,128)S(1)}, u32[]{:S(2)}, u32[]{:S(2)}) %collective-permute-start.7) | collective-permute-done | bytes 311328 | tf_op jit(solution)/shard_map/ppermute | solution.py:677
  36.5 2.2 %collective-permute-start.2 = (f32[3,4,64,128]{3,2,1,0:T(8,128)S(1)}, f32[3,4,64,128]{3,2,1,0:T(8,128)S(1)}, u32[]{:S(2)}, u32[]{:S(2)}) collective-permute-start(f32[3,4,64,128]{3,2,1,0:T(8,128)S(1)} %pad_maximum_fusion.own), channel_id=1, source_target_pairs={{0,2},{2,4},{3,1},{4,6},{5,3},{6,8},{7,5},{8,10},{9,7},{10,12},{11... | collective-permute-start | bytes 1179656 | tf_op jit(solution)/shard_map/ppermute | solution.py:693
  38.8 9.4 %collective-permute-done.2.skip = f32[3,4,64,128]{3,2,1,0:T(8,128)S(1)} collective-permute-done((f32[3,4,64,128]{3,2,1,0:T(8,128)S(1)}, f32[3,4,64,128]{3,2,1,0:T(8,128)S(1)}, u32[]{:S(2)}, u32[]{:S(2)}) %collective-permute-start.2) | collective-permute-done | bytes 393248 | tf_op jit(solution)/shard_map/ppermute | solution.py:693
  48.1 10.7 %shard_map.68 = (f32[2,4,64,128]{3,2,1,0:T(8,128)S(1)}, f32[2,12,64,128]{3,2,1,0:T(8,128)S(1)}, f32[2,10,64,128]{3,2,1,0:T(8,128)S(1)}, f32[2,8,64,128]{3,2,1,0:...) custom-call(s32[3]{0:T(128)S(1)} %pad_add_fusion.at, ...), custom_call_target="tpu_custom_call" | custom-call | flops 297697760 | bytes 7442444 | tf_op jit(solution)/shard_map/pallas_call | solution.py:172
  58.8 2.3 %collective-permute-start.10 = (f32[1,72,128]{2,1,0:T(8,128)S(1)}, f32[1,72,128]{2,1,0:T(8,128)S(1)}, u32[]{:S(2)}, u32[]{:S(2)}) collective-permute-start(f32[1,72,128]{2,1,0:T(8,128)S(1)} %bitcast.12), channel_id=1, source_target_pairs={{0,8},{1,9},{2,10},{3,11},{4,12},{5,13},{6,14},{7,15},{8,0},{9,1},... | collective-permute-start | bytes 110600 | tf_op jit(solution)/shard_map/ppermute | solution.py:677
  61.1 1.3 %collective-permute-start.11 = (f32[1,72,128]{2,1,0:T(8,128)S(1)}, f32[1,72,128]{2,1,0:T(8,128)S(1)}, u32[]{:S(2)}, u32[]{:S(2)}) collective-permute-start(f32[1,72,128]{2,1,0:T(8,128)S(1)} %bitcast.13), channel_id=1, source_target_pairs={{0,12},{1,13},{2,14},{3,15},{4,8},{5,9},{6,10},{7,11},{8,4},{9,5},... | collective-permute-start | bytes 110600 | tf_op jit(solution)/shard_map/ppermute | solution.py:677
  62.5 1.5 %collective-permute-done.10 = f32[1,72,128]{2,1,0:T(8,128)S(1)} collective-permute-done((f32[1,72,128]{2,1,0:T(8,128)S(1)}, f32[1,72,128]{2,1,0:T(8,128)S(1)}, u32[]{:S(2)}, u32[]{:S(2)}) %collective-permute-start.10) | collective-permute-done | bytes 36896 | tf_op jit(solution)/shard_map/ppermute | solution.py:677
  64.0 3.1 %collective-permute-done.11 = f32[1,72,128]{2,1,0:T(8,128)S(1)} collective-permute-done((f32[1,72,128]{2,1,0:T(8,128)S(1)}, f32[1,72,128]{2,1,0:T(8,128)S(1)}, u32[]{:S(2)}, u32[]{:S(2)}) %collective-permute-start.11) | collective-permute-done | bytes 36896 | tf_op jit(solution)/shard_map/ppermute | solution.py:677
  67.6 1.8 %collective-permute-start.12 = (f32[4,72,128]{2,1,0:T(8,128)S(1)}, f32[4,72,128]{2,1,0:T(8,128)S(1)}, u32[]{:S(2)}, u32[]{:S(2)}) collective-permute-start(f32[4,72,128]{2,1,0:T(8,128)S(1)} %pad_maximum_fusion.2), channel_id=1, source_target_pairs={{0,2},{1,3},{2,0},{3,1},{4,6},{5,7},{6,4},{7,5},{8,10},{9,11},{10,... | collective-permute-start | bytes 442376 | tf_op jit(solution)/shard_map/ppermute | solution.py:677
  69.5 4.1 %collective-permute-done.12 = f32[4,72,128]{2,1,0:T(8,128)S(1)} collective-permute-done((f32[4,72,128]{2,1,0:T(8,128)S(1)}, f32[4,72,128]{2,1,0:T(8,128)S(1)}, u32[]{:S(2)}, u32[]{:S(2)}) %collective-permute-start.12) | collective-permute-done | bytes 147488 | tf_op jit(solution)/shard_map/ppermute | solution.py:677
  73.7 1.6 %shard_map.69 = (f32[128,1024]{1,0:T(8,128)S(1)}, f32[8,1024]{1,0:T(8,128)S(1)}) custom-call(s32[3]{0:T(128)S(1)} %pad_add_fusion.at, f32[8,152,128]{2,1,0:T(8,128)S(1)} %constant_dynamic-update-slice_fusion.refs_0_, f32[8,152,128]{2,1,0:T(8,128)S(1)} %collective-permute-done.8.refs_1_), custom_call_target="tpu_custom_call" | custom-call | flops 72090080 | bytes 1802252 | tf_op jit(solution)/shard_map/pallas_call | solution.py:172
  75.3 8.0 %shard_map.70 = (f32[2,4,64,128]{3,2,1,0:T(8,128)S(1)}, f32[2,4,64,128]{3,2,1,0:T(8,128)S(1)}, f32[2,4,64,128]{3,2,1,0:T(8,128)S(1)}, f32[16,8,128]{2,1,0:T(8,128)S(1)}, f32[8,128]{1,0:T(8,128)S(1)}) custom-call(s32[3]{0:T(128)S(1)} %pad_add_fusion.at, f32[3,4,64,128]{3,2,1,0:T(8,128)S(1)} %pad_maximum_fusion.own, ...), custom_call_target="tpu_custom_call" | custom-call | flops 266240480 | bytes 6656012 | tf_op jit(solution)/shard_map/pallas_call | solution.py:172
  83.3 10.7 %all_to_all.5.got = f32[16,8,128]{2,1,0:T(8,128)S(1)} all-to-all(f32[16,8,128]{2,1,0:T(8,128)S(1)} %get-tuple-element.34), channel_id=1, replica_groups=mesh['clip'=2,'gz'=16] {'gz'}, dimensions={0} | all-to-all | bytes 131072 | tf_op jit(solution)/shard_map/all_to_all | solution.py:803
  94.0 1.5 %shard_map.71 = (f32[2,4,64,128]{3,2,1,0:T(8,128)}, f32[2,4,64,128]{3,2,1,0:T(8,128)}, f32[2,64]{1,0:T(2,128)}) custom-call(s32[3]{0:T(128)S(1)} %pad_add_fusion.at, f32[2,4,64,128]{3,2,1,0:T(8,128)S(1)} %get-tuple-element.19.direction, f32[2,4,64,128]{3,2,1,0:T(8,128)S(1)} %get-tuple-element.30.corrected, ...), custom_call_target="tpu_custom_call" | custom-call | flops 65720800 | bytes 1643020 | tf_op jit(solution)/shard_map/pallas_call | solution.py:172
  (33 shorter events, 1.6 us)
Async XLA Ops:
  0.6 1.0 %copy-start.1 = (f32[2,4,64,128]{3,2,1,0:T(8,128)S(1)}, f32[2,4,64,128]{3,2,1,0:T(8,128)}, u32[]{:S(2)}) copy-start(f32[2,4,64,128]{3,2,1,0:T(8,128)} %param.4) | copy-start | bytes 786436
  1.7 5.9 %collective-permute-start.1 = (f32[3,4,64,128]{3,2,1,0:T(8,128)S(1)}, f32[3,4,64,128]{3,2,1,0:T(8,128)S(1)}, u32[]{:S(2)}, u32[]{:S(2)}) collective-permute-start(f32[3,4,64,128]{3,2,1,0:T(8,128)S(1)} %pad_maximum_fusion.own), channel_id=1, source_target_pairs={{1,2},{2,1},{3,4},{4,3},{5,6},{6,5},{7,8},{8,7},{9,10},{10,9},{11,... | collective-permute-start | bytes 1179656 | tf_op jit(solution)/shard_map/ppermute | solution.py:684
  2.4 5.7 %collective-permute-start = (f32[3,4,64,128]{3,2,1,0:T(8,128)S(1)}, f32[3,4,64,128]{3,2,1,0:T(8,128)S(1)}, u32[]{:S(2)}, u32[]{:S(2)}) collective-permute-start(f32[3,4,64,128]{3,2,1,0:T(8,128)S(1)} %pad_maximum_fusion.own), channel_id=1, source_target_pairs={{0,1},{1,0},{2,3},{3,2},{4,5},{5,4},{6,7},{7,6},{8,9},{9,8},{10,11... | collective-permute-start | bytes 1179656 | tf_op jit(solution)/shard_map/ppermute | solution.py:677
  6.8 0.7 copy-start.2
  9.9 9.4 %collective-permute-start.4 = (f32[1,152,128]{2,1,0:T(8,128)S(1)}, f32[1,152,128]{2,1,0:T(8,128)S(1)}, u32[]{:S(2)}, u32[]{:S(2)}) collective-permute-start(f32[1,152,128]{2,1,0:T(8,128)S(1)} %bitcast.8), channel_id=1, source_target_pairs={{0,4},{1,5},{2,6},{3,7},{4,0},{5,1},{6,2},{7,3},{8,12},{9,13},{10,... | collective-permute-start | bytes 233480 | tf_op jit(solution)/shard_map/ppermute | solution.py:677
  16.7 6.1 %collective-permute-start.5 = (f32[1,152,128]{2,1,0:T(8,128)S(1)}, f32[1,152,128]{2,1,0:T(8,128)S(1)}, u32[]{:S(2)}, u32[]{:S(2)}) collective-permute-start(f32[1,152,128]{2,1,0:T(8,128)S(1)} %bitcast.9), channel_id=1, source_target_pairs={{0,8},{1,9},{2,10},{3,11},{4,12},{5,13},{6,14},{7,15},{8,0},{9,1},... | collective-permute-start | bytes 233480 | tf_op jit(solution)/shard_map/ppermute | solution.py:677
  19.3 6.2 %collective-permute-start.6 = (f32[1,152,128]{2,1,0:T(8,128)S(1)}, f32[1,152,128]{2,1,0:T(8,128)S(1)}, u32[]{:S(2)}, u32[]{:S(2)}) collective-permute-start(f32[1,152,128]{2,1,0:T(8,128)S(1)} %bitcast.10), channel_id=1, source_target_pairs={{0,12},{1,13},{2,14},{3,15},{4,8},{5,9},{6,10},{7,11},{8,4},{9,5},... | collective-permute-start | bytes 233480 | tf_op jit(solution)/shard_map/ppermute | solution.py:677
  25.5 10.8 %collective-permute-start.7 = (f32[4,152,128]{2,1,0:T(8,128)S(1)}, f32[4,152,128]{2,1,0:T(8,128)S(1)}, u32[]{:S(2)}, u32[]{:S(2)}) collective-permute-start(f32[4,152,128]{2,1,0:T(8,128)S(1)} %pad_maximum_fusion.1), channel_id=1, source_target_pairs={{0,2},{1,3},{2,0},{3,1},{4,6},{5,7},{6,4},{7,5},{8,10},{9,11},{10,... | collective-permute-start | bytes 933896 | tf_op jit(solution)/shard_map/ppermute | solution.py:677
  36.4 11.8 %collective-permute-start.8 = (f32[8,152,128]{2,1,0:T(8,128)S(1)}, f32[8,152,128]{2,1,0:T(8,128)S(1)}, u32[]{:S(2)}, u32[]{:S(2)}) collective-permute-start(f32[8,152,128]{2,1,0:T(8,128)S(1)} %constant_dynamic-update-slice_fusion.refs_0_), channel_id=1, source_target_pairs={{0,1},{1,0},{2,3},{3,2},{4,5},{5,4},{6,7},{7,6},{8,9},{9,8},{10,11... | collective-permute-start | bytes 1867784 | tf_op jit(solution)/shard_map/ppermute | solution.py:677
  36.5 11.7 %collective-permute-start.2 = (f32[3,4,64,128]{3,2,1,0:T(8,128)S(1)}, f32[3,4,64,128]{3,2,1,0:T(8,128)S(1)}, u32[]{:S(2)}, u32[]{:S(2)}) collective-permute-start(f32[3,4,64,128]{3,2,1,0:T(8,128)S(1)} %pad_maximum_fusion.own), channel_id=1, source_target_pairs={{0,2},{2,4},{3,1},{4,6},{5,3},{6,8},{7,5},{8,10},{9,7},{10,12},{11... | collective-permute-start | bytes 1179656 | tf_op jit(solution)/shard_map/ppermute | solution.py:693
  38.7 9.5 %collective-permute-start.3 = (f32[3,4,64,128]{3,2,1,0:T(8,128)S(1)}, f32[3,4,64,128]{3,2,1,0:T(8,128)S(1)}, u32[]{:S(2)}, u32[]{:S(2)}) collective-permute-start(f32[3,4,64,128]{3,2,1,0:T(8,128)S(1)} %collective-permute-done.1.swap), channel_id=1, source_target_pairs={{0,1},{1,0},{2,3},{3,2},{4,5},{5,4},{6,7},{7,6},{8,9},{9,8},{10,11... | collective-permute-start | bytes 1179656 | tf_op jit(solution)/shard_map/ppermute | solution.py:677
  58.8 5.2 %collective-permute-start.10 = (f32[1,72,128]{2,1,0:T(8,128)S(1)}, f32[1,72,128]{2,1,0:T(8,128)S(1)}, u32[]{:S(2)}, u32[]{:S(2)}) collective-permute-start(f32[1,72,128]{2,1,0:T(8,128)S(1)} %bitcast.12), channel_id=1, source_target_pairs={{0,8},{1,9},{2,10},{3,11},{4,12},{5,13},{6,14},{7,15},{8,0},{9,1},... | collective-permute-start | bytes 110600 | tf_op jit(solution)/shard_map/ppermute | solution.py:677
  61.1 6.0 %collective-permute-start.11 = (f32[1,72,128]{2,1,0:T(8,128)S(1)}, f32[1,72,128]{2,1,0:T(8,128)S(1)}, u32[]{:S(2)}, u32[]{:S(2)}) collective-permute-start(f32[1,72,128]{2,1,0:T(8,128)S(1)} %bitcast.13), channel_id=1, source_target_pairs={{0,12},{1,13},{2,14},{3,15},{4,8},{5,9},{6,10},{7,11},{8,4},{9,5},... | collective-permute-start | bytes 110600 | tf_op jit(solution)/shard_map/ppermute | solution.py:677
  62.5 5.1 %collective-permute-start.9 = (f32[1,72,128]{2,1,0:T(8,128)S(1)}, f32[1,72,128]{2,1,0:T(8,128)S(1)}, u32[]{:S(2)}, u32[]{:S(2)}) collective-permute-start(f32[1,72,128]{2,1,0:T(8,128)S(1)} %bitcast.14), channel_id=1, source_target_pairs={{0,4},{1,5},{2,6},{3,7},{4,0},{5,1},{6,2},{7,3},{8,12},{9,13},{10,... | collective-permute-start | bytes 110600 | tf_op jit(solution)/shard_map/ppermute | solution.py:677
  67.6 5.9 %collective-permute-start.12 = (f32[4,72,128]{2,1,0:T(8,128)S(1)}, f32[4,72,128]{2,1,0:T(8,128)S(1)}, u32[]{:S(2)}, u32[]{:S(2)}) collective-permute-start(f32[4,72,128]{2,1,0:T(8,128)S(1)} %pad_maximum_fusion.2), channel_id=1, source_target_pairs={{0,2},{1,3},{2,0},{3,1},{4,6},{5,7},{6,4},{7,5},{8,10},{9,11},{10,... | collective-permute-start | bytes 442376 | tf_op jit(solution)/shard_map/ppermute | solution.py:677
  73.6 1.7 %copy-start = (f32[128,128]{1,0:T(8,128)S(1)}, f32[128,128]{1,0:T(8,128)}, u32[]{:S(2)}) copy-start(f32[128,128]{1,0:T(8,128)} %constant.22.clone.ytable) | copy-start | bytes 196612
  73.6 1.7 %collective-permute-start.13 = (f32[8,72,128]{2,1,0:T(8,128)S(1)}, f32[8,72,128]{2,1,0:T(8,128)S(1)}, u32[]{:S(2)}, u32[]{:S(2)}) collective-permute-start(f32[8,72,128]{2,1,0:T(8,128)S(1)} %constant_dynamic-update-slice_fusion.5.refs_0_), channel_id=1, source_target_pairs={{0,1},{1,0},{2,3},{3,2},{4,5},{5,4},{6,7},{7,6},{8,9},{9,8},{10,11... | collective-permute-start | bytes 884744 | tf_op jit(solution)/shard_map/ppermute | solution.py:677

commit v2 on v1

--- a/solution.py
+++ b/solution.py
@@ -16,8 +16,9 @@
 RELAX = 0.8
 KEEP = 1.0 - RELAX
 PLANES = 4
-OWN = 2 * PLANES
-WINDOW = 5 * PLANES
+OUTER = 2
+OWN = PLANES + OUTER
+WINDOW = PLANES + 2 * OWN
 PAD1 = 8
 PAD2 = 4
 H1 = 0.25
@@ -180,9 +181,28 @@
     )(*inputs)
 
 
-def first_kernel(at, own, near, swap, orders, out, u, e1, u2, tmp, tmp1):
+def pack_kernel(at, source, material, own, inner, outer):
+    odd = at[1]
+    nx = source.shape[2]
+
+    def join(p, r0, rows):
+        for c in range(2):
+            own[c, p, rows] = source[c, p, rows]
+        own[2, p, rows] = (material[p, rows] + 1).astype(F32)
+
+    planes_of(0, PLANES, nx, join)
+
+    def halves(p, r0, rows):
+        for c in range(3):
+            inner[c, p, rows] = own[c, p + OUTER * odd, rows]
+            outer[c, p, rows] = own[c, p + OUTER * (1 - odd), rows]
+
+    planes_of(0, OUTER, nx, halves)
+
+
+def first_kernel(at, own, near, swap, static, out, u, e1, u2, tmp):
     odd, zero = at[1], at[2]
-    nx, ny = own.shape[2:]
+    nx, _ = own.shape[2:]
 
     def fill(block, lower, upper, first):
         def body(p, r0, rows):
@@ -197,7 +217,7 @@
 
     @pl.when(odd == 0)
     def _():
-        fill(swap, 2, 4, -2)
+        fill(swap, 0, 2, 0)
         fill(near, 0, 2, 6)
 
     @pl.when(odd == 1)
@@ -227,7 +247,7 @@
 
     @pl.when(odd == 0)
     def _():
-        outer(swap, PLANES - 1, 1)
+        outer(swap, OUTER - 1, 1)
         outer(near, 0, 6)
 
     @pl.when(odd == 1)
@@ -235,29 +255,39 @@
         outer(near, PLANES - 1, 1)
         outer(swap, 0, 6)
 
+    half = nx // 2
+    for q in range(PLANES // 2):
+        for r0 in range(0, nx, CHUNK):
+            rows = pl.ds(r0, CHUNK)
+            total = [0.0, 0.0]
+            for p in (2 * q, 2 * q + 1):
+                s = around(u2, 2 + p, r0, zero)
+                for c in range(2):
+                    total[c] = total[c] + KEEP * e1[c, p, rows] + s[c]
+            for c in range(2):
+                tmp[q, c, rows] = total[c]
+        out[pl.ds(half * q, half), :] = restrict_fine(tmp.at[q])
+    out[pl.ds(2 * half, static.shape[0]), :] = static[...]
+
+
+def static_kernel(at, own, orders, out, tmp, tmp1):
+    nx, ny = own.shape[2:]
     half = nx // 2
     planes = []
     for q in range(PLANES // 2):
         for r0 in range(0, nx, CHUNK):
             rows = pl.ds(r0, CHUNK)
-            total = [0.0, 0.0, 0.0, 0.0]
-            for p in (2 * q, 2 * q + 1):
-                s = around(u2, 2 + p, r0, zero)
-                shift = shift_of(own[2, p, rows])
-                for c in range(2):
-                    total[c] = total[c] + KEEP * e1[c, p, rows] + s[c]
-                    total[2 + c] = total[2 + c] + shift[c]
-            for k in range(4):
-                tmp[q, k // 2, k % 2, rows] = total[k]
-        out[pl.ds(half * q, half), :] = restrict_fine(tmp.at[q, 0])
-        shift = restrict_fine(tmp.at[q, 1])
-        out[pl.ds(half * (2 + q), half), :] = weights_packed(shift, ny // 2, H1)
+            below, above = shift_of(own[2, 2 * q, rows]), shift_of(own[2, 2 * q + 1, rows])
+            for c in range(2):
+                tmp[q, c, rows] = below[c] + above[c]
+        shift = restrict_fine(tmp.at[q])
+        out[pl.ds(half * q, half), :] = weights_packed(shift, ny // 2, H1)
         planes.append(shift)
     tmp1[...] = planes[0] + planes[1]
     pooled = tmp1[pl.ds(0, half // 2, stride=2), :] + tmp1[pl.ds(1, half // 2, stride=2), :]
     shift2 = dot(pooled, pool_level1(ny))
-    out[pl.ds(4 * half, half // 2), :] = weights_packed(shift2, ny // 4, H2)
-    out[pl.ds(4 * half + half // 2, 8), :] = jnp.broadcast_to(orders[...], (8, ny))
+    out[pl.ds(2 * half, half // 2), :] = weights_packed(shift2, ny // 4, H2)
+    out[pl.ds(2 * half + half // 2, 8), :] = jnp.broadcast_to(orders[...], (8, ny))
 
 
 def coarse_shapes(group, nx, ny):
@@ -354,7 +384,7 @@
             put_packed(dst, p, n, v)
 
         chunked(PAD2, group, 16, sweep)
-    reach2 = (reach + 2) // 2
+    reach2 = (reach + 3) // 2
     count = 2 * reach2 + 1
     flat = mid_packed(vb, PAD2 + me - reach2, count).reshape(count * quarter, ny)
     r, c = iota2(ny, ny)
@@ -384,7 +414,7 @@
     chunked(start - reach, 2 * reach + 2, 5, fourth)
 
 
-def add_correction(ec, v, tmp, planes, nx):
+def add_correction(ec, before, v, tmp, planes, nx):
     half, ny = ec.shape[1:]
     r, c = iota2(ny, 2 * ny)
     spread = jnp.where(c // 2 == r, 1.0, 0.0).astype(F32)
@@ -402,21 +432,15 @@
                 for r0 in range(0, nx, CHUNK):
                     add = tmp[j, c, pl.ds(r0, CHUNK)]
                     for p in (2 * (k + j), 2 * (k + j) + 1):
-                        put(v, c, p, r0, mid(v, c, p, r0) + add, nx)
+                        put(v, c, p, r0, mid(before, c, p, r0) + add, nx)
         return carry
 
     lax.fori_loop(0, planes // 2, body, 0)
 
 
-def second_kernel(masks, layout, at, own, near, swap, skip, far, *refs):
-    n = max(i for i, _ in layout) + 1
-    gathered, refs = refs[:n], refs[n:]
-    (direction, image, smooth2, weight8, pay, w1r, w1i, w2r, w2i), refs = refs[:9], refs[9:]
-    f, weight, u, u2, v, code, tmp, ec, e1 = refs[:9]
-    coarse = refs[9:]
-    me, odd, zero = at[0], at[1], at[2]
-    nx, ny = own.shape[2:]
-    pieces = [(gathered[i], j) for i, j in layout]
+def ahead_kernel(at, own, near, swap, swap_outer, skip, far, f, weight, v, code, u):
+    odd, zero = at[1], at[2]
+    nx = own.shape[2]
 
     def fill(block, first):
         def body(q, r0, rows):
@@ -431,13 +455,15 @@
             put(u, 1, p, r0, ui, nx)
             code[p, rows] = c
 
-        planes_of(0, PLANES, nx, body)
-
+        planes_of(0, block.shape[1], nx, body)
+
+    top = OWN + PLANES
     fill(own, OWN)
-    fill(near, OWN + PLANES - 2 * PLANES * odd)
-    fill(swap, OWN - PLANES + 2 * PLANES * odd)
-    fill(skip, 4 * PLANES * odd)
-    fill(far, 4 * PLANES - 4 * PLANES * odd)
+    fill(near, top - 2 * PLANES * odd)
+    fill(swap, PLANES + 3 * OUTER * odd)
+    fill(swap_outer, OUTER + 5 * OUTER * odd)
+    fill(skip, (WINDOW - OUTER) * odd)
+    fill(far, (WINDOW - OUTER) * (1 - odd))
 
     def pre(p, r0, rows):
         sr, si = around(u, p, r0, zero)
@@ -447,10 +473,21 @@
         put(v, 0, p, r0, mid(u, 0, p, r0) + vr, nx)
         put(v, 1, p, r0, mid(u, 1, p, r0) + vi, nx)
 
-    planes_of(1, WINDOW - 1, nx, pre, 6)
+    planes_of(1, WINDOW - 1, nx, pre, 7)
+
+
+def second_kernel(masks, layout, at, f, weight, before, code, *refs):
+    n = max(i for i, _ in layout) + 1
+    gathered, refs = refs[:n], refs[n:]
+    (direction, image, to_near, to_swap, pay, w1r, w1i, w2r, w2i), refs = refs[:9], refs[9:]
+    u, u2, v, tmp, ec, e1 = refs[:6]
+    coarse = refs[6:]
+    me, odd, zero = at[0], at[1], at[2]
+    nx, ny = f.shape[2:]
+    pieces = [(gathered[i], j) for i, j in layout]
     coarse_weights(me, masks, pieces, w1r, w1i, w2r, w2i)
-    coarse_solve(me, zero, masks, pieces, 4, w1r, w1i, w2r, w2i, *coarse, ec)
-    add_correction(ec, v, tmp, WINDOW // 2, nx)
+    coarse_solve(me, zero, masks, pieces, OWN // 2, w1r, w1i, w2r, w2i, *coarse, ec)
+    add_correction(ec, before, v, tmp, WINDOW // 2, nx)
 
     def sweep(src, dst, p, r0, rows):
         sr, si = around(src, p, r0, zero)
@@ -459,7 +496,7 @@
         put(dst, 1, p, r0, KEEP * mid(src, 1, p, r0) + vi, nx)
 
     planes_of(2, WINDOW - 2, nx, lambda *a: sweep(v, u, *a))
-    planes_of(3, WINDOW - 3, nx, lambda *a: sweep(u, v, *a), 7)
+    planes_of(3, WINDOW - 3, nx, lambda *a: sweep(u, v, *a), 5)
 
     def apply(p, r0, rows):
         sr, si = around(v, p, r0, zero)
@@ -480,7 +517,7 @@
     for q in range(PLANES):
         for r0 in range(0, nx, CHUNK):
             rows = pl.ds(r0, CHUNK)
-            fr, fi = own[0, q, rows], own[1, q, rows]
+            fr, fi = f[0, OWN + q, rows], f[1, OWN + q, rows]
             ir, ii = image[0, OWN - 4 + q, rows], image[1, OWN - 4 + q, rows]
             rho = rho + fr * fr + fi * fi
             cross_r = cross_r + fr * ir + fi * ii
@@ -493,6 +530,13 @@
     tail = jnp.where(row == 0, sums[0], jnp.where(row == 1, sums[1], jnp.where(row == 2, sums[2], 0.0)))
     pay[pl.ds(2 * half, 8), :] = tail
 
+    def edges(q, r0, rows):
+        for c in range(2):
+            to_near[c, q, rows] = image[c, OWN - 4 + q + 2 * odd, rows]
+            to_swap[c, q, rows] = image[c, OWN - 2 + q - 2 * odd, rows]
+
+    planes_of(0, 2, nx, edges)
+
     def pre2(p, r0, rows):
         sr, si = around(u, p, r0, zero)
         er = KEEP * image[0, p - 4, rows] + sr
@@ -501,10 +545,8 @@
         e1[0, p, rows], e1[1, p, rows] = er, ei
         put(u2, 0, p, r0, vr, nx)
         put(u2, 1, p, r0, vi, nx)
-        smooth2[0, p - 5, rows] = mid(u, 0, p, r0) + vr
-        smooth2[1, p - 5, rows] = mid(u, 1, p, r0) + vi
-
-    planes_of(5, WINDOW - 5, nx, pre2, 5)
+
+    planes_of(OWN - 1, OWN + PLANES + 1, nx, pre2, 6)
     for q in range(PLANES // 2):
         for r0 in range(0, nx, CHUNK):
             rows = pl.ds(r0, CHUNK)
@@ -518,11 +560,35 @@
                 tmp[q, c, rows] = total[c]
         pay[pl.ds(half * q, half), :] = restrict_fine(tmp.at[q])
 
-    def copy(p, r0, rows):
-        for c in range(2):
-            weight8[c, p, rows] = weight[c, p + OWN - 2, rows]
-
-    planes_of(0, PLANES + 4, nx, copy)
+
+def widen_kernel(at, image, near, swap, weight, wide, smooth, u):
+    odd, zero = at[1], at[2]
+    nx = image.shape[2]
+
+    def fill(block, first):
+        def body(q, r0, rows):
+            p = first + q
+            fr, fi = block[0, q, rows], block[1, q, rows]
+            ur, ui = cmul(weight[0, p + OUTER, rows], weight[1, p + OUTER, rows], fr, fi)
+            wide[0, p, rows], wide[1, p, rows] = fr, fi
+            put(u, 0, p, r0, ur, nx)
+            put(u, 1, p, r0, ui, nx)
+
+        planes_of(0, block.shape[1], nx, body)
+
+    fill(image, 2)
+    fill(near, 10 - 10 * odd)
+    fill(swap, 10 * odd)
+
+    def pre(p, r0, rows):
+        sr, si = around(u, p, r0, zero)
+        er = KEEP * wide[0, p, rows] + sr
+        ei = KEEP * wide[1, p, rows] + si
+        vr, vi = cmul(weight[0, p + OUTER, rows], weight[1, p + OUTER, rows], er, ei)
+        put(smooth, 0, p, r0, mid(u, 0, p, r0) + vr, nx)
+        put(smooth, 1, p, r0, mid(u, 1, p, r0) + vi, nx)
+
+    planes_of(1, 11, nx, pre, 5)
 
 
 def phase_kernel(masks, layout, row, at, *refs):
@@ -549,7 +615,7 @@
 
 
 def third_kernel(
-    masks, layout, at, own, direction, image, smooth2, weight8, w1r, w1i, w2r, w2i, ytable, xtable, qrow, *refs
+    masks, layout, at, own, direction, image, smooth2, weight, w1r, w1i, w2r, w2i, ytable, xtable, qrow, *refs
 ):
     n = max(i for i, _ in layout) + 1
     gathered, refs = refs[:n], refs[n:]
@@ -561,17 +627,11 @@
     nx, ny = own.shape[2:]
     half = nx // 2
     coarse_solve(me, zero, masks, pieces, 2, w1r, w1i, w2r, w2i, *coarse, ec)
-
-    def take(p, r0, rows):
-        for c in range(2):
-            put(v, c, p, r0, smooth2[c, p - 1, rows], nx)
-
-    planes_of(1, 11, nx, take)
-    add_correction(ec, v, tmp, 6, nx)
+    add_correction(ec, smooth2, v, tmp, 6, nx)
 
     def sweep(src, dst, p, r0, rows):
         sr, si = around(src, p, r0, zero)
-        wr, wi = weight8[0, p - 2, rows], weight8[1, p - 2, rows]
+        wr, wi = weight[0, p + OUTER, rows], weight[1, p + OUTER, rows]
         vr, vi = cmul(wr, wi, image[0, p, rows] + sr, image[1, p, rows] + si)
         put(dst, 0, p, r0, KEEP * mid(src, 0, p, r0) + vr, nx)
         put(dst, 1, p, r0, KEEP * mid(src, 1, p, r0) + vi, nx)
@@ -735,42 +795,54 @@
     at = jnp.stack([me, me % 2, me * 0]).astype(jnp.int32)
     half = nx // 2
 
-    own = jnp.concatenate([source_term, (material + 1).astype(F32)[None]], axis=0)
+    fine = (2, PLANES, nx, ny)
+    half_block = (3, OUTER, nx, ny)
+    own, inner, outer = call(
+        pack_kernel, [(3, PLANES, nx, ny), half_block, half_block], [at, source_term, material], []
+    )
+    swap = swap_across(inner, group)
     near = exchange(own, 1, group)
-    swap = swap_across(own, group)
+    swap_outer = swap_across(outer, group)
+    skip = skip_across(outer, group)
+    far = exchange(swap, 1, group)
     order_row = orders.astype(F32).reshape(1, ny)
-    fine = (2, PLANES, nx, ny)
     tall = nx + 2 * HALO
+    (pay0,) = call(static_kernel, [(2 * half + half // 2 + 8, ny)], [at, own, order_row], [(2, 2, nx, ny), (half, ny)])
     (pay1,) = call(
         first_kernel,
         [(4 * half + half // 2 + 8, ny)],
-        [at, own, near, swap, order_row],
-        [(2, 8, tall, ny), fine, (2, 8, tall, ny), (2, 2, 2, nx, ny), (half, ny)],
+        [at, own, near, swap, pay0],
+        [(2, 8, tall, ny), fine, (2, 8, tall, ny), (2, 2, nx, ny)],
     )
     gathered1, masks, layout = gather(pay1, group)
-    skip = skip_across(own, group)
-    far = exchange(swap, 1, group)
-
     window = (2, WINDOW, nx, ny)
     haloed = (2, WINDOW, tall, ny)
     shapes1 = (2 * group + 2 * PAD1, half, ny)
     shapes2 = (group + 2 * PAD2, half // 2, ny)
-    direction, image, smooth2, weight8, pay2, w1r, w1i, w2r, w2i = call(
+    f, weight, before, code = call(
+        ahead_kernel, [window, window, haloed, (WINDOW, nx, ny)], [at, own, near, swap, swap_outer, skip, far], [haloed]
+    )
+    edge = (2, 2, nx, ny)
+    direction, image, to_near, to_swap, pay2, w1r, w1i, w2r, w2i = call(
         functools.partial(second_kernel, masks, layout),
         [
             fine,
-            (2, 12, nx, ny),
-            (2, 10, nx, ny),
-            (2, PLANES + 4, nx, ny),
+            (2, WINDOW - 8, nx, ny),
+            edge,
+            edge,
             (2 * half + 8, ny),
             shapes1,
             shapes1,
             shapes2,
             shapes2,
         ],
-        [at, own, near, swap, skip, far, *gathered1],
-        [window, window, haloed, haloed, haloed, (WINDOW, nx, ny), (2, 2, nx, ny), (10, half, ny), window]
-        + coarse_shapes(group, nx, ny),
+        [at, f, weight, before, code, *gathered1],
+        [haloed, haloed, haloed, (2, 2, nx, ny), (WINDOW // 2, half, ny), window] + coarse_shapes(group, nx, ny),
+    )
+    near2 = exchange(to_near, 1, group)
+    swap2 = swap_across(to_swap, group)
+    wide, smooth2 = call(
+        widen_kernel, [(2, 12, nx, ny), (2, 12, tall, ny)], [at, image, near2, swap2, weight], [(2, 12, tall, ny)]
     )
     xtable, qrow = call(
         functools.partial(phase_kernel, masks, layout, 4 * half + half // 2),
@@ -786,9 +858,9 @@
             at,
             own,
             direction,
-            image,
+            wide,
             smooth2,
-            weight8,
+            weight,
             w1r,
             w1i,
             w2r,

time: 95.7 us -> 101 us (1.055)
  blocking collectives: 10.7 us -> 14.6 us
  waiting for transfers between devices: 32.7 us -> 30 us
  Pallas kernels: 23.5 us -> 25.2 us
  local copies, waits for them, and re-layouts: 0.89 us -> 2.02 us
    ppermute x1, waiting for transfers between devices: 9.39 us -> 5.18 us  [skip_across(): return lax.ppermute(x, 'gz', pairs)]
    all_to_all x1, blocking collectives: 10.7 us -> 14.6 us  [on_device(): got = lax.all_to_all(pay3, 'gz', 0, 0)]
    ppermute x12 -> x13, starting transfers between devices: 22.9 us -> 19.2 us  [exchange(): return lax.ppermute(x, 'gz', [(i, i ^ mask) for i in range(group)])]
    ppermute x1, starting transfers between devices: 2.21 us -> 5.27 us  [skip_across(): return lax.ppermute(x, 'gz', pairs)]
    pallas_call x5 -> x9, Pallas kernels: 23.5 us -> 25.2 us  [call(): pl.pallas_call(body, out_shape=[full(o) for o in outs], in_specs=[SM] + [...]
    ppermute x12 -> x13, waiting for transfers between devices: 23.3 us -> 24.9 us  [exchange(): return lax.ppermute(x, 'gz', [(i, i ^ mask) for i in range(group)])]
    ppermute x1 -> x3, starting transfers between devices: 0.69 us -> 2.12 us  [swap_across(): return lax.ppermute(x, 'gz', pairs)]
    unnamed x14, local copies, waits for them, and re-layouts: 0.77 us -> 1.9 us
  transfers between devices with their start and end apart: 14 -> 17, of which waited for: 9 -> 7; matrix products, arithmetic and copies ran while one was open for 0% -> 1% of each run, Pallas kernels for 2% -> 5%
where the time goes in v2:
time: 101 us; the launch traced here: 100 us
  waiting for transfers between devices  30 us (30%)
  starting transfers between devices  26.6 us (26%)
  Pallas kernels  25.2 us (25%)
  blocking collectives  14.6 us (14%)
  local copies, waits for them, and re-layouts  2.02 us (2%)
    pallas_call x9, Pallas kernels, call(): pl.pallas_call(body, out_shape=[full(o) for o in outs], in_specs=[SM] + [...  25.2 us
    ppermute x13, waiting for transfers between devices, exchange(): return lax.ppermute(x, 'gz', [(i, i ^ mask) for i in range(group)])  24.9 us
    ppermute x13, starting transfers between devices, exchange(): return lax.ppermute(x, 'gz', [(i, i ^ mask) for i in range(group)])  19.2 us
    all_to_all x1, blocking collectives, on_device(): got = lax.all_to_all(pay3, 'gz', 0, 0)  14.6 us
    ppermute x1, starting transfers between devices, skip_across(): return lax.ppermute(x, 'gz', pairs)  5.27 us
    ppermute x1, waiting for transfers between devices, skip_across(): return lax.ppermute(x, 'gz', pairs)  5.18 us
    ppermute x3, starting transfers between devices, swap_across(): return lax.ppermute(x, 'gz', pairs)  2.12 us
  transfers between devices with their start and end apart: 17, of which 7 were waited for; matrix products, arithmetic and copies ran while one was open for 1% of the time, Pallas kernels for 5%

profile of v2, /device:TPU:0, one launch (start us, length us, event | category | flops | bytes accessed | tf_op | source)
XLA Modules:
  0.0 100.2 jit_solution(10282005859397478383)
XLA Ops:
  0.7 0.9 copy-done
  5.2 1.1 %shard_map.69.static = f32[88,128]{1,0:T(8,128)S(1)} custom-call(s32[3]{0:T(128)S(1)} %pad_add_fusion.at, f32[3,4,64,128]{3,2,1,0:T(8,128)S(1)} %get-tuple-element.28.own, f32[1,128]{1,0:T(1,128)S(1)} %reshape.9.orders), custom_call_target="tpu_custom_call" | custom-call | flops 17551840 | bytes 438796 | tf_op jit(solution)/shard_map/pallas_call | solution.py:173
  6.3 1.4 %shard_map.70 = f32[152,128]{1,0:T(8,128)S(1)} custom-call(s32[3]{0:T(128)S(1)} %pad_add_fusion.at, f32[3,4,64,128]{3,2,1,0:T(8,128)S(1)} %get-tuple-element.28.own, f32[3,4,64,128]{3,2,1,0:T(8,128)S(1)} %collective-permute-done.near, f32[3,2,64,128]{3,2,1,0:T(8,128)S(1)} %collective-permute-done.1.swap, f32[88,128]{1,0:T(8,128)S(1)} %shard_map.69.static), custom_call_target="tpu_custom_call" | custom-call | flops 44237280 | bytes 1105932 | tf_op jit(solution)/shard_map/pallas_call | solution.py:173
  7.7 8.0 %collective-permute-start.5 = (f32[1,152,128]{2,1,0:T(8,128)S(1)}, f32[1,152,128]{2,1,0:T(8,128)S(1)}, u32[]{:S(2)}, u32[]{:S(2)}) collective-permute-start(f32[1,152,128]{2,1,0:T(8,128)S(1)} %bitcast.6), channel_id=1, source_target_pairs={{0,4},{1,5},{2,6},{3,7},{4,0},{5,1},{6,2},{7,3},{8,12},{9,13},{10,... | collective-permute-start | bytes 233480 | tf_op jit(solution)/shard_map/ppermute | solution.py:737
  15.8 2.6 %collective-permute-start.6 = (f32[1,152,128]{2,1,0:T(8,128)S(1)}, f32[1,152,128]{2,1,0:T(8,128)S(1)}, u32[]{:S(2)}, u32[]{:S(2)}) collective-permute-start(f32[1,152,128]{2,1,0:T(8,128)S(1)} %bitcast.7), channel_id=1, source_target_pairs={{0,8},{1,9},{2,10},{3,11},{4,12},{5,13},{6,14},{7,15},{8,0},{9,1},... | collective-permute-start | bytes 233480 | tf_op jit(solution)/shard_map/ppermute | solution.py:737
  18.4 4.8 %collective-permute-done.6 = f32[1,152,128]{2,1,0:T(8,128)S(1)} collective-permute-done((f32[1,152,128]{2,1,0:T(8,128)S(1)}, f32[1,152,128]{2,1,0:T(8,128)S(1)}, u32[]{:S(2)}, u32[]{:S(2)}) %collective-permute-start.6) | collective-permute-done | bytes 77856 | tf_op jit(solution)/shard_map/ppermute | solution.py:737
  23.2 2.2 %collective-permute-done.7 = f32[1,152,128]{2,1,0:T(8,128)S(1)} collective-permute-done((f32[1,152,128]{2,1,0:T(8,128)S(1)}, f32[1,152,128]{2,1,0:T(8,128)S(1)}, u32[]{:S(2)}, u32[]{:S(2)}) %collective-permute-start.7) | collective-permute-done | bytes 77856 | tf_op jit(solution)/shard_map/ppermute | solution.py:737
  25.5 1.5 %collective-permute-start.8 = (f32[4,152,128]{2,1,0:T(8,128)S(1)}, f32[4,152,128]{2,1,0:T(8,128)S(1)}, u32[]{:S(2)}, u32[]{:S(2)}) collective-permute-start(f32[4,152,128]{2,1,0:T(8,128)S(1)} %pad_maximum_fusion), channel_id=1, source_target_pairs={{0,2},{1,3},{2,0},{3,1},{4,6},{5,7},{6,4},{7,5},{8,10},{9,11},{10,... | collective-permute-start | bytes 933896 | tf_op jit(solution)/shard_map/ppermute | solution.py:737
  27.0 7.9 %collective-permute-done.8 = f32[4,152,128]{2,1,0:T(8,128)S(1)} collective-permute-done((f32[4,152,128]{2,1,0:T(8,128)S(1)}, f32[4,152,128]{2,1,0:T(8,128)S(1)}, u32[]{:S(2)}, u32[]{:S(2)}) %collective-permute-start.8) | collective-permute-done | bytes 311328 | tf_op jit(solution)/shard_map/ppermute | solution.py:737
  35.6 5.3 %collective-permute-start.3 = (f32[3,2,64,128]{3,2,1,0:T(8,128)S(1)}, f32[3,2,64,128]{3,2,1,0:T(8,128)S(1)}, u32[]{:S(2)}, u32[]{:S(2)}) collective-permute-start(f32[3,2,64,128]{3,2,1,0:T(8,128)S(1)} %get-tuple-element.30), channel_id=1, source_target_pairs={{0,2},{2,4},{3,1},{4,6},{5,3},{6,8},{7,5},{8,10},{9,7},{10,12},{11... | collective-permute-start | bytes 589832 | tf_op jit(solution)/shard_map/ppermute | solution.py:753
  41.0 5.2 %collective-permute-done.3.skip = f32[3,2,64,128]{3,2,1,0:T(8,128)S(1)} collective-permute-done((f32[3,2,64,128]{3,2,1,0:T(8,128)S(1)}, f32[3,2,64,128]{3,2,1,0:T(8,128)S(1)}, u32[]{:S(2)}, u32[]{:S(2)}) %collective-permute-start.3) | collective-permute-done | bytes 196640 | tf_op jit(solution)/shard_map/ppermute | solution.py:753
  46.2 1.6 %shard_map.68 = (f32[2,16,64,128]{3,2,1,0:T(8,128)S(1)}, f32[2,16,64,128]{3,2,1,0:T(8,128)S(1)}, f32[2,16,80,128]{3,2,1,0:T(8,128)S(1)}, f32[16,64,128]{2,1,0:T(8,128)S(1)}) custom-call(s32[3]{0:T(128)S(1)} %pad_add_fusion.at, f32[3,4,64,128]{3,2,1,0:T(8,128)S(1)} %get-tuple-element.28.own, f32[3,4,64,128]{3,2,1,0:T(8,128)S(1)} %collective-permute-done.near, ...), custom_call_target="tpu_custom_call" | custom-call | flops 220201440 | bytes 5505036 | tf_op jit(solution)/shard_map/pallas_call | solution.py:173
  47.8 8.3 %shard_map.71 = (f32[2,4,64,128]{3,2,1,0:T(8,128)S(1)}, f32[2,8,64,128]{3,2,1,0:T(8,128)S(1)}, f32[2,2,64,128]{3,2,1,0:T(8,128)S(1)}, f32[2,2,64,128]{3,2,1,0:T(...) custom-call(s32[3]{0:T(128)S(1)} %pad_add_fusion.at, ...), custom_call_target="tpu_custom_call" | custom-call | flops 329155040 | bytes 8228876 | tf_op jit(solution)/shard_map/pallas_call | solution.py:173
  56.1 1.9 %collective-permute-start.12 = (f32[1,72,128]{2,1,0:T(8,128)S(1)}, f32[1,72,128]{2,1,0:T(8,128)S(1)}, u32[]{:S(2)}, u32[]{:S(2)}) collective-permute-start(f32[1,72,128]{2,1,0:T(8,128)S(1)} %bitcast.10), channel_id=1, source_target_pairs={{0,4},{1,5},{2,6},{3,7},{4,0},{5,1},{6,2},{7,3},{8,12},{9,13},{10,... | collective-permute-start | bytes 110600 | tf_op jit(solution)/shard_map/ppermute | solution.py:737
  58.0 2.1 %collective-permute-start.13 = (f32[1,72,128]{2,1,0:T(8,128)S(1)}, f32[1,72,128]{2,1,0:T(8,128)S(1)}, u32[]{:S(2)}, u32[]{:S(2)}) collective-permute-start(f32[1,72,128]{2,1,0:T(8,128)S(1)} %bitcast.11), channel_id=1, source_target_pairs={{0,8},{1,9},{2,10},{3,11},{4,12},{5,13},{6,14},{7,15},{8,0},{9,1},... | collective-permute-start | bytes 110600 | tf_op jit(solution)/shard_map/ppermute | solution.py:737
  60.6 2.6 %collective-permute-done.13 = f32[1,72,128]{2,1,0:T(8,128)S(1)} collective-permute-done((f32[1,72,128]{2,1,0:T(8,128)S(1)}, f32[1,72,128]{2,1,0:T(8,128)S(1)}, u32[]{:S(2)}, u32[]{:S(2)}) %collective-permute-start.13) | collective-permute-done | bytes 36896 | tf_op jit(solution)/shard_map/ppermute | solution.py:737
  63.2 2.8 %collective-permute-done.14 = f32[1,72,128]{2,1,0:T(8,128)S(1)} collective-permute-done((f32[1,72,128]{2,1,0:T(8,128)S(1)}, f32[1,72,128]{2,1,0:T(8,128)S(1)}, u32[]{:S(2)}, u32[]{:S(2)}) %collective-permute-start.14) | collective-permute-done | bytes 36896 | tf_op jit(solution)/shard_map/ppermute | solution.py:737
  66.0 1.4 %collective-permute-start.15 = (f32[4,72,128]{2,1,0:T(8,128)S(1)}, f32[4,72,128]{2,1,0:T(8,128)S(1)}, u32[]{:S(2)}, u32[]{:S(2)}) collective-permute-start(f32[4,72,128]{2,1,0:T(8,128)S(1)} %pad_maximum_fusion.1), channel_id=1, source_target_pairs={{0,2},{1,3},{2,0},{3,1},{4,6},{5,7},{6,4},{7,5},{8,10},{9,11},{10,... | collective-permute-start | bytes 442376 | tf_op jit(solution)/shard_map/ppermute | solution.py:737
  67.4 4.5 %collective-permute-done.15 = f32[4,72,128]{2,1,0:T(8,128)S(1)} collective-permute-done((f32[4,72,128]{2,1,0:T(8,128)S(1)}, f32[4,72,128]{2,1,0:T(8,128)S(1)}, u32[]{:S(2)}, u32[]{:S(2)}) %collective-permute-start.15) | collective-permute-done | bytes 147488 | tf_op jit(solution)/shard_map/ppermute | solution.py:737
  73.3 1.6 %shard_map.73 = (f32[128,1024]{1,0:T(8,128)S(1)}, f32[8,1024]{1,0:T(8,128)S(1)}) custom-call(s32[3]{0:T(128)S(1)} %pad_add_fusion.at, f32[8,152,128]{2,1,0:T(8,128)S(1)} %constant_dynamic-update-slice_fusion.refs_0_, f32[8,152,128]{2,1,0:T(8,128)S(1)} %collective-permute-done.9.refs_1_), custom_call_target="tpu_custom_call" | custom-call | flops 72090080 | bytes 1802252 | tf_op jit(solution)/shard_map/pallas_call | solution.py:173
  75.0 1.2 %shard_map.72 = (f32[2,12,64,128]{3,2,1,0:T(8,128)S(1)}, f32[2,12,80,128]{3,2,1,0:T(8,128)S(1)}) custom-call(s32[3]{0:T(128)S(1)} %pad_add_fusion.at, f32[2,8,64,128]{3,2,1,0:T(8,128)S(1)} %get-tuple-element.36.image, f32[2,2,64,128]{3,2,1,0:T(8,128)S(1)} %collective-permute-done.10.near, f32[2,2,64,128]{3,2,1,0:T(8,128)S(1)} %collective-permute-done.11.swap, ...), custom_call_target="tpu_custom_call" | custom-call | flops 144179680 | bytes 3604492 | tf_op jit(solution)/shard_map/pallas_call | solution.py:173
  76.2 7.9 %shard_map.74 = (f32[2,4,64,128]{3,2,1,0:T(8,128)S(1)}, f32[2,4,64,128]{3,2,1,0:T(8,128)S(1)}, f32[2,4,64,128]{3,2,1,0:T(8,128)S(1)}, f32[16,8,128]{2,1,0:T(8,128)S(1)}, f32[8,128]{1,0:T(8,128)S(1)}) custom-call(s32[3]{0:T(128)S(1)} %pad_add_fusion.at, f32[3,4,64,128]{3,2,1,0:T(8,128)S(1)} %get-tuple-element.28.own, ...), custom_call_target="tpu_custom_call" | custom-call | flops 300319200 | bytes 7507980 | tf_op jit(solution)/shard_map/pallas_call | solution.py:173
  84.1 14.6 %all_to_all.5.got = f32[16,8,128]{2,1,0:T(8,128)S(1)} all-to-all(f32[16,8,128]{2,1,0:T(8,128)S(1)} %get-tuple-element.52), channel_id=1, replica_groups=mesh['clip'=2,'gz'=16] {'gz'}, dimensions={0} | all-to-all | bytes 131072 | tf_op jit(solution)/shard_map/all_to_all | solution.py:875
  98.7 1.5 %shard_map.75 = (f32[2,4,64,128]{3,2,1,0:T(8,128)}, f32[2,4,64,128]{3,2,1,0:T(8,128)}, f32[2,64]{1,0:T(2,128)}) custom-call(s32[3]{0:T(128)S(1)} %pad_add_fusion.at, f32[2,4,64,128]{3,2,1,0:T(8,128)S(1)} %get-tuple-element.35.direction, f32[2,4,64,128]{3,2,1,0:T(8,128)S(1)} %get-tuple-element.48.corrected, ...), custom_call_target="tpu_custom_call" | custom-call | flops 65720800 | bytes 1643020 | tf_op jit(solution)/shard_map/pallas_call | solution.py:173
  (41 shorter events, 6.3 us)
Async XLA Ops:
  0.7 1.0 copy-start
  1.7 0.9 copy-start.1
  3.2 3.1 %collective-permute-start = (f32[3,4,64,128]{3,2,1,0:T(8,128)S(1)}, f32[3,4,64,128]{3,2,1,0:T(8,128)S(1)}, u32[]{:S(2)}, u32[]{:S(2)}) collective-permute-start(f32[3,4,64,128]{3,2,1,0:T(8,128)S(1)} %get-tuple-element.28.own), channel_id=1, source_target_pairs={{0,1},{1,0},{2,3},{3,2},{4,5},{5,4},{6,7},{7,6},{8,9},{9,8},{10,11... | collective-permute-start | bytes 1179656 | tf_op jit(solution)/shard_map/ppermute | solution.py:737
  3.7 2.6 %collective-permute-start.1 = (f32[3,2,64,128]{3,2,1,0:T(8,128)S(1)}, f32[3,2,64,128]{3,2,1,0:T(8,128)S(1)}, u32[]{:S(2)}, u32[]{:S(2)}) collective-permute-start(f32[3,2,64,128]{3,2,1,0:T(8,128)S(1)} %get-tuple-element.29), channel_id=1, source_target_pairs={{1,2},{2,1},{3,4},{4,3},{5,6},{6,5},{7,8},{8,7},{9,10},{10,9},{11,... | collective-permute-start | bytes 589832 | tf_op jit(solution)/shard_map/ppermute | solution.py:744
  7.7 10.6 %collective-permute-start.5 = (f32[1,152,128]{2,1,0:T(8,128)S(1)}, f32[1,152,128]{2,1,0:T(8,128)S(1)}, u32[]{:S(2)}, u32[]{:S(2)}) collective-permute-start(f32[1,152,128]{2,1,0:T(8,128)S(1)} %bitcast.6), channel_id=1, source_target_pairs={{0,4},{1,5},{2,6},{3,7},{4,0},{5,1},{6,2},{7,3},{8,12},{9,13},{10,... | collective-permute-start | bytes 233480 | tf_op jit(solution)/shard_map/ppermute | solution.py:737
  15.8 7.5 %collective-permute-start.6 = (f32[1,152,128]{2,1,0:T(8,128)S(1)}, f32[1,152,128]{2,1,0:T(8,128)S(1)}, u32[]{:S(2)}, u32[]{:S(2)}) collective-permute-start(f32[1,152,128]{2,1,0:T(8,128)S(1)} %bitcast.7), channel_id=1, source_target_pairs={{0,8},{1,9},{2,10},{3,11},{4,12},{5,13},{6,14},{7,15},{8,0},{9,1},... | collective-permute-start | bytes 233480 | tf_op jit(solution)/shard_map/ppermute | solution.py:737
  18.4 7.1 %collective-permute-start.7 = (f32[1,152,128]{2,1,0:T(8,128)S(1)}, f32[1,152,128]{2,1,0:T(8,128)S(1)}, u32[]{:S(2)}, u32[]{:S(2)}) collective-permute-start(f32[1,152,128]{2,1,0:T(8,128)S(1)} %bitcast.8), channel_id=1, source_target_pairs={{0,12},{1,13},{2,14},{3,15},{4,8},{5,9},{6,10},{7,11},{8,4},{9,5},... | collective-permute-start | bytes 233480 | tf_op jit(solution)/shard_map/ppermute | solution.py:737
  25.5 9.4 %collective-permute-start.8 = (f32[4,152,128]{2,1,0:T(8,128)S(1)}, f32[4,152,128]{2,1,0:T(8,128)S(1)}, u32[]{:S(2)}, u32[]{:S(2)}) collective-permute-start(f32[4,152,128]{2,1,0:T(8,128)S(1)} %pad_maximum_fusion), channel_id=1, source_target_pairs={{0,2},{1,3},{2,0},{3,1},{4,6},{5,7},{6,4},{7,5},{8,10},{9,11},{10,... | collective-permute-start | bytes 933896 | tf_op jit(solution)/shard_map/ppermute | solution.py:737
  34.9 12.9 %collective-permute-start.9 = (f32[8,152,128]{2,1,0:T(8,128)S(1)}, f32[8,152,128]{2,1,0:T(8,128)S(1)}, u32[]{:S(2)}, u32[]{:S(2)}) collective-permute-start(f32[8,152,128]{2,1,0:T(8,128)S(1)} %constant_dynamic-update-slice_fusion.refs_0_), channel_id=1, source_target_pairs={{0,1},{1,0},{2,3},{3,2},{4,5},{5,4},{6,7},{7,6},{8,9},{9,8},{10,11... | collective-permute-start | bytes 1867784 | tf_op jit(solution)/shard_map/ppermute | solution.py:737
  35.0 6.0 %collective-permute-start.2 = (f32[3,2,64,128]{3,2,1,0:T(8,128)S(1)}, f32[3,2,64,128]{3,2,1,0:T(8,128)S(1)}, u32[]{:S(2)}, u32[]{:S(2)}) collective-permute-start(f32[3,2,64,128]{3,2,1,0:T(8,128)S(1)} %get-tuple-element.30), channel_id=1, source_target_pairs={{1,2},{2,1},{3,4},{4,3},{5,6},{6,5},{7,8},{8,7},{9,10},{10,9},{11,... | collective-permute-start | bytes 589832 | tf_op jit(solution)/shard_map/ppermute | solution.py:744
  35.6 10.5 %collective-permute-start.3 = (f32[3,2,64,128]{3,2,1,0:T(8,128)S(1)}, f32[3,2,64,128]{3,2,1,0:T(8,128)S(1)}, u32[]{:S(2)}, u32[]{:S(2)}) collective-permute-start(f32[3,2,64,128]{3,2,1,0:T(8,128)S(1)} %get-tuple-element.30), channel_id=1, source_target_pairs={{0,2},{2,4},{3,1},{4,6},{5,3},{6,8},{7,5},{8,10},{9,7},{10,12},{11... | collective-permute-start | bytes 589832 | tf_op jit(solution)/shard_map/ppermute | solution.py:753
  40.9 5.3 %collective-permute-start.4 = (f32[3,2,64,128]{3,2,1,0:T(8,128)S(1)}, f32[3,2,64,128]{3,2,1,0:T(8,128)S(1)}, u32[]{:S(2)}, u32[]{:S(2)}) collective-permute-start(f32[3,2,64,128]{3,2,1,0:T(8,128)S(1)} %collective-permute-done.1.swap), channel_id=1, source_target_pairs={{0,1},{1,0},{2,3},{3,2},{4,5},{5,4},{6,7},{7,6},{8,9},{9,8},{10,11... | collective-permute-start | bytes 589832 | tf_op jit(solution)/shard_map/ppermute | solution.py:737
  56.1 4.5 %collective-permute-start.12 = (f32[1,72,128]{2,1,0:T(8,128)S(1)}, f32[1,72,128]{2,1,0:T(8,128)S(1)}, u32[]{:S(2)}, u32[]{:S(2)}) collective-permute-start(f32[1,72,128]{2,1,0:T(8,128)S(1)} %bitcast.10), channel_id=1, source_target_pairs={{0,4},{1,5},{2,6},{3,7},{4,0},{5,1},{6,2},{7,3},{8,12},{9,13},{10,... | collective-permute-start | bytes 110600 | tf_op jit(solution)/shard_map/ppermute | solution.py:737
  58.0 5.2 %collective-permute-start.13 = (f32[1,72,128]{2,1,0:T(8,128)S(1)}, f32[1,72,128]{2,1,0:T(8,128)S(1)}, u32[]{:S(2)}, u32[]{:S(2)}) collective-permute-start(f32[1,72,128]{2,1,0:T(8,128)S(1)} %bitcast.11), channel_id=1, source_target_pairs={{0,8},{1,9},{2,10},{3,11},{4,12},{5,13},{6,14},{7,15},{8,0},{9,1},... | collective-permute-start | bytes 110600 | tf_op jit(solution)/shard_map/ppermute | solution.py:737
  60.1 5.8 %collective-permute-start.14 = (f32[1,72,128]{2,1,0:T(8,128)S(1)}, f32[1,72,128]{2,1,0:T(8,128)S(1)}, u32[]{:S(2)}, u32[]{:S(2)}) collective-permute-start(f32[1,72,128]{2,1,0:T(8,128)S(1)} %bitcast.12), channel_id=1, source_target_pairs={{0,12},{1,13},{2,14},{3,15},{4,8},{5,9},{6,10},{7,11},{8,4},{9,5},... | collective-permute-start | bytes 110600 | tf_op jit(solution)/shard_map/ppermute | solution.py:737
  66.0 6.0 %collective-permute-start.15 = (f32[4,72,128]{2,1,0:T(8,128)S(1)}, f32[4,72,128]{2,1,0:T(8,128)S(1)}, u32[]{:S(2)}, u32[]{:S(2)}) collective-permute-start(f32[4,72,128]{2,1,0:T(8,128)S(1)} %pad_maximum_fusion.1), channel_id=1, source_target_pairs={{0,2},{1,3},{2,0},{3,1},{4,6},{5,7},{6,4},{7,5},{8,10},{9,11},{10,... | collective-permute-start | bytes 442376 | tf_op jit(solution)/shard_map/ppermute | solution.py:737
  71.9 4.2 %collective-permute-start.16 = (f32[8,72,128]{2,1,0:T(8,128)S(1)}, f32[8,72,128]{2,1,0:T(8,128)S(1)}, u32[]{:S(2)}, u32[]{:S(2)}) collective-permute-start(f32[8,72,128]{2,1,0:T(8,128)S(1)} %constant_dynamic-update-slice_fusion.5.refs_0_), channel_id=1, source_target_pairs={{0,1},{1,0},{2,3},{3,2},{4,5},{5,4},{6,7},{7,6},{8,9},{9,8},{10,11... | collective-permute-start | bytes 884744 | tf_op jit(solution)/shard_map/ppermute | solution.py:737
  72.0 2.9 %collective-permute-start.10 = (f32[2,2,64,128]{3,2,1,0:T(8,128)S(1)}, f32[2,2,64,128]{3,2,1,0:T(8,128)S(1)}, u32[]{:S(2)}, u32[]{:S(2)}) collective-permute-start(f32[2,2,64,128]{3,2,1,0:T(8,128)S(1)} %get-tuple-element.37), channel_id=1, source_target_pairs={{0,1},{1,0},{2,3},{3,2},{4,5},{5,4},{6,7},{7,6},{8,9},{9,8},{10,11... | collective-permute-start | bytes 393224 | tf_op jit(solution)/shard_map/ppermute | solution.py:737
  72.5 3.7 %copy-start.2 = (f32[128,128]{1,0:T(8,128)S(1)}, f32[128,128]{1,0:T(8,128)}, u32[]{:S(2)}) copy-start(f32[128,128]{1,0:T(8,128)} %constant.21.clone.ytable) | copy-start | bytes 196612
  72.5 2.4 %collective-permute-start.11 = (f32[2,2,64,128]{3,2,1,0:T(8,128)S(1)}, f32[2,2,64,128]{3,2,1,0:T(8,128)S(1)}, u32[]{:S(2)}, u32[]{:S(2)}) collective-permute-start(f32[2,2,64,128]{3,2,1,0:T(8,128)S(1)} %get-tuple-element.38), channel_id=1, source_target_pairs={{1,2},{2,1},{3,4},{4,3},{5,6},{6,5},{7,8},{8,7},{9,10},{10,9},{11,... | collective-permute-start | bytes 393224 | tf_op jit(solution)/shard_map/ppermute | solution.py:744

commit v3 on v2

--- a/solution.py
+++ b/solution.py
@@ -135,8 +135,12 @@
     return jnp.where(real_lane, dr, -di) * scale
 
 
-def dot(a, b):
-    return jnp.dot(a, b, precision=lax.Precision.HIGHEST, preferred_element_type=F32)
+def dot_exact(a, b):
+    high = a.astype(jnp.bfloat16)
+    low = (a - high.astype(F32)).astype(jnp.bfloat16)
+    b = b.astype(jnp.bfloat16)
+    both = jnp.concatenate([high, low], axis=1)
+    return jnp.dot(both, jnp.concatenate([b, b], axis=0), preferred_element_type=F32)
 
 
 def iota2(rows, cols):
@@ -152,7 +156,7 @@
     rows = [tmp[c, pl.ds(0, half, stride=2), :] + tmp[c, pl.ds(1, half, stride=2), :] for c in range(2)]
     r, c = iota2(2 * ny, ny)
     pool = jnp.where(r // 2 == c, 0.125, 0.0).astype(F32)
-    return dot(jnp.concatenate(rows, axis=1), pool)
+    return dot_exact(jnp.concatenate(rows, axis=1), pool)
 
 
 def pool_level1(ny):
@@ -285,9 +289,11 @@
         planes.append(shift)
     tmp1[...] = planes[0] + planes[1]
     pooled = tmp1[pl.ds(0, half // 2, stride=2), :] + tmp1[pl.ds(1, half // 2, stride=2), :]
-    shift2 = dot(pooled, pool_level1(ny))
+    shift2 = dot_exact(pooled, pool_level1(ny))
     out[pl.ds(2 * half, half // 2), :] = weights_packed(shift2, ny // 4, H2)
-    out[pl.ds(2 * half + half // 2, 8), :] = jnp.broadcast_to(orders[...], (8, ny))
+    wanted = orders[...].astype(F32)
+    line = jnp.concatenate([wanted[0:1], wanted[1:2]], axis=1)
+    out[pl.ds(2 * half + half // 2, 8), :] = jnp.broadcast_to(line, (8, ny))
 
 
 def coarse_shapes(group, nx, ny):
@@ -372,7 +378,7 @@
     chunked(PAD1, n1, 8, coarser)
     rows = group * quarter
     flat = pool[pl.ds(0, rows, stride=2), :] + pool[pl.ds(1, rows, stride=2), :]
-    r2 = dot(flat, pool_level1(ny)).reshape(group, quarter, ny)
+    r2 = dot_exact(flat, pool_level1(ny)).reshape(group, quarter, ny)
     inside = pl.ds(PAD2, group)
     g2[inside] = r2
     put_packed(va, PAD2, group, cmul_packed(w2r[inside], w2i[inside], r2, part2))
@@ -389,7 +395,7 @@
     flat = mid_packed(vb, PAD2 + me - reach2, count).reshape(count * quarter, ny)
     r, c = iota2(ny, ny)
     spread = jnp.where(c // 2 == r, 1.0, 0.0).astype(F32)
-    e2 = dot(flat, spread)
+    e2 = dot_exact(flat, spread)
     pool[pl.ds(0, count * quarter, stride=2), :] = e2
     pool[pl.ds(1, count * quarter, stride=2), :] = e2
     base = PAD1 + 2 * (me - reach2)
@@ -421,7 +427,7 @@
 
     def body(m, carry):
         k = 2 * m
-        both = dot(ec[pl.ds(k, 2)].reshape(2 * half, ny), spread)
+        both = dot_exact(ec[pl.ds(k, 2)].reshape(2 * half, ny), spread)
         for j in range(2):
             for c in range(2):
                 e = both[j * half : (j + 1) * half, c * ny : (c + 1) * ny]
@@ -591,13 +597,13 @@
     planes_of(1, 11, nx, pre, 5)
 
 
-def phase_kernel(masks, layout, row, at, *refs):
+def phase_kernel(masks, layout, row, at, ytable, direction, *refs):
     n = max(i for i, _ in layout) + 1
     gathered = refs[:n]
-    table, qrow, found = refs[n:]
+    table, qrow, picks, found = refs[n:]
     me = at[0]
     ny = found.shape[1]
-    nx = table.shape[0] // 2
+    nx = table.shape[0] // 6
     for mask, (i, j) in zip(masks, layout, strict=True):
         found[pl.ds(me ^ mask, 1), :] = gathered[i][j, pl.ds(row, 1), :]
     low = lanes((1, ny)) < ny // 2
@@ -609,13 +615,48 @@
         q = jnp.where(low, pltpu.roll(even, ny // 2, 1), odd)
         turns = (x * p.astype(jnp.int32)) & (nx - 1)
         angle = turns.astype(F32) * (2.0 * math.pi / nx)
-        table[pl.ds(0, nx), pl.ds(pair * ny, ny)] = jnp.cos(angle)
-        table[pl.ds(nx, nx), pl.ds(pair * ny, ny)] = -jnp.sin(angle)
+        for k, values in enumerate((jnp.cos(angle), -jnp.sin(angle))):
+            high = values.astype(jnp.bfloat16)
+            rest = (values - high.astype(F32)).astype(jnp.bfloat16)
+            for part, value in enumerate((high, high, rest)):
+                table[pl.ds((2 * part + k) * nx, nx), pl.ds(pair * ny, ny)] = value
         qrow[:, pl.ds(pair * ny, ny)] = jnp.broadcast_to(q, (8, ny))
+    for pair, found_now in enumerate(picks_of(direction, ytable, table, qrow)):
+        picks[2 * pair : 2 * pair + 2, :] = jnp.concatenate(found_now, axis=0)
+
+
+def picks_of(field, ytable, table, qrow):
+    nx, ny = field.shape[2:]
+    plane = field[:, PLANES - 1].reshape(2 * nx, ny)
+    m = lax.dot_general(
+        ytable[...],
+        plane,
+        (((1,), (1,)), ((), ())),
+        precision=lax.Precision.HIGHEST,
+        preferred_element_type=F32,
+    )
+    sign = jnp.where(lanes((nx, ny)) < ny // 2, -1.0, 1.0)
+    t = m[:nx] + sign * pltpu.roll(m[nx:], nx, 1)
+    both = jnp.concatenate([-sign * t, pltpu.roll(t, nx, 1)], axis=0) * (1.0 / math.sqrt(nx * ny))
+    high = both.astype(jnp.bfloat16)
+    rest = (both - high.astype(F32)).astype(jnp.bfloat16)
+    spectrum = jnp.dot(jnp.concatenate([high, rest, high], axis=1), table[...], preferred_element_type=F32)
+    at_row = lax.broadcasted_iota(jnp.int32, (nx, ny), 0).astype(F32) - ORD_HALF
+    result = []
+    for pair in range(qrow.shape[1] // ny):
+        columns = slice(pair * ny, (pair + 1) * ny)
+        chosen = at_row == qrow[0:1, columns]
+        result.append(
+            [
+                jnp.sum(jnp.where(chosen, spectrum[k * nx : (k + 1) * nx, columns], 0.0), axis=0, keepdims=True)
+                for k in range(2)
+            ]
+        )
+    return result
 
 
 def third_kernel(
-    masks, layout, at, own, direction, image, smooth2, weight, w1r, w1i, w2r, w2i, ytable, xtable, qrow, *refs
+    masks, layout, at, own, direction, image, smooth2, weight, w1r, w1i, w2r, w2i, ytable, xtable, qrow, picks, *refs
 ):
     n = max(i for i, _ in layout) + 1
     gathered, refs = refs[:n], refs[n:]
@@ -672,35 +713,10 @@
     row = lax.broadcasted_iota(jnp.int32, (8, ny), 0)
     alpha[...] = jnp.where(row == 0, ar, ai)
 
-    sign = jnp.where(lanes((nx, ny)) < ny // 2, -1.0, 1.0)
-    stacked = []
-    for field in (direction, corrected):
-        plane = field[:, PLANES - 1].reshape(2 * nx, ny)
-        m = lax.dot_general(
-            ytable[...],
-            plane,
-            (((1,), (1,)), ((), ())),
-            precision=lax.Precision.HIGHEST,
-            preferred_element_type=F32,
-        )
-        t = m[:nx] + sign * pltpu.roll(m[nx:], nx, 1)
-        stacked += [-sign * t, pltpu.roll(t, nx, 1)]
-    spectrum = dot(jnp.concatenate(stacked, axis=0), xtable[...])
-    scale = 1.0 / math.sqrt(nx * ny)
-    at_row = lax.broadcasted_iota(jnp.int32, (nx, ny), 0).astype(F32) - ORD_HALF
-    for pair in range(len(masks) // 2):
-        chosen = at_row == qrow[0:1, pair * ny : (pair + 1) * ny]
-        found = [
-            scale
-            * jnp.sum(
-                jnp.where(chosen, spectrum[k * nx : (k + 1) * nx, pair * ny : (pair + 1) * ny], 0.0),
-                axis=0,
-                keepdims=True,
-            )
-            for k in range(4)
-        ]
+    for pair, found in enumerate(picks_of(corrected, ytable, xtable, qrow)):
         block = 0.0
-        for k, line in enumerate(found + dots):
+        lines = [picks[2 * pair : 2 * pair + 1], picks[2 * pair + 1 : 2 * pair + 2]] + found + dots
+        for k, line in enumerate(lines):
             block = jnp.where(row == k, line, block)
         pay[2 * pair] = block
         pay[2 * pair + 1] = block
@@ -805,9 +821,8 @@
     swap_outer = swap_across(outer, group)
     skip = skip_across(outer, group)
     far = exchange(swap, 1, group)
-    order_row = orders.astype(F32).reshape(1, ny)
     tall = nx + 2 * HALO
-    (pay0,) = call(static_kernel, [(2 * half + half // 2 + 8, ny)], [at, own, order_row], [(2, 2, nx, ny), (half, ny)])
+    (pay0,) = call(static_kernel, [(2 * half + half // 2 + 8, ny)], [at, own, orders], [(2, 2, nx, ny), (half, ny)])
     (pay1,) = call(
         first_kernel,
         [(4 * half + half // 2 + 8, ny)],
@@ -844,12 +859,22 @@
     wide, smooth2 = call(
         widen_kernel, [(2, 12, nx, ny), (2, 12, tall, ny)], [at, image, near2, swap2, weight], [(2, 12, tall, ny)]
     )
-    xtable, qrow = call(
+    ytable = jnp.asarray(y_phases(nx, ny))
+    wanted = group * ny // 2
+    xtable, qrow, picks = pl.pallas_call(
         functools.partial(phase_kernel, masks, layout, 4 * half + half // 2),
-        [(2 * nx, group * ny // 2), (8, group * ny // 2)],
-        [at, *gathered1],
-        [(group, ny)],
-    )
+        out_shape=[
+            jax.ShapeDtypeStruct((6 * nx, wanted), jnp.bfloat16),
+            full((8, wanted)),
+            full((group, ny)),
+        ],
+        in_specs=[SM] + [VM] * (2 + len(gathered1)),
+        out_specs=[VM] * 3,
+        scratch_shapes=[pltpu.VMEM((group, ny), F32)],
+        compiler_params=pltpu.CompilerParams(vmem_limit_bytes=VMEM_LIMIT),
+        cost_estimate=pl.CostEstimate(flops=4000000, bytes_accessed=600000, transcendentals=0),
+        name="phases",
+    )(at, ytable, direction, *gathered1)
     gathered2, masks, layout = gather(pay2, group)
     corrected, last_image, halfway, pay3, alpha = call(
         functools.partial(third_kernel, masks, layout),
@@ -865,9 +890,10 @@
             w1i,
             w2r,
             w2i,
-            jnp.asarray(y_phases(nx, ny)),
+            ytable,
             xtable,
             qrow,
+            picks,
             *gathered2,
         ],
         [(2, 12, tall, ny), (2, 12, tall, ny), (2, 2, nx, ny), (6, half, ny)] + coarse_shapes(group, nx, ny),

time: 101 us -> 97.9 us (0.969)
  waiting for transfers between devices: 30 us -> 25.6 us
  starting transfers between devices: 26.6 us -> 29 us
    ppermute x13, starting transfers between devices: 19.2 us -> 24.8 us  [exchange(): return lax.ppermute(x, 'gz', [(i, i ^ mask) for i in range(group)])]
    ppermute x1, starting transfers between devices: 5.27 us -> 2.2 us  [skip_across(): return lax.ppermute(x, 'gz', pairs)]
    pallas_call x9 -> x8, Pallas kernels: 25.2 us -> 22.2 us  [call(): pl.pallas_call(body, out_shape=[full(o) for o in outs], in_specs=[SM] + [...]
    ppermute x13, waiting for transfers between devices: 24.9 us -> 21.8 us  [exchange(): return lax.ppermute(x, 'gz', [(i, i ^ mask) for i in range(group)])]
    pallas_call x0 -> x1, Pallas kernels: none -> 2.17 us  [on_device(): pl.pallas_call(functools.partial(phase_kernel, masks, layout, 4 * half +...]
    ppermute x1, waiting for transfers between devices: 5.18 us -> 3.73 us  [skip_across(): return lax.ppermute(x, 'gz', pairs)]
    unnamed x14 -> x16, local copies, waits for them, and re-layouts: 1.9 us -> 2.58 us
  transfers between devices with their start and end apart: 17 -> 17, of which waited for: 7 -> 7; matrix products, arithmetic and copies ran while one was open for 1% -> 0% of each run, Pallas kernels for 5% -> 6%
where the time goes in v3:
time: 97.9 us; the launch traced here: 97.6 us
  starting transfers between devices  29 us (30%)
  waiting for transfers between devices  25.6 us (26%)
  Pallas kernels  24.4 us (25%)
  blocking collectives  15.1 us (15%)
  local copies, waits for them, and re-layouts  2.61 us (3%)
    ppermute x13, starting transfers between devices, exchange(): return lax.ppermute(x, 'gz', [(i, i ^ mask) for i in range(group)])  24.8 us
    pallas_call x8, Pallas kernels, call(): pl.pallas_call(body, out_shape=[full(o) for o in outs], in_specs=[SM] + [...  22.2 us
    ppermute x13, waiting for transfers between devices, exchange(): return lax.ppermute(x, 'gz', [(i, i ^ mask) for i in range(group)])  21.8 us
    all_to_all x1, blocking collectives, on_device(): got = lax.all_to_all(pay3, 'gz', 0, 0)  15.1 us
    ppermute x1, waiting for transfers between devices, skip_across(): return lax.ppermute(x, 'gz', pairs)  3.73 us
    unnamed x16, local copies, waits for them, and re-layouts  2.58 us
    ppermute x1, starting transfers between devices, skip_across(): return lax.ppermute(x, 'gz', pairs)  2.2 us
    pallas_call x1, Pallas kernels, on_device(): pl.pallas_call(functools.partial(phase_kernel, masks, layout, 4 * half +...  2.17 us
  transfers between devices with their start and end apart: 17, of which 7 were waited for; matrix products, arithmetic and copies ran while one was open for 0% of the time, Pallas kernels for 6%

profile of v3, /device:TPU:0, one launch (start us, length us, event | category | flops | bytes accessed | tf_op | source)
XLA Modules:
  0.0 97.6 jit_solution(12672571078211972898)
XLA Ops:
  0.7 0.9 copy-done.1
  5.1 0.9 shard_map.69.static
  6.1 1.4 %shard_map.70 = f32[152,128]{1,0:T(8,128)S(1)} custom-call(s32[3]{0:T(128)S(1)} %pad_add_fusion.at, f32[3,4,64,128]{3,2,1,0:T(8,128)S(1)} %get-tuple-element.29.own, f32[3,4,64,128]{3,2,1,0:T(8,128)S(1)} %collective-permute-done.near, f32[3,2,64,128]{3,2,1,0:T(8,128)S(1)} %collective-permute-done.1.swap, f32[88,128]{1,0:T(8,128)S(1)} %shard_map.69.static), custom_call_target="tpu_custom_call" | custom-call | flops 44237280 | bytes 1105932 | tf_op jit(solution)/shard_map/pallas_call | solution.py:177
  7.5 10.3 %collective-permute-start.7 = (f32[1,152,128]{2,1,0:T(8,128)S(1)}, f32[1,152,128]{2,1,0:T(8,128)S(1)}, u32[]{:S(2)}, u32[]{:S(2)}) collective-permute-start(f32[1,152,128]{2,1,0:T(8,128)S(1)} %bitcast.6), channel_id=1, source_target_pairs={{0,12},{1,13},{2,14},{3,15},{4,8},{5,9},{6,10},{7,11},{8,4},{9,5},... | collective-permute-start | bytes 233480 | tf_op jit(solution)/shard_map/ppermute | solution.py:753
  18.4 1.8 %collective-permute-done.7 = f32[1,152,128]{2,1,0:T(8,128)S(1)} collective-permute-done((f32[1,152,128]{2,1,0:T(8,128)S(1)}, f32[1,152,128]{2,1,0:T(8,128)S(1)}, u32[]{:S(2)}, u32[]{:S(2)}) %collective-permute-start.7) | collective-permute-done | bytes 77856 | tf_op jit(solution)/shard_map/ppermute | solution.py:753
  20.2 4.6 %collective-permute-done.6 = f32[1,152,128]{2,1,0:T(8,128)S(1)} collective-permute-done((f32[1,152,128]{2,1,0:T(8,128)S(1)}, f32[1,152,128]{2,1,0:T(8,128)S(1)}, u32[]{:S(2)}, u32[]{:S(2)}) %collective-permute-start.6) | collective-permute-done | bytes 77856 | tf_op jit(solution)/shard_map/ppermute | solution.py:753
  24.8 1.7 %collective-permute-start.8 = (f32[4,152,128]{2,1,0:T(8,128)S(1)}, f32[4,152,128]{2,1,0:T(8,128)S(1)}, u32[]{:S(2)}, u32[]{:S(2)}) collective-permute-start(f32[4,152,128]{2,1,0:T(8,128)S(1)} %pad_maximum_fusion), channel_id=1, source_target_pairs={{0,2},{1,3},{2,0},{3,1},{4,6},{5,7},{6,4},{7,5},{8,10},{9,11},{10,... | collective-permute-start | bytes 933896 | tf_op jit(solution)/shard_map/ppermute | solution.py:753
  26.6 8.0 %collective-permute-done.8 = f32[4,152,128]{2,1,0:T(8,128)S(1)} collective-permute-done((f32[4,152,128]{2,1,0:T(8,128)S(1)}, f32[4,152,128]{2,1,0:T(8,128)S(1)}, u32[]{:S(2)}, u32[]{:S(2)}) %collective-permute-start.8) | collective-permute-done | bytes 311328 | tf_op jit(solution)/shard_map/ppermute | solution.py:753
  34.7 2.2 %collective-permute-start.3 = (f32[3,2,64,128]{3,2,1,0:T(8,128)S(1)}, f32[3,2,64,128]{3,2,1,0:T(8,128)S(1)}, u32[]{:S(2)}, u32[]{:S(2)}) collective-permute-start(f32[3,2,64,128]{3,2,1,0:T(8,128)S(1)} %get-tuple-element.31), channel_id=1, source_target_pairs={{0,2},{2,4},{3,1},{4,6},{5,3},{6,8},{7,5},{8,10},{9,7},{10,12},{11... | collective-permute-start | bytes 589832 | tf_op jit(solution)/shard_map/ppermute | solution.py:769
  37.6 3.5 %collective-permute-start.4 = (f32[3,2,64,128]{3,2,1,0:T(8,128)S(1)}, f32[3,2,64,128]{3,2,1,0:T(8,128)S(1)}, u32[]{:S(2)}, u32[]{:S(2)}) collective-permute-start(f32[3,2,64,128]{3,2,1,0:T(8,128)S(1)} %collective-permute-done.1.swap), channel_id=1, source_target_pairs={{0,1},{1,0},{2,3},{3,2},{4,5},{5,4},{6,7},{7,6},{8,9},{9,8},{10,11... | collective-permute-start | bytes 589832 | tf_op jit(solution)/shard_map/ppermute | solution.py:753
  41.1 3.7 %collective-permute-done.3.skip = f32[3,2,64,128]{3,2,1,0:T(8,128)S(1)} collective-permute-done((f32[3,2,64,128]{3,2,1,0:T(8,128)S(1)}, f32[3,2,64,128]{3,2,1,0:T(8,128)S(1)}, u32[]{:S(2)}, u32[]{:S(2)}) %collective-permute-start.3) | collective-permute-done | bytes 196640 | tf_op jit(solution)/shard_map/ppermute | solution.py:769
  44.9 1.6 %shard_map.68 = (f32[2,16,64,128]{3,2,1,0:T(8,128)S(1)}, f32[2,16,64,128]{3,2,1,0:T(8,128)S(1)}, f32[2,16,80,128]{3,2,1,0:T(8,128)S(1)}, f32[16,64,128]{2,1,0:T(8,128)S(1)}) custom-call(s32[3]{0:T(128)S(1)} %pad_add_fusion.at, f32[3,4,64,128]{3,2,1,0:T(8,128)S(1)} %get-tuple-element.29.own, f32[3,4,64,128]{3,2,1,0:T(8,128)S(1)} %collective-permute-done.near, ...), custom_call_target="tpu_custom_call" | custom-call | flops 220201440 | bytes 5505036 | tf_op jit(solution)/shard_map/pallas_call | solution.py:177
  46.5 7.9 %shard_map.71 = (f32[2,4,64,128]{3,2,1,0:T(8,128)S(1)}, f32[2,8,64,128]{3,2,1,0:T(8,128)S(1)}, f32[2,2,64,128]{3,2,1,0:T(8,128)S(1)}, f32[2,2,64,128]{3,2,1,0:T(...) custom-call(s32[3]{0:T(128)S(1)} %pad_add_fusion.at, ...), custom_call_target="tpu_custom_call" | custom-call | flops 329155040 | bytes 8228876 | tf_op jit(solution)/shard_map/pallas_call | solution.py:177
  54.4 3.0 %collective-permute-start.14 = (f32[1,72,128]{2,1,0:T(8,128)S(1)}, f32[1,72,128]{2,1,0:T(8,128)S(1)}, u32[]{:S(2)}, u32[]{:S(2)}) collective-permute-start(f32[1,72,128]{2,1,0:T(8,128)S(1)} %bitcast.10), channel_id=1, source_target_pairs={{0,12},{1,13},{2,14},{3,15},{4,8},{5,9},{6,10},{7,11},{8,4},{9,5},... | collective-permute-start | bytes 110600 | tf_op jit(solution)/shard_map/ppermute | solution.py:753
  57.5 1.3 %collective-permute-start.12 = (f32[1,72,128]{2,1,0:T(8,128)S(1)}, f32[1,72,128]{2,1,0:T(8,128)S(1)}, u32[]{:S(2)}, u32[]{:S(2)}) collective-permute-start(f32[1,72,128]{2,1,0:T(8,128)S(1)} %bitcast.12), channel_id=1, source_target_pairs={{0,4},{1,5},{2,6},{3,7},{4,0},{5,1},{6,2},{7,3},{8,12},{9,13},{10,... | collective-permute-start | bytes 110600 | tf_op jit(solution)/shard_map/ppermute | solution.py:753
  58.8 1.4 %collective-permute-done.14 = f32[1,72,128]{2,1,0:T(8,128)S(1)} collective-permute-done((f32[1,72,128]{2,1,0:T(8,128)S(1)}, f32[1,72,128]{2,1,0:T(8,128)S(1)}, u32[]{:S(2)}, u32[]{:S(2)}) %collective-permute-start.14) | collective-permute-done | bytes 36896 | tf_op jit(solution)/shard_map/ppermute | solution.py:753
  60.2 2.1 %collective-permute-done.13 = f32[1,72,128]{2,1,0:T(8,128)S(1)} collective-permute-done((f32[1,72,128]{2,1,0:T(8,128)S(1)}, f32[1,72,128]{2,1,0:T(8,128)S(1)}, u32[]{:S(2)}, u32[]{:S(2)}) %collective-permute-start.13) | collective-permute-done | bytes 36896 | tf_op jit(solution)/shard_map/ppermute | solution.py:753
  62.3 2.9 %collective-permute-start.15 = (f32[4,72,128]{2,1,0:T(8,128)S(1)}, f32[4,72,128]{2,1,0:T(8,128)S(1)}, u32[]{:S(2)}, u32[]{:S(2)}) collective-permute-start(f32[4,72,128]{2,1,0:T(8,128)S(1)} %pad_maximum_fusion.1), channel_id=1, source_target_pairs={{0,2},{1,3},{2,0},{3,1},{4,6},{5,7},{6,4},{7,5},{8,10},{9,11},{10,... | collective-permute-start | bytes 442376 | tf_op jit(solution)/shard_map/ppermute | solution.py:753
  65.3 3.9 %collective-permute-done.15 = f32[4,72,128]{2,1,0:T(8,128)S(1)} collective-permute-done((f32[4,72,128]{2,1,0:T(8,128)S(1)}, f32[4,72,128]{2,1,0:T(8,128)S(1)}, u32[]{:S(2)}, u32[]{:S(2)}) %collective-permute-start.15) | collective-permute-done | bytes 147488 | tf_op jit(solution)/shard_map/ppermute | solution.py:753
  70.5 2.2 %phases.1 = (bf16[384,1024]{1,0:T(8,128)(2,1)S(1)}, f32[8,1024]{1,0:T(8,128)S(1)}, f32[16,128]{1,0:T(8,128)S(1)}) custom-call(s32[3]{0:T(128)S(1)} %pad_add_fusion.at, f32[128,128]{1,0:T(8,128)S(1)} %copy-done, f32[2,4,64,128]{3,2,1,0:T(8,128)S(1)} %get-tuple-element.36.direction, f32[8,152,128]{2,1,0:T(8,128)S(1)} %constant_dynamic-update-slice_fusion.refs_0_, ...), custom_call_target="tpu_custom_call" | custom-call | flops 4000000 | bytes 600000 | tf_op jit(solution)/shard_map/phases/pallas_call | solution.py:864
  72.7 1.2 %shard_map.72 = (f32[2,12,64,128]{3,2,1,0:T(8,128)S(1)}, f32[2,12,80,128]{3,2,1,0:T(8,128)S(1)}) custom-call(s32[3]{0:T(128)S(1)} %pad_add_fusion.at, f32[2,8,64,128]{3,2,1,0:T(8,128)S(1)} %get-tuple-element.37.image, f32[2,2,64,128]{3,2,1,0:T(8,128)S(1)} %collective-permute-done.10.near, f32[2,2,64,128]{3,2,1,0:T(8,128)S(1)} %collective-permute-done.11.swap, ...), custom_call_target="tpu_custom_call" | custom-call | flops 144179680 | bytes 3604492 | tf_op jit(solution)/shard_map/pallas_call | solution.py:177
  73.9 7.1 %shard_map.73 = (f32[2,4,64,128]{3,2,1,0:T(8,128)S(1)}, f32[2,4,64,128]{3,2,1,0:T(8,128)S(1)}, f32[2,4,64,128]{3,2,1,0:T(8,128)S(1)}, f32[16,8,128]{2,1,0:T(8,128)S(1)}, f32[8,128]{1,0:T(8,128)S(1)}) custom-call(s32[3]{0:T(128)S(1)} %pad_add_fusion.at, f32[3,4,64,128]{3,2,1,0:T(8,128)S(1)} %get-tuple-element.29.own, ...), custom_call_target="tpu_custom_call" | custom-call | flops 342589920 | bytes 8564748 | tf_op jit(solution)/shard_map/pallas_call | solution.py:177
  81.0 15.1 %all_to_all.5.got = f32[16,8,128]{2,1,0:T(8,128)S(1)} all-to-all(f32[16,8,128]{2,1,0:T(8,128)S(1)} %get-tuple-element.54), channel_id=1, replica_groups=mesh['clip'=2,'gz'=16] {'gz'}, dimensions={0} | all-to-all | bytes 131072 | tf_op jit(solution)/shard_map/all_to_all | solution.py:901
  96.1 1.5 %shard_map.74 = (f32[2,4,64,128]{3,2,1,0:T(8,128)}, f32[2,4,64,128]{3,2,1,0:T(8,128)}, f32[2,64]{1,0:T(2,128)}) custom-call(s32[3]{0:T(128)S(1)} %pad_add_fusion.at, f32[2,4,64,128]{3,2,1,0:T(8,128)S(1)} %get-tuple-element.36.direction, f32[2,4,64,128]{3,2,1,0:T(8,128)S(1)} %get-tuple-element.50.corrected, ...), custom_call_target="tpu_custom_call" | custom-call | flops 65720800 | bytes 1643020 | tf_op jit(solution)/shard_map/pallas_call | solution.py:177
  (41 shorter events, 6.4 us)
Async XLA Ops:
  0.7 1.0 copy-start.1
  1.7 0.9 copy-start.2
  3.2 2.9 %collective-permute-start = (f32[3,4,64,128]{3,2,1,0:T(8,128)S(1)}, f32[3,4,64,128]{3,2,1,0:T(8,128)S(1)}, u32[]{:S(2)}, u32[]{:S(2)}) collective-permute-start(f32[3,4,64,128]{3,2,1,0:T(8,128)S(1)} %get-tuple-element.29.own), channel_id=1, source_target_pairs={{0,1},{1,0},{2,3},{3,2},{4,5},{5,4},{6,7},{7,6},{8,9},{9,8},{10,11... | collective-permute-start | bytes 1179656 | tf_op jit(solution)/shard_map/ppermute | solution.py:753
  3.7 2.3 %collective-permute-start.1 = (f32[3,2,64,128]{3,2,1,0:T(8,128)S(1)}, f32[3,2,64,128]{3,2,1,0:T(8,128)S(1)}, u32[]{:S(2)}, u32[]{:S(2)}) collective-permute-start(f32[3,2,64,128]{3,2,1,0:T(8,128)S(1)} %get-tuple-element.30), channel_id=1, source_target_pairs={{1,2},{2,1},{3,4},{4,3},{5,6},{6,5},{7,8},{8,7},{9,10},{10,9},{11,... | collective-permute-start | bytes 589832 | tf_op jit(solution)/shard_map/ppermute | solution.py:760
  4.4 0.7 copy-start.3
  7.5 12.8 %collective-permute-start.7 = (f32[1,152,128]{2,1,0:T(8,128)S(1)}, f32[1,152,128]{2,1,0:T(8,128)S(1)}, u32[]{:S(2)}, u32[]{:S(2)}) collective-permute-start(f32[1,152,128]{2,1,0:T(8,128)S(1)} %bitcast.6), channel_id=1, source_target_pairs={{0,12},{1,13},{2,14},{3,15},{4,8},{5,9},{6,10},{7,11},{8,4},{9,5},... | collective-permute-start | bytes 233480 | tf_op jit(solution)/shard_map/ppermute | solution.py:753
  17.8 7.0 %collective-permute-start.6 = (f32[1,152,128]{2,1,0:T(8,128)S(1)}, f32[1,152,128]{2,1,0:T(8,128)S(1)}, u32[]{:S(2)}, u32[]{:S(2)}) collective-permute-start(f32[1,152,128]{2,1,0:T(8,128)S(1)} %bitcast.7), channel_id=1, source_target_pairs={{0,8},{1,9},{2,10},{3,11},{4,12},{5,13},{6,14},{7,15},{8,0},{9,1},... | collective-permute-start | bytes 233480 | tf_op jit(solution)/shard_map/ppermute | solution.py:753
  17.8 7.0 %collective-permute-start.5 = (f32[1,152,128]{2,1,0:T(8,128)S(1)}, f32[1,152,128]{2,1,0:T(8,128)S(1)}, u32[]{:S(2)}, u32[]{:S(2)}) collective-permute-start(f32[1,152,128]{2,1,0:T(8,128)S(1)} %bitcast.8), channel_id=1, source_target_pairs={{0,4},{1,5},{2,6},{3,7},{4,0},{5,1},{6,2},{7,3},{8,12},{9,13},{10,... | collective-permute-start | bytes 233480 | tf_op jit(solution)/shard_map/ppermute | solution.py:753
  24.8 9.8 %collective-permute-start.8 = (f32[4,152,128]{2,1,0:T(8,128)S(1)}, f32[4,152,128]{2,1,0:T(8,128)S(1)}, u32[]{:S(2)}, u32[]{:S(2)}) collective-permute-start(f32[4,152,128]{2,1,0:T(8,128)S(1)} %pad_maximum_fusion), channel_id=1, source_target_pairs={{0,2},{1,3},{2,0},{3,1},{4,6},{5,7},{6,4},{7,5},{8,10},{9,11},{10,... | collective-permute-start | bytes 933896 | tf_op jit(solution)/shard_map/ppermute | solution.py:753
  34.6 11.8 %collective-permute-start.9 = (f32[8,152,128]{2,1,0:T(8,128)S(1)}, f32[8,152,128]{2,1,0:T(8,128)S(1)}, u32[]{:S(2)}, u32[]{:S(2)}) collective-permute-start(f32[8,152,128]{2,1,0:T(8,128)S(1)} %constant_dynamic-update-slice_fusion.refs_0_), channel_id=1, source_target_pairs={{0,1},{1,0},{2,3},{3,2},{4,5},{5,4},{6,7},{7,6},{8,9},{9,8},{10,11... | collective-permute-start | bytes 1867784 | tf_op jit(solution)/shard_map/ppermute | solution.py:753
  34.7 10.2 %collective-permute-start.3 = (f32[3,2,64,128]{3,2,1,0:T(8,128)S(1)}, f32[3,2,64,128]{3,2,1,0:T(8,128)S(1)}, u32[]{:S(2)}, u32[]{:S(2)}) collective-permute-start(f32[3,2,64,128]{3,2,1,0:T(8,128)S(1)} %get-tuple-element.31), channel_id=1, source_target_pairs={{0,2},{2,4},{3,1},{4,6},{5,3},{6,8},{7,5},{8,10},{9,7},{10,12},{11... | collective-permute-start | bytes 589832 | tf_op jit(solution)/shard_map/ppermute | solution.py:769
  36.9 8.0 %collective-permute-start.2 = (f32[3,2,64,128]{3,2,1,0:T(8,128)S(1)}, f32[3,2,64,128]{3,2,1,0:T(8,128)S(1)}, u32[]{:S(2)}, u32[]{:S(2)}) collective-permute-start(f32[3,2,64,128]{3,2,1,0:T(8,128)S(1)} %get-tuple-element.31), channel_id=1, source_target_pairs={{1,2},{2,1},{3,4},{4,3},{5,6},{6,5},{7,8},{8,7},{9,10},{10,9},{11,... | collective-permute-start | bytes 589832 | tf_op jit(solution)/shard_map/ppermute | solution.py:760
  37.6 7.3 %collective-permute-start.4 = (f32[3,2,64,128]{3,2,1,0:T(8,128)S(1)}, f32[3,2,64,128]{3,2,1,0:T(8,128)S(1)}, u32[]{:S(2)}, u32[]{:S(2)}) collective-permute-start(f32[3,2,64,128]{3,2,1,0:T(8,128)S(1)} %collective-permute-done.1.swap), channel_id=1, source_target_pairs={{0,1},{1,0},{2,3},{3,2},{4,5},{5,4},{6,7},{7,6},{8,9},{9,8},{10,11... | collective-permute-start | bytes 589832 | tf_op jit(solution)/shard_map/ppermute | solution.py:753
  46.5 24.0 %copy-start = (f32[128,128]{1,0:T(8,128)S(1)}, f32[128,128]{1,0:T(8,128)}, u32[]{:S(2)}) copy-start(f32[128,128]{1,0:T(8,128)} %constant.21.clone.ytable) | copy-start | bytes 196612
  54.4 5.8 %collective-permute-start.14 = (f32[1,72,128]{2,1,0:T(8,128)S(1)}, f32[1,72,128]{2,1,0:T(8,128)S(1)}, u32[]{:S(2)}, u32[]{:S(2)}) collective-permute-start(f32[1,72,128]{2,1,0:T(8,128)S(1)} %bitcast.10), channel_id=1, source_target_pairs={{0,12},{1,13},{2,14},{3,15},{4,8},{5,9},{6,10},{7,11},{8,4},{9,5},... | collective-permute-start | bytes 110600 | tf_op jit(solution)/shard_map/ppermute | solution.py:753
  57.4 4.9 %collective-permute-start.13 = (f32[1,72,128]{2,1,0:T(8,128)S(1)}, f32[1,72,128]{2,1,0:T(8,128)S(1)}, u32[]{:S(2)}, u32[]{:S(2)}) collective-permute-start(f32[1,72,128]{2,1,0:T(8,128)S(1)} %bitcast.11), channel_id=1, source_target_pairs={{0,8},{1,9},{2,10},{3,11},{4,12},{5,13},{6,14},{7,15},{8,0},{9,1},... | collective-permute-start | bytes 110600 | tf_op jit(solution)/shard_map/ppermute | solution.py:753
  57.5 4.8 %collective-permute-start.12 = (f32[1,72,128]{2,1,0:T(8,128)S(1)}, f32[1,72,128]{2,1,0:T(8,128)S(1)}, u32[]{:S(2)}, u32[]{:S(2)}) collective-permute-start(f32[1,72,128]{2,1,0:T(8,128)S(1)} %bitcast.12), channel_id=1, source_target_pairs={{0,4},{1,5},{2,6},{3,7},{4,0},{5,1},{6,2},{7,3},{8,12},{9,13},{10,... | collective-permute-start | bytes 110600 | tf_op jit(solution)/shard_map/ppermute | solution.py:753
  62.3 6.9 %collective-permute-start.15 = (f32[4,72,128]{2,1,0:T(8,128)S(1)}, f32[4,72,128]{2,1,0:T(8,128)S(1)}, u32[]{:S(2)}, u32[]{:S(2)}) collective-permute-start(f32[4,72,128]{2,1,0:T(8,128)S(1)} %pad_maximum_fusion.1), channel_id=1, source_target_pairs={{0,2},{1,3},{2,0},{3,1},{4,6},{5,7},{6,4},{7,5},{8,10},{9,11},{10,... | collective-permute-start | bytes 442376 | tf_op jit(solution)/shard_map/ppermute | solution.py:753
  69.2 4.7 %collective-permute-start.16 = (f32[8,72,128]{2,1,0:T(8,128)S(1)}, f32[8,72,128]{2,1,0:T(8,128)S(1)}, u32[]{:S(2)}, u32[]{:S(2)}) collective-permute-start(f32[8,72,128]{2,1,0:T(8,128)S(1)} %constant_dynamic-update-slice_fusion.5.refs_0_), channel_id=1, source_target_pairs={{0,1},{1,0},{2,3},{3,2},{4,5},{5,4},{6,7},{7,6},{8,9},{9,8},{10,11... | collective-permute-start | bytes 884744 | tf_op jit(solution)/shard_map/ppermute | solution.py:753
  69.3 3.4 %collective-permute-start.10 = (f32[2,2,64,128]{3,2,1,0:T(8,128)S(1)}, f32[2,2,64,128]{3,2,1,0:T(8,128)S(1)}, u32[]{:S(2)}, u32[]{:S(2)}) collective-permute-start(f32[2,2,64,128]{3,2,1,0:T(8,128)S(1)} %get-tuple-element.38), channel_id=1, source_target_pairs={{0,1},{1,0},{2,3},{3,2},{4,5},{5,4},{6,7},{7,6},{8,9},{9,8},{10,11... | collective-permute-start | bytes 393224 | tf_op jit(solution)/shard_map/ppermute | solution.py:753
  69.8 2.9 %collective-permute-start.11 = (f32[2,2,64,128]{3,2,1,0:T(8,128)S(1)}, f32[2,2,64,128]{3,2,1,0:T(8,128)S(1)}, u32[]{:S(2)}, u32[]{:S(2)}) collective-permute-start(f32[2,2,64,128]{3,2,1,0:T(8,128)S(1)} %get-tuple-element.39), channel_id=1, source_target_pairs={{1,2},{2,1},{3,4},{4,3},{5,6},{6,5},{7,8},{8,7},{9,10},{10,9},{11,... | collective-permute-start | bytes 393224 | tf_op jit(solution)/shard_map/ppermute | solution.py:760

commit v4 on v3

--- a/solution.py
+++ b/solution.py
@@ -348,10 +348,10 @@
     group = len(masks)
     part1, part2 = ny // 2, ny // 4
     n1 = 2 * group
-    clear_edges(g1, PAD1, PAD1 - 1)
+    clear_edges(g1, PAD1, reach + 1)
     clear_edges(u1, PAD1, 1)
     clear_edges(u2, PAD1, 1)
-    clear_edges(v1, PAD1, PAD1 - 1)
+    clear_edges(v1, PAD1, reach + 2)
     clear_edges(va, PAD2, 1)
     clear_edges(vb, PAD2, PAD2 - 1)
     for mask, (piece, j) in zip(masks, pieces, strict=True):
@@ -367,7 +367,7 @@
         put_packed(u2, p, n, u)
         put_packed(v1, p, n, mid_packed(u1, p, n) + u)
 
-    chunked(PAD1, n1, 8, pre)
+    chunked(PAD1, n1, 16, pre)
 
     def coarser(p, n):
         e = KEEP * e1[pl.ds(p, n), pl.ds(0, half), :] + H1 * around_packed(u2, p, n, part1, zero)
@@ -375,7 +375,7 @@
         pairs = (e[:, 0] + e[:, 1]).reshape(n // 2 * half, ny)
         pool[pl.ds((p - PAD1) // 2 * half, n // 2 * half), :] = pairs
 
-    chunked(PAD1, n1, 8, coarser)
+    chunked(PAD1, n1, 16, coarser)
     rows = group * quarter
     flat = pool[pl.ds(0, rows, stride=2), :] + pool[pl.ds(1, rows, stride=2), :]
     r2 = dot_exact(flat, pool_level1(ny)).reshape(group, quarter, ny)
@@ -416,8 +416,8 @@
     def fourth(p, n):
         out[pl.ds(p - (start - reach), n)] = post(u1, p, n)
 
-    chunked(start - reach - 1, 2 * reach + 4, 6, third)
-    chunked(start - reach, 2 * reach + 2, 5, fourth)
+    chunked(start - reach - 1, 2 * reach + 4, 10, third)
+    chunked(start - reach, 2 * reach + 2, 8, fourth)
 
 
 def add_correction(ec, before, v, tmp, planes, nx):
@@ -501,8 +501,8 @@
         put(dst, 0, p, r0, KEEP * mid(src, 0, p, r0) + vr, nx)
         put(dst, 1, p, r0, KEEP * mid(src, 1, p, r0) + vi, nx)
 
-    planes_of(2, WINDOW - 2, nx, lambda *a: sweep(v, u, *a))
-    planes_of(3, WINDOW - 3, nx, lambda *a: sweep(u, v, *a), 5)
+    planes_of(2, WINDOW - 2, nx, lambda *a: sweep(v, u, *a), 6)
+    planes_of(3, WINDOW - 3, nx, lambda *a: sweep(u, v, *a), 10)
 
     def apply(p, r0, rows):
         sr, si = around(v, p, r0, zero)
@@ -518,7 +518,7 @@
         put(u, 0, p, r0, ur, nx)
         put(u, 1, p, r0, ui, nx)
 
-    planes_of(4, WINDOW - 4, nx, apply)
+    planes_of(4, WINDOW - 4, nx, apply, 8)
     rho, cross_r, cross_i = 0.0, 0.0, 0.0
     for q in range(PLANES):
         for r0 in range(0, nx, CHUNK):
@@ -677,8 +677,8 @@
         put(dst, 0, p, r0, KEEP * mid(src, 0, p, r0) + vr, nx)
         put(dst, 1, p, r0, KEEP * mid(src, 1, p, r0) + vi, nx)
 
-    planes_of(2, 10, nx, lambda *a: sweep(v, u, *a))
-    planes_of(3, 9, nx, lambda *a: sweep(u, v, *a))
+    planes_of(2, 10, nx, lambda *a: sweep(v, u, *a), 8)
+    planes_of(3, 9, nx, lambda *a: sweep(u, v, *a), 6)
 
     sums = 0.0
     for i, j in layout:

time: 97.9 us -> 95.9 us (0.980)
  Pallas kernels: 24.4 us -> 22.4 us
    pallas_call x8, Pallas kernels: 22.2 us -> 20.3 us  [call(): pl.pallas_call(body, out_shape=[full(o) for o in outs], in_specs=[SM] + [...]
where the time goes in v4:
time: 95.9 us; the launch traced here: 95.6 us
  starting transfers between devices  29 us (30%)
  waiting for transfers between devices  25.6 us (27%)
  Pallas kernels  22.4 us (23%)
  blocking collectives  15.1 us (16%)
  local copies, waits for them, and re-layouts  2.61 us (3%)
    ppermute x13, starting transfers between devices, exchange(): return lax.ppermute(x, 'gz', [(i, i ^ mask) for i in range(group)])  24.8 us
    ppermute x13, waiting for transfers between devices, exchange(): return lax.ppermute(x, 'gz', [(i, i ^ mask) for i in range(group)])  21.8 us
    pallas_call x8, Pallas kernels, call(): pl.pallas_call(body, out_shape=[full(o) for o in outs], in_specs=[SM] + [...  20.3 us
    all_to_all x1, blocking collectives, on_device(): got = lax.all_to_all(pay3, 'gz', 0, 0)  15.1 us
    ppermute x1, waiting for transfers between devices, skip_across(): return lax.ppermute(x, 'gz', pairs)  3.73 us
    unnamed x16, local copies, waits for them, and re-layouts  2.58 us
    ppermute x1, starting transfers between devices, skip_across(): return lax.ppermute(x, 'gz', pairs)  2.2 us
    pallas_call x1, Pallas kernels, on_device(): pl.pallas_call(functools.partial(phase_kernel, masks, layout, 4 * half +...  2.17 us
  transfers between devices with their start and end apart: 17, of which 7 were waited for; matrix products, arithmetic and copies ran while one was open for 0% of the time, Pallas kernels for 6%

profile of v4, /device:TPU:0, one launch (start us, length us, event | category | flops | bytes accessed | tf_op | source)
XLA Modules:
  0.0 95.6 jit_solution(8873876338144985702)
XLA Ops:
  0.7 0.9 copy-done.1
  5.1 0.9 shard_map.69.static
  6.1 1.4 %shard_map.70 = f32[152,128]{1,0:T(8,128)S(1)} custom-call(s32[3]{0:T(128)S(1)} %pad_add_fusion.at, f32[3,4,64,128]{3,2,1,0:T(8,128)S(1)} %get-tuple-element.29.own, f32[3,4,64,128]{3,2,1,0:T(8,128)S(1)} %collective-permute-done.near, f32[3,2,64,128]{3,2,1,0:T(8,128)S(1)} %collective-permute-done.1.swap, f32[88,128]{1,0:T(8,128)S(1)} %shard_map.69.static), custom_call_target="tpu_custom_call" | custom-call | flops 44237280 | bytes 1105932 | tf_op jit(solution)/shard_map/pallas_call | solution.py:177
  7.5 10.3 %collective-permute-start.7 = (f32[1,152,128]{2,1,0:T(8,128)S(1)}, f32[1,152,128]{2,1,0:T(8,128)S(1)}, u32[]{:S(2)}, u32[]{:S(2)}) collective-permute-start(f32[1,152,128]{2,1,0:T(8,128)S(1)} %bitcast.6), channel_id=1, source_target_pairs={{0,12},{1,13},{2,14},{3,15},{4,8},{5,9},{6,10},{7,11},{8,4},{9,5},... | collective-permute-start | bytes 233480 | tf_op jit(solution)/shard_map/ppermute | solution.py:753
  18.4 1.8 %collective-permute-done.7 = f32[1,152,128]{2,1,0:T(8,128)S(1)} collective-permute-done((f32[1,152,128]{2,1,0:T(8,128)S(1)}, f32[1,152,128]{2,1,0:T(8,128)S(1)}, u32[]{:S(2)}, u32[]{:S(2)}) %collective-permute-start.7) | collective-permute-done | bytes 77856 | tf_op jit(solution)/shard_map/ppermute | solution.py:753
  20.2 4.6 %collective-permute-done.6 = f32[1,152,128]{2,1,0:T(8,128)S(1)} collective-permute-done((f32[1,152,128]{2,1,0:T(8,128)S(1)}, f32[1,152,128]{2,1,0:T(8,128)S(1)}, u32[]{:S(2)}, u32[]{:S(2)}) %collective-permute-start.6) | collective-permute-done | bytes 77856 | tf_op jit(solution)/shard_map/ppermute | solution.py:753
  24.8 1.7 %collective-permute-start.8 = (f32[4,152,128]{2,1,0:T(8,128)S(1)}, f32[4,152,128]{2,1,0:T(8,128)S(1)}, u32[]{:S(2)}, u32[]{:S(2)}) collective-permute-start(f32[4,152,128]{2,1,0:T(8,128)S(1)} %pad_maximum_fusion), channel_id=1, source_target_pairs={{0,2},{1,3},{2,0},{3,1},{4,6},{5,7},{6,4},{7,5},{8,10},{9,11},{10,... | collective-permute-start | bytes 933896 | tf_op jit(solution)/shard_map/ppermute | solution.py:753
  26.6 8.0 %collective-permute-done.8 = f32[4,152,128]{2,1,0:T(8,128)S(1)} collective-permute-done((f32[4,152,128]{2,1,0:T(8,128)S(1)}, f32[4,152,128]{2,1,0:T(8,128)S(1)}, u32[]{:S(2)}, u32[]{:S(2)}) %collective-permute-start.8) | collective-permute-done | bytes 311328 | tf_op jit(solution)/shard_map/ppermute | solution.py:753
  34.7 2.2 %collective-permute-start.3 = (f32[3,2,64,128]{3,2,1,0:T(8,128)S(1)}, f32[3,2,64,128]{3,2,1,0:T(8,128)S(1)}, u32[]{:S(2)}, u32[]{:S(2)}) collective-permute-start(f32[3,2,64,128]{3,2,1,0:T(8,128)S(1)} %get-tuple-element.31), channel_id=1, source_target_pairs={{0,2},{2,4},{3,1},{4,6},{5,3},{6,8},{7,5},{8,10},{9,7},{10,12},{11... | collective-permute-start | bytes 589832 | tf_op jit(solution)/shard_map/ppermute | solution.py:769
  37.6 3.5 %collective-permute-start.4 = (f32[3,2,64,128]{3,2,1,0:T(8,128)S(1)}, f32[3,2,64,128]{3,2,1,0:T(8,128)S(1)}, u32[]{:S(2)}, u32[]{:S(2)}) collective-permute-start(f32[3,2,64,128]{3,2,1,0:T(8,128)S(1)} %collective-permute-done.1.swap), channel_id=1, source_target_pairs={{0,1},{1,0},{2,3},{3,2},{4,5},{5,4},{6,7},{7,6},{8,9},{9,8},{10,11... | collective-permute-start | bytes 589832 | tf_op jit(solution)/shard_map/ppermute | solution.py:753
  41.1 3.7 %collective-permute-done.3.skip = f32[3,2,64,128]{3,2,1,0:T(8,128)S(1)} collective-permute-done((f32[3,2,64,128]{3,2,1,0:T(8,128)S(1)}, f32[3,2,64,128]{3,2,1,0:T(8,128)S(1)}, u32[]{:S(2)}, u32[]{:S(2)}) %collective-permute-start.3) | collective-permute-done | bytes 196640 | tf_op jit(solution)/shard_map/ppermute | solution.py:769
  44.9 1.6 %shard_map.68 = (f32[2,16,64,128]{3,2,1,0:T(8,128)S(1)}, f32[2,16,64,128]{3,2,1,0:T(8,128)S(1)}, f32[2,16,80,128]{3,2,1,0:T(8,128)S(1)}, f32[16,64,128]{2,1,0:T(8,128)S(1)}) custom-call(s32[3]{0:T(128)S(1)} %pad_add_fusion.at, f32[3,4,64,128]{3,2,1,0:T(8,128)S(1)} %get-tuple-element.29.own, f32[3,4,64,128]{3,2,1,0:T(8,128)S(1)} %collective-permute-done.near, ...), custom_call_target="tpu_custom_call" | custom-call | flops 220201440 | bytes 5505036 | tf_op jit(solution)/shard_map/pallas_call | solution.py:177
  46.5 7.0 %shard_map.71 = (f32[2,4,64,128]{3,2,1,0:T(8,128)S(1)}, f32[2,8,64,128]{3,2,1,0:T(8,128)S(1)}, f32[2,2,64,128]{3,2,1,0:T(8,128)S(1)}, f32[2,2,64,128]{3,2,1,0:T(...) custom-call(s32[3]{0:T(128)S(1)} %pad_add_fusion.at, ...), custom_call_target="tpu_custom_call" | custom-call | flops 329155040 | bytes 8228876 | tf_op jit(solution)/shard_map/pallas_call | solution.py:177
  53.4 3.0 %collective-permute-start.14 = (f32[1,72,128]{2,1,0:T(8,128)S(1)}, f32[1,72,128]{2,1,0:T(8,128)S(1)}, u32[]{:S(2)}, u32[]{:S(2)}) collective-permute-start(f32[1,72,128]{2,1,0:T(8,128)S(1)} %bitcast.10), channel_id=1, source_target_pairs={{0,12},{1,13},{2,14},{3,15},{4,8},{5,9},{6,10},{7,11},{8,4},{9,5},... | collective-permute-start | bytes 110600 | tf_op jit(solution)/shard_map/ppermute | solution.py:753
  56.6 1.3 %collective-permute-start.12 = (f32[1,72,128]{2,1,0:T(8,128)S(1)}, f32[1,72,128]{2,1,0:T(8,128)S(1)}, u32[]{:S(2)}, u32[]{:S(2)}) collective-permute-start(f32[1,72,128]{2,1,0:T(8,128)S(1)} %bitcast.12), channel_id=1, source_target_pairs={{0,4},{1,5},{2,6},{3,7},{4,0},{5,1},{6,2},{7,3},{8,12},{9,13},{10,... | collective-permute-start | bytes 110600 | tf_op jit(solution)/shard_map/ppermute | solution.py:753
  57.9 1.4 %collective-permute-done.14 = f32[1,72,128]{2,1,0:T(8,128)S(1)} collective-permute-done((f32[1,72,128]{2,1,0:T(8,128)S(1)}, f32[1,72,128]{2,1,0:T(8,128)S(1)}, u32[]{:S(2)}, u32[]{:S(2)}) %collective-permute-start.14) | collective-permute-done | bytes 36896 | tf_op jit(solution)/shard_map/ppermute | solution.py:753
  59.2 2.1 %collective-permute-done.13 = f32[1,72,128]{2,1,0:T(8,128)S(1)} collective-permute-done((f32[1,72,128]{2,1,0:T(8,128)S(1)}, f32[1,72,128]{2,1,0:T(8,128)S(1)}, u32[]{:S(2)}, u32[]{:S(2)}) %collective-permute-start.13) | collective-permute-done | bytes 36896 | tf_op jit(solution)/shard_map/ppermute | solution.py:753
  61.4 2.9 %collective-permute-start.15 = (f32[4,72,128]{2,1,0:T(8,128)S(1)}, f32[4,72,128]{2,1,0:T(8,128)S(1)}, u32[]{:S(2)}, u32[]{:S(2)}) collective-permute-start(f32[4,72,128]{2,1,0:T(8,128)S(1)} %pad_maximum_fusion.1), channel_id=1, source_target_pairs={{0,2},{1,3},{2,0},{3,1},{4,6},{5,7},{6,4},{7,5},{8,10},{9,11},{10,... | collective-permute-start | bytes 442376 | tf_op jit(solution)/shard_map/ppermute | solution.py:753
  64.3 3.9 %collective-permute-done.15 = f32[4,72,128]{2,1,0:T(8,128)S(1)} collective-permute-done((f32[4,72,128]{2,1,0:T(8,128)S(1)}, f32[4,72,128]{2,1,0:T(8,128)S(1)}, u32[]{:S(2)}, u32[]{:S(2)}) %collective-permute-start.15) | collective-permute-done | bytes 147488 | tf_op jit(solution)/shard_map/ppermute | solution.py:753
  69.5 2.2 %phases.1 = (bf16[384,1024]{1,0:T(8,128)(2,1)S(1)}, f32[8,1024]{1,0:T(8,128)S(1)}, f32[16,128]{1,0:T(8,128)S(1)}) custom-call(s32[3]{0:T(128)S(1)} %pad_add_fusion.at, f32[128,128]{1,0:T(8,128)S(1)} %copy-done, f32[2,4,64,128]{3,2,1,0:T(8,128)S(1)} %get-tuple-element.36.direction, f32[8,152,128]{2,1,0:T(8,128)S(1)} %constant_dynamic-update-slice_fusion.refs_0_, ...), custom_call_target="tpu_custom_call" | custom-call | flops 4000000 | bytes 600000 | tf_op jit(solution)/shard_map/phases/pallas_call | solution.py:864
  71.7 1.2 %shard_map.72 = (f32[2,12,64,128]{3,2,1,0:T(8,128)S(1)}, f32[2,12,80,128]{3,2,1,0:T(8,128)S(1)}) custom-call(s32[3]{0:T(128)S(1)} %pad_add_fusion.at, f32[2,8,64,128]{3,2,1,0:T(8,128)S(1)} %get-tuple-element.37.image, f32[2,2,64,128]{3,2,1,0:T(8,128)S(1)} %collective-permute-done.10.near, f32[2,2,64,128]{3,2,1,0:T(8,128)S(1)} %collective-permute-done.11.swap, ...), custom_call_target="tpu_custom_call" | custom-call | flops 144179680 | bytes 3604492 | tf_op jit(solution)/shard_map/pallas_call | solution.py:177
  73.0 6.1 %shard_map.73 = (f32[2,4,64,128]{3,2,1,0:T(8,128)S(1)}, f32[2,4,64,128]{3,2,1,0:T(8,128)S(1)}, f32[2,4,64,128]{3,2,1,0:T(8,128)S(1)}, f32[16,8,128]{2,1,0:T(8,128)S(1)}, f32[8,128]{1,0:T(8,128)S(1)}) custom-call(s32[3]{0:T(128)S(1)} %pad_add_fusion.at, f32[3,4,64,128]{3,2,1,0:T(8,128)S(1)} %get-tuple-element.29.own, ...), custom_call_target="tpu_custom_call" | custom-call | flops 342589920 | bytes 8564748 | tf_op jit(solution)/shard_map/pallas_call | solution.py:177
  79.0 15.1 %all_to_all.5.got = f32[16,8,128]{2,1,0:T(8,128)S(1)} all-to-all(f32[16,8,128]{2,1,0:T(8,128)S(1)} %get-tuple-element.54), channel_id=1, replica_groups=mesh['clip'=2,'gz'=16] {'gz'}, dimensions={0} | all-to-all | bytes 131072 | tf_op jit(solution)/shard_map/all_to_all | solution.py:901
  94.1 1.5 %shard_map.74 = (f32[2,4,64,128]{3,2,1,0:T(8,128)}, f32[2,4,64,128]{3,2,1,0:T(8,128)}, f32[2,64]{1,0:T(2,128)}) custom-call(s32[3]{0:T(128)S(1)} %pad_add_fusion.at, f32[2,4,64,128]{3,2,1,0:T(8,128)S(1)} %get-tuple-element.36.direction, f32[2,4,64,128]{3,2,1,0:T(8,128)S(1)} %get-tuple-element.50.corrected, ...), custom_call_target="tpu_custom_call" | custom-call | flops 65720800 | bytes 1643020 | tf_op jit(solution)/shard_map/pallas_call | solution.py:177
  (41 shorter events, 6.4 us)
Async XLA Ops:
  0.7 1.0 copy-start.1
  1.7 0.9 copy-start.2
  3.2 2.9 %collective-permute-start = (f32[3,4,64,128]{3,2,1,0:T(8,128)S(1)}, f32[3,4,64,128]{3,2,1,0:T(8,128)S(1)}, u32[]{:S(2)}, u32[]{:S(2)}) collective-permute-start(f32[3,4,64,128]{3,2,1,0:T(8,128)S(1)} %get-tuple-element.29.own), channel_id=1, source_target_pairs={{0,1},{1,0},{2,3},{3,2},{4,5},{5,4},{6,7},{7,6},{8,9},{9,8},{10,11... | collective-permute-start | bytes 1179656 | tf_op jit(solution)/shard_map/ppermute | solution.py:753
  3.7 2.3 %collective-permute-start.1 = (f32[3,2,64,128]{3,2,1,0:T(8,128)S(1)}, f32[3,2,64,128]{3,2,1,0:T(8,128)S(1)}, u32[]{:S(2)}, u32[]{:S(2)}) collective-permute-start(f32[3,2,64,128]{3,2,1,0:T(8,128)S(1)} %get-tuple-element.30), channel_id=1, source_target_pairs={{1,2},{2,1},{3,4},{4,3},{5,6},{6,5},{7,8},{8,7},{9,10},{10,9},{11,... | collective-permute-start | bytes 589832 | tf_op jit(solution)/shard_map/ppermute | solution.py:760
  4.4 0.7 copy-start.3
  7.5 12.8 %collective-permute-start.7 = (f32[1,152,128]{2,1,0:T(8,128)S(1)}, f32[1,152,128]{2,1,0:T(8,128)S(1)}, u32[]{:S(2)}, u32[]{:S(2)}) collective-permute-start(f32[1,152,128]{2,1,0:T(8,128)S(1)} %bitcast.6), channel_id=1, source_target_pairs={{0,12},{1,13},{2,14},{3,15},{4,8},{5,9},{6,10},{7,11},{8,4},{9,5},... | collective-permute-start | bytes 233480 | tf_op jit(solution)/shard_map/ppermute | solution.py:753
  17.8 7.0 %collective-permute-start.6 = (f32[1,152,128]{2,1,0:T(8,128)S(1)}, f32[1,152,128]{2,1,0:T(8,128)S(1)}, u32[]{:S(2)}, u32[]{:S(2)}) collective-permute-start(f32[1,152,128]{2,1,0:T(8,128)S(1)} %bitcast.7), channel_id=1, source_target_pairs={{0,8},{1,9},{2,10},{3,11},{4,12},{5,13},{6,14},{7,15},{8,0},{9,1},... | collective-permute-start | bytes 233480 | tf_op jit(solution)/shard_map/ppermute | solution.py:753
  17.8 7.0 %collective-permute-start.5 = (f32[1,152,128]{2,1,0:T(8,128)S(1)}, f32[1,152,128]{2,1,0:T(8,128)S(1)}, u32[]{:S(2)}, u32[]{:S(2)}) collective-permute-start(f32[1,152,128]{2,1,0:T(8,128)S(1)} %bitcast.8), channel_id=1, source_target_pairs={{0,4},{1,5},{2,6},{3,7},{4,0},{5,1},{6,2},{7,3},{8,12},{9,13},{10,... | collective-permute-start | bytes 233480 | tf_op jit(solution)/shard_map/ppermute | solution.py:753
  24.8 9.8 %collective-permute-start.8 = (f32[4,152,128]{2,1,0:T(8,128)S(1)}, f32[4,152,128]{2,1,0:T(8,128)S(1)}, u32[]{:S(2)}, u32[]{:S(2)}) collective-permute-start(f32[4,152,128]{2,1,0:T(8,128)S(1)} %pad_maximum_fusion), channel_id=1, source_target_pairs={{0,2},{1,3},{2,0},{3,1},{4,6},{5,7},{6,4},{7,5},{8,10},{9,11},{10,... | collective-permute-start | bytes 933896 | tf_op jit(solution)/shard_map/ppermute | solution.py:753
  34.6 11.8 %collective-permute-start.9 = (f32[8,152,128]{2,1,0:T(8,128)S(1)}, f32[8,152,128]{2,1,0:T(8,128)S(1)}, u32[]{:S(2)}, u32[]{:S(2)}) collective-permute-start(f32[8,152,128]{2,1,0:T(8,128)S(1)} %constant_dynamic-update-slice_fusion.refs_0_), channel_id=1, source_target_pairs={{0,1},{1,0},{2,3},{3,2},{4,5},{5,4},{6,7},{7,6},{8,9},{9,8},{10,11... | collective-permute-start | bytes 1867784 | tf_op jit(solution)/shard_map/ppermute | solution.py:753
  34.7 10.2 %collective-permute-start.3 = (f32[3,2,64,128]{3,2,1,0:T(8,128)S(1)}, f32[3,2,64,128]{3,2,1,0:T(8,128)S(1)}, u32[]{:S(2)}, u32[]{:S(2)}) collective-permute-start(f32[3,2,64,128]{3,2,1,0:T(8,128)S(1)} %get-tuple-element.31), channel_id=1, source_target_pairs={{0,2},{2,4},{3,1},{4,6},{5,3},{6,8},{7,5},{8,10},{9,7},{10,12},{11... | collective-permute-start | bytes 589832 | tf_op jit(solution)/shard_map/ppermute | solution.py:769
  36.9 8.0 %collective-permute-start.2 = (f32[3,2,64,128]{3,2,1,0:T(8,128)S(1)}, f32[3,2,64,128]{3,2,1,0:T(8,128)S(1)}, u32[]{:S(2)}, u32[]{:S(2)}) collective-permute-start(f32[3,2,64,128]{3,2,1,0:T(8,128)S(1)} %get-tuple-element.31), channel_id=1, source_target_pairs={{1,2},{2,1},{3,4},{4,3},{5,6},{6,5},{7,8},{8,7},{9,10},{10,9},{11,... | collective-permute-start | bytes 589832 | tf_op jit(solution)/shard_map/ppermute | solution.py:760
  37.6 7.3 %collective-permute-start.4 = (f32[3,2,64,128]{3,2,1,0:T(8,128)S(1)}, f32[3,2,64,128]{3,2,1,0:T(8,128)S(1)}, u32[]{:S(2)}, u32[]{:S(2)}) collective-permute-start(f32[3,2,64,128]{3,2,1,0:T(8,128)S(1)} %collective-permute-done.1.swap), channel_id=1, source_target_pairs={{0,1},{1,0},{2,3},{3,2},{4,5},{5,4},{6,7},{7,6},{8,9},{9,8},{10,11... | collective-permute-start | bytes 589832 | tf_op jit(solution)/shard_map/ppermute | solution.py:753
  46.5 23.1 %copy-start = (f32[128,128]{1,0:T(8,128)S(1)}, f32[128,128]{1,0:T(8,128)}, u32[]{:S(2)}) copy-start(f32[128,128]{1,0:T(8,128)} %constant.21.clone.ytable) | copy-start | bytes 196612
  53.4 5.8 %collective-permute-start.14 = (f32[1,72,128]{2,1,0:T(8,128)S(1)}, f32[1,72,128]{2,1,0:T(8,128)S(1)}, u32[]{:S(2)}, u32[]{:S(2)}) collective-permute-start(f32[1,72,128]{2,1,0:T(8,128)S(1)} %bitcast.10), channel_id=1, source_target_pairs={{0,12},{1,13},{2,14},{3,15},{4,8},{5,9},{6,10},{7,11},{8,4},{9,5},... | collective-permute-start | bytes 110600 | tf_op jit(solution)/shard_map/ppermute | solution.py:753
  56.5 4.9 %collective-permute-start.13 = (f32[1,72,128]{2,1,0:T(8,128)S(1)}, f32[1,72,128]{2,1,0:T(8,128)S(1)}, u32[]{:S(2)}, u32[]{:S(2)}) collective-permute-start(f32[1,72,128]{2,1,0:T(8,128)S(1)} %bitcast.11), channel_id=1, source_target_pairs={{0,8},{1,9},{2,10},{3,11},{4,12},{5,13},{6,14},{7,15},{8,0},{9,1},... | collective-permute-start | bytes 110600 | tf_op jit(solution)/shard_map/ppermute | solution.py:753
  56.6 4.8 %collective-permute-start.12 = (f32[1,72,128]{2,1,0:T(8,128)S(1)}, f32[1,72,128]{2,1,0:T(8,128)S(1)}, u32[]{:S(2)}, u32[]{:S(2)}) collective-permute-start(f32[1,72,128]{2,1,0:T(8,128)S(1)} %bitcast.12), channel_id=1, source_target_pairs={{0,4},{1,5},{2,6},{3,7},{4,0},{5,1},{6,2},{7,3},{8,12},{9,13},{10,... | collective-permute-start | bytes 110600 | tf_op jit(solution)/shard_map/ppermute | solution.py:753
  61.4 6.9 %collective-permute-start.15 = (f32[4,72,128]{2,1,0:T(8,128)S(1)}, f32[4,72,128]{2,1,0:T(8,128)S(1)}, u32[]{:S(2)}, u32[]{:S(2)}) collective-permute-start(f32[4,72,128]{2,1,0:T(8,128)S(1)} %pad_maximum_fusion.1), channel_id=1, source_target_pairs={{0,2},{1,3},{2,0},{3,1},{4,6},{5,7},{6,4},{7,5},{8,10},{9,11},{10,... | collective-permute-start | bytes 442376 | tf_op jit(solution)/shard_map/ppermute | solution.py:753
  68.3 4.7 %collective-permute-start.16 = (f32[8,72,128]{2,1,0:T(8,128)S(1)}, f32[8,72,128]{2,1,0:T(8,128)S(1)}, u32[]{:S(2)}, u32[]{:S(2)}) collective-permute-start(f32[8,72,128]{2,1,0:T(8,128)S(1)} %constant_dynamic-update-slice_fusion.5.refs_0_), channel_id=1, source_target_pairs={{0,1},{1,0},{2,3},{3,2},{4,5},{5,4},{6,7},{7,6},{8,9},{9,8},{10,11... | collective-permute-start | bytes 884744 | tf_op jit(solution)/shard_map/ppermute | solution.py:753
  68.4 3.4 %collective-permute-start.10 = (f32[2,2,64,128]{3,2,1,0:T(8,128)S(1)}, f32[2,2,64,128]{3,2,1,0:T(8,128)S(1)}, u32[]{:S(2)}, u32[]{:S(2)}) collective-permute-start(f32[2,2,64,128]{3,2,1,0:T(8,128)S(1)} %get-tuple-element.38), channel_id=1, source_target_pairs={{0,1},{1,0},{2,3},{3,2},{4,5},{5,4},{6,7},{7,6},{8,9},{9,8},{10,11... | collective-permute-start | bytes 393224 | tf_op jit(solution)/shard_map/ppermute | solution.py:753
  68.9 2.9 %collective-permute-start.11 = (f32[2,2,64,128]{3,2,1,0:T(8,128)S(1)}, f32[2,2,64,128]{3,2,1,0:T(8,128)S(1)}, u32[]{:S(2)}, u32[]{:S(2)}) collective-permute-start(f32[2,2,64,128]{3,2,1,0:T(8,128)S(1)} %get-tuple-element.39), channel_id=1, source_target_pairs={{1,2},{2,1},{3,4},{4,3},{5,6},{6,5},{7,8},{8,7},{9,10},{10,9},{11,... | collective-permute-start | bytes 393224 | tf_op jit(solution)/shard_map/ppermute | solution.py:760
